TPU v7x, 32 devices: a whole 2x2x4 slice. The times are simulated.
32 devices in a mesh: exp: 8 (over z, x), tp: 4 (over y, core).
Axes of the slice: x: 2, y: 2, z: 4, core: 2. Of those that a mesh axis runs over, the one named last changes fastest.
Arguments:
- tokens: bfloat16 [4096, 2048], P(('exp', 'tp')), may hold values from -6 to 6
- cotangent: bfloat16 [4096, 2048], P(('exp', 'tp')), may hold values from -6 to 6
- attention_gain: float32 [2048], replicated, may hold values from 0.5 to 1.5
- query_weight: bfloat16 [2048, 2048], P(None, 'tp'), may hold values from -0.125 to 0.125
- key_weight: bfloat16 [2048, 2048], P(None, 'tp'), may hold values from -0.125 to 0.125
- value_weight: bfloat16 [2048, 2048], P(None, 'tp'), may hold values from -0.125 to 0.125
- output_weight: bfloat16 [2048, 2048], P('tp'), may hold values from -1 to 1
- query_norm: float32 [2048], P('tp'), may hold values from 0.5 to 1.5
- key_norm: float32 [2048], P('tp'), may hold values from 0.5 to 1.5
- mixture_gain: float32 [2048], replicated, may hold values from 0.5 to 1.5
- router_weight: bfloat16 [2048, 16], replicated, may hold values from -0.0625 to 0.0625
- gate_weight: bfloat16 [16, 2048, 1024], P('exp', None, 'tp'), may hold values from -0.125 to 0.125
- up_weight: bfloat16 [16, 2048, 1024], P('exp', None, 'tp'), may hold values from -0.125 to 0.125
- down_weight: bfloat16 [16, 1024, 2048], P('exp', 'tp'), may hold values from -3 to 3
- routes: int32 [4096, 8], P(('exp', 'tp')), may hold values from 0 to 15, all different within a row
- segments: int32 [8, 512], P('exp'), may hold values from 0 to 3, never falling along the last dimension, each value on 1 to 256 neighbouring positions
Outputs:
- output: bfloat16 [4096, 2048], P(('exp', 'tp'))
- tokens_grad: float32 [4096, 2048], P(('exp', 'tp'))
- attention_gain_grad: float32 [2048], replicated
- query_weight_grad: float32 [2048, 2048], P(None, 'tp')
- key_weight_grad: float32 [2048, 2048], P(None, 'tp')
- value_weight_grad: float32 [2048, 2048], P(None, 'tp')
- output_weight_grad: float32 [2048, 2048], P('tp')
- query_norm_grad: float32 [2048], P('tp')
- key_norm_grad: float32 [2048], P('tp')
- mixture_gain_grad: float32 [2048], replicated
- router_weight_grad: float32 [2048, 16], replicated
- gate_weight_grad: float32 [16, 2048, 1024], P('exp', None, 'tp')
- up_weight_grad: float32 [16, 2048, 1024], P('exp', None, 'tp')
- down_weight_grad: float32 [16, 1024, 2048], P('exp', 'tp')
Inputs may be any that keep to these rules, and one draw needn't show every extreme that they name: `routes`: each token names 8 different experts; every expert is named by some token. `segments`: in each row the ids never fall and start at 0; each of the 4 ids covers 1 to 256 consecutive positions, one exactly 256.
All inputs are finite; a program needn't handle non-finite values.
Results may differ from a plain program's by a relative error of at most 0.025.
Values may be sent and summed in bfloat16 or wider, within the bound.
No kernel may reach another device: no remote copies, remote signals or barrier semaphores. Data moves between devices by JAX's collectives and lax.ppermute only.
A program may use at most 256 MiB of HBM per device.

v0:
```python
import math

import jax
import jax.numpy as jnp
from jax import lax
from jax.sharding import PartitionSpec as P

HD = 128


EPS = 1e-05
HIGH = lax.Precision.HIGHEST


def inverse_rms(values):
    return lax.rsqrt(jnp.mean(values * values, axis=-1, keepdims=True) + EPS)


def norm_backward(grad_normed, normalized_input, factor):
    return factor * (
        grad_normed
        - normalized_input * jnp.mean(grad_normed * normalized_input, axis=-1, keepdims=True)
    )


def contract_rows(first_arg, second_arg):
    return lax.dot_general(
        first_arg, second_arg, (((0,), (0,)), ((), ())), preferred_element_type=jnp.float32
    )


def contract_cols(first_arg, second_arg):
    return lax.dot_general(
        first_arg, second_arg, (((1,), (1,)), ((), ())), preferred_element_type=jnp.float32
    )


def positions_of(segment_row):
    earlier = jnp.sum((segment_row[None, :] < segment_row[:, None]).astype(jnp.int32), axis=1)
    return jnp.arange(segment_row.shape[0], dtype=jnp.int32) - earlier


def rope_tables(positions, head_size):
    half_dim = head_size // 2
    inverse_freq = 10000.0 ** (-2.0 * jnp.arange(half_dim).astype(jnp.float32) / head_size)
    angles = positions.astype(jnp.float32)[:, None] * inverse_freq[None, :]
    return (jnp.cos(angles)[:, None, :], jnp.sin(angles)[:, None, :])


def rotate(values, cos_table, sin_table):
    half_dim = values.shape[-1] // 2
    first_half = values[..., :half_dim]
    second_half = values[..., half_dim:]
    return jnp.concatenate(
        [
            first_half * cos_table - second_half * sin_table,
            second_half * cos_table + first_half * sin_table,
        ],
        axis=-1,
    )


def gather_expert_rows(local_rows):
    return lax.all_gather(local_rows, "tp", axis=1, tiled=True)


def body(
    tokens,
    cotangent,
    attention_gain,
    query_weight,
    key_weight,
    value_weight,
    output_weight,
    query_norm,
    key_norm,
    mixture_gain,
    router_weight,
    gate_weight,
    up_weight,
    down_weight,
    routes,
    segments,
):
    tok_rows, model_width = tokens.shape
    top_count = routes.shape[1]
    experts_all = router_weight.shape[1]
    capacity = tok_rows * top_count * 7 // (8 * experts_all)
    local_width = query_weight.shape[1]
    head_count = local_width // HD
    inv_sqrt = 1.0 / math.sqrt(HD)
    inputs = tokens.astype(jnp.float32)
    scale_one = inverse_rms(inputs)
    normed_one = inputs * scale_one
    attention_in = (normed_one * attention_gain).astype(jnp.bfloat16)
    gathered_rows = lax.all_gather(attention_in, "tp", axis=0, tiled=True)
    row_length = gathered_rows.shape[0]
    queries = jnp.dot(gathered_rows, query_weight, preferred_element_type=jnp.float32).reshape(
        row_length, head_count, HD
    )
    key_rows = jnp.dot(gathered_rows, key_weight, preferred_element_type=jnp.float32).reshape(
        row_length, head_count, HD
    )
    value_rows = (
        jnp.dot(gathered_rows, value_weight, preferred_element_type=jnp.float32)
        .astype(jnp.bfloat16)
        .reshape(row_length, head_count, HD)
    )
    query_gain = query_norm.reshape(head_count, HD)
    key_gain = key_norm.reshape(head_count, HD)
    query_scale = inverse_rms(queries)
    query_hat = queries * query_scale
    key_scale = inverse_rms(key_rows)
    key_hat = key_rows * key_scale
    segment_row = segments[0]
    cos_table, sin_table = rope_tables(positions_of(segment_row), HD)
    query_rot = rotate(query_hat * query_gain, cos_table, sin_table).astype(jnp.bfloat16)
    key_rot = rotate(key_hat * key_gain, cos_table, sin_table).astype(jnp.bfloat16)
    block_rows = min(512, row_length)
    position = jnp.arange(row_length, dtype=jnp.int32)

    def block_scores(first_row):
        scores = (
            jnp.einsum("ihd,jhd->hij", query_rot, key_rot, preferred_element_type=jnp.float32)
            * inv_sqrt
        )
        allowed = (
            segment_row[first_row : first_row + block_rows, None] == segment_row[None, :]
        ) & (position[None, :] <= position[first_row : first_row + block_rows, None])
        return jnp.where(allowed[None], scores, -1e30)

    first_row = 0
    scores = block_scores(first_row)
    row_peak = jnp.max(scores, axis=-1, keepdims=True)
    shifted = jnp.exp(scores - row_peak)
    denominator = jnp.sum(shifted, axis=-1, keepdims=True)
    weights = (shifted / denominator).astype(jnp.bfloat16)
    log_totals = [row_peak + jnp.log(denominator)]
    attended_parts = jnp.einsum(
        "hij,jhd->ihd", weights, value_rows, preferred_element_type=jnp.float32
    ).reshape(block_rows, local_width)
    attended = attended_parts.astype(jnp.bfloat16)
    attention_block = lax.psum_scatter(
        jnp.dot(attended, output_weight, preferred_element_type=jnp.float32).astype(jnp.bfloat16),
        "tp",
        scatter_dimension=0,
        tiled=True,
    ).astype(jnp.float32)
    middle = inputs + attention_block
    scale_two = inverse_rms(middle)
    normed_two = middle * scale_two
    mixture_in = (normed_two * mixture_gain).astype(jnp.bfloat16)
    logits = jnp.dot(mixture_in, router_weight, preferred_element_type=jnp.float32)
    probabilities = jax.nn.softmax(logits, axis=-1)
    expert_ids = jnp.arange(experts_all, dtype=jnp.int32)
    chosen = (routes[:, :, None] == expert_ids[None, None, :]).astype(jnp.float32)
    gate_values = jnp.sum(chosen * probabilities[:, None, :], axis=-1)
    assigned = routes.reshape(-1)
    matches = (assigned[:, None] == expert_ids[None, :]).astype(jnp.int32)
    earlier = jnp.sum(jnp.cumsum(matches, axis=0) * matches, axis=1) - 1
    slot_ids = jnp.where(earlier < capacity, assigned * capacity + earlier, experts_all * capacity)
    assign_count = tok_rows * top_count
    owners = (
        jnp.full((experts_all * capacity + 1,), assign_count, jnp.int32)
        .at[slot_ids]
        .set(jnp.arange(assign_count, dtype=jnp.int32))[:-1]
    )
    source_rows = owners // top_count
    input_pad = jnp.concatenate([mixture_in, jnp.zeros((1, model_width), jnp.bfloat16)], axis=0)
    outgoing = input_pad[source_rows].reshape(experts_all, capacity, model_width)
    arrived = lax.all_to_all(outgoing, "exp", split_axis=0, concat_axis=1, tiled=True)
    expert_in = gather_expert_rows(arrived)
    gate_pre = jnp.einsum(
        "erd,edf->erf", expert_in, gate_weight, preferred_element_type=jnp.float32
    )
    up_pre = jnp.einsum("erd,edf->erf", expert_in, up_weight, preferred_element_type=jnp.float32)
    hidden = (jax.nn.silu(gate_pre) * up_pre).astype(jnp.bfloat16)
    partial_out = jnp.einsum(
        "erf,efd->erd", hidden, down_weight, preferred_element_type=jnp.float32
    )
    returned = lax.psum_scatter(
        partial_out.astype(jnp.bfloat16), "tp", scatter_dimension=1, tiled=True
    )
    combined = lax.all_to_all(returned, "exp", split_axis=1, concat_axis=0, tiled=True)
    output_pad = jnp.concatenate(
        [combined.reshape(-1, model_width), jnp.zeros((1, model_width), jnp.bfloat16)], axis=0
    )
    expert_out = output_pad[slot_ids].astype(jnp.float32).reshape(tok_rows, top_count, model_width)
    mixture = jnp.sum(gate_values[:, :, None] * expert_out, axis=1)
    output = (middle + mixture).astype(jnp.bfloat16)
    grad_out = cotangent.astype(jnp.float32)
    grad_gate = jnp.sum(grad_out[:, None, :] * expert_out, axis=-1)
    grad_sent = (
        (gate_values[:, :, None] * grad_out[:, None, :])
        .reshape(assign_count, model_width)
        .astype(jnp.bfloat16)
    )
    grad_pad = jnp.concatenate([grad_sent, jnp.zeros((1, model_width), jnp.bfloat16)], axis=0)
    grad_outgoing = grad_pad[owners].reshape(experts_all, capacity, model_width)
    grad_arrived = lax.all_to_all(grad_outgoing, "exp", split_axis=0, concat_axis=1, tiled=True)
    grad_expert = lax.all_gather(grad_arrived, "tp", axis=1, tiled=True)
    gate_pre = jnp.einsum(
        "erd,edf->erf", expert_in, gate_weight, preferred_element_type=jnp.float32
    )
    up_pre = jnp.einsum("erd,edf->erf", expert_in, up_weight, preferred_element_type=jnp.float32)
    gate_sig = jax.nn.sigmoid(gate_pre)
    gate_act = gate_pre * gate_sig
    hidden = (gate_act * up_pre).astype(jnp.bfloat16)
    grad_hidden = jnp.einsum(
        "erd,efd->erf", grad_expert, down_weight, preferred_element_type=jnp.float32
    )
    down_grad = jnp.einsum("erf,erd->efd", hidden, grad_expert, preferred_element_type=jnp.float32)
    grad_gate_pre = (grad_hidden * up_pre * gate_sig * (1.0 + gate_pre * (1.0 - gate_sig))).astype(
        jnp.bfloat16
    )
    grad_up_pre = (grad_hidden * gate_act).astype(jnp.bfloat16)
    gate_grad = jnp.einsum(
        "erd,erf->edf", expert_in, grad_gate_pre, preferred_element_type=jnp.float32
    )
    up_grad = jnp.einsum("erd,erf->edf", expert_in, grad_up_pre, preferred_element_type=jnp.float32)
    grad_in_part = jnp.einsum(
        "erf,edf->erd", grad_gate_pre, gate_weight, preferred_element_type=jnp.float32
    ) + jnp.einsum("erf,edf->erd", grad_up_pre, up_weight, preferred_element_type=jnp.float32)
    grad_in = lax.psum_scatter(
        grad_in_part.astype(jnp.bfloat16), "tp", scatter_dimension=1, tiled=True
    )
    grad_home = lax.all_to_all(grad_in, "exp", split_axis=1, concat_axis=0, tiled=True)
    home_pad = jnp.concatenate(
        [grad_home.reshape(-1, model_width), jnp.zeros((1, model_width), jnp.bfloat16)], axis=0
    )
    grad_assigned = home_pad[slot_ids].astype(jnp.float32).reshape(tok_rows, top_count, model_width)
    grad_probs = jnp.sum(chosen * grad_gate[:, :, None], axis=1)
    grad_logits = probabilities * (
        grad_probs - jnp.sum(grad_probs * probabilities, axis=-1, keepdims=True)
    )
    router_grad = jnp.dot(mixture_in.astype(jnp.float32).T, grad_logits, precision=HIGH)
    grad_mixture_in = jnp.sum(grad_assigned, axis=1) + jnp.dot(
        grad_logits, router_weight.astype(jnp.float32).T, precision=HIGH
    )
    mixture_gain_grad = jnp.sum(grad_mixture_in * normed_two, axis=0)
    grad_middle = grad_out + norm_backward(grad_mixture_in * mixture_gain, normed_two, scale_two)
    grad_attention = grad_middle.astype(jnp.bfloat16)
    row_grad = lax.all_gather(grad_attention, "tp", axis=0, tiled=True)
    output_weight_grad = contract_rows(attended, row_grad)
    grad_attended = contract_cols(row_grad, output_weight).astype(jnp.bfloat16)
    grad_query_parts = []
    grad_key_rows = jnp.zeros((row_length, head_count, HD), jnp.float32)
    grad_value_rows = jnp.zeros((row_length, head_count, HD), jnp.float32)
    for block_index, first_row in enumerate(range(0, row_length, block_rows)):
        scores = block_scores(first_row)
        probs_block = jnp.exp(scores - log_totals[block_index])
        weights = probs_block.astype(jnp.bfloat16)
        grad_block = grad_attended.reshape(block_rows, head_count, HD)
        grad_weights = jnp.einsum(
            "ihd,jhd->hij", grad_block, value_rows, preferred_element_type=jnp.float32
        )
        inner_sum = jnp.sum(grad_weights * probs_block, axis=-1, keepdims=True)
        grad_scores = (probs_block * (grad_weights - inner_sum)).astype(jnp.bfloat16)
        grad_query_parts.append(
            jnp.einsum("hij,jhd->ihd", grad_scores, key_rot, preferred_element_type=jnp.float32)
            * inv_sqrt
        )
        grad_key_rows = (
            jnp.einsum("hij,ihd->jhd", grad_scores, query_rot, preferred_element_type=jnp.float32)
            * inv_sqrt
        )
        grad_value_rows = jnp.einsum(
            "hij,ihd->jhd", weights, grad_block, preferred_element_type=jnp.float32
        )
    grad_query_norm = rotate(grad_query_parts[0], cos_table, -sin_table)
    grad_key_norm = rotate(grad_key_rows, cos_table, -sin_table)
    query_norm_grad = jnp.sum(grad_query_norm * query_hat, axis=0).reshape(local_width)
    key_norm_grad = jnp.sum(grad_key_norm * key_hat, axis=0).reshape(local_width)
    grad_queries = (
        norm_backward(grad_query_norm * query_gain, query_hat, query_scale)
        .reshape(row_length, local_width)
        .astype(jnp.bfloat16)
    )
    grad_keys = (
        norm_backward(grad_key_norm * key_gain, key_hat, key_scale)
        .reshape(row_length, local_width)
        .astype(jnp.bfloat16)
    )
    grad_values = grad_value_rows.reshape(row_length, local_width).astype(jnp.bfloat16)
    query_weight_grad = contract_rows(gathered_rows, grad_queries)
    key_weight_grad = contract_rows(gathered_rows, grad_keys)
    value_weight_grad = contract_rows(gathered_rows, grad_values)
    total_grad = contract_cols(grad_queries, query_weight)
    total_grad = total_grad + contract_cols(grad_keys, key_weight)
    grad_attention_in = lax.psum_scatter(
        (total_grad + contract_cols(grad_values, value_weight)).astype(jnp.bfloat16),
        "tp",
        scatter_dimension=0,
        tiled=True,
    ).astype(jnp.float32)
    attention_gain_grad = jnp.sum(grad_attention_in * normed_one, axis=0)
    tokens_grad = grad_middle + norm_backward(
        grad_attention_in * attention_gain, normed_one, scale_one
    )
    head_sums = (
        lax.psum(query_weight_grad.astype(jnp.bfloat16), "exp").astype(jnp.float32),
        lax.psum(key_weight_grad.astype(jnp.bfloat16), "exp").astype(jnp.float32),
        lax.psum(value_weight_grad.astype(jnp.bfloat16), "exp").astype(jnp.float32),
        lax.psum(output_weight_grad.astype(jnp.bfloat16), "exp").astype(jnp.float32),
        lax.psum(query_norm_grad.astype(jnp.bfloat16), "exp").astype(jnp.float32),
        lax.psum(key_norm_grad.astype(jnp.bfloat16), "exp").astype(jnp.float32),
    )
    shared_sums = lax.psum((attention_gain_grad, mixture_gain_grad, router_grad), ("exp", "tp"))
    return (
        output,
        tokens_grad,
        shared_sums[0],
        head_sums[0],
        head_sums[1],
        head_sums[2],
        head_sums[3],
        head_sums[4],
        head_sums[5],
        shared_sums[1],
        shared_sums[2],
        gate_grad,
        up_grad,
        down_grad,
    )


def solution(mesh):
    return jax.shard_map(
        body,
        mesh=mesh,
        in_specs=(
            P(("exp", "tp"), None),
            P(("exp", "tp"), None),
            P(),
            P(None, "tp"),
            P(None, "tp"),
            P(None, "tp"),
            P("tp", None),
            P("tp"),
            P("tp"),
            P(),
            P(),
            P("exp", None, "tp"),
            P("exp", None, "tp"),
            P("exp", "tp", None),
            P(("exp", "tp"), None),
            P("exp", None),
        ),
        out_specs=(
            P(("exp", "tp"), None),
            P(("exp", "tp"), None),
            P(),
            P(None, "tp"),
            P(None, "tp"),
            P(None, "tp"),
            P("tp", None),
            P("tp"),
            P("tp"),
            P(),
            P(),
            P("exp", None, "tp"),
            P("exp", None, "tp"),
            P("exp", "tp", None),
        ),
        check_vma=False,
    )
```

profile of v0, /device:TPU:0, one launch (start us, length us, event | category | flops | bytes accessed | tf_op | source)
XLA Modules:
  0.0 1259.1 jit_solution(2690776216427497176)
XLA Ops:
  9.2 2.0 fusion.23
  12.3 1.7 fusion.33
  13.9 1.8 fusion.35
  15.7 21.0 %all-gather.5.cloned.1.call-done = bf16[512,2048]{1,0:T(8,128)(2,1)} async-done(((bf16[128,2048]{1,0:T(8,128)(2,1)}), bf16[512,2048]{1,0:T(8,128)(2,1)}) %all-gather.5.cloned.1.call-update) | async-done | bytes 2097168 | tf_op jit(solution)/shard_map/all_gather | solution.py:96
  36.7 3.5 multiply_reduce_fusion.6
  41.6 4.5 multiply_reduce_fusion.7
  47.7 2.2 multiply_multiply_fusion
  52.9 2.5 copy-done.36
  59.1 2.6 convolution_convert_fusion.5
  62.5 4.5 reduce-window.6
  67.5 4.3 scatter_custom_fusion
  71.9 21.5 %reduce-scatter.5.cloned.1.call-done = bf16[128,2048]{1,0:T(8,128)(2,1)} async-done(((bf16[512,2048]{1,0:T(8,128)(2,1)}), bf16[128,2048]{1,0:T(8,128)(2,1)}) %reduce-scatter.5.cloned.1.call-update) | async-done | bytes 524304 | tf_op jit(solution)/shard_map/reduce_scatter | solution.py:143
  96.8 5.0 gather_fusion
  101.7 87.5 %all_to_all.66 = bf16[16,56,2048]{2,1,0:T(8,128)(2,1)S(1)} all-to-all(bf16[16,56,2048]{2,1,0:T(8,128)(2,1)} %bitcast.163), channel_id=1, replica_groups=mesh['exp'=8,'tp'=4] {'exp'}, dimensions={0} | all-to-all | bytes 7340032 | tf_op jit(solution)/shard_map/all_to_all | solution.py:171
  189.2 2.3 copy.150
  195.2 2.5 concatenate.34
  197.7 12.3 gather_fusion.2
  210.0 85.0 %all_to_all.67 = bf16[16,56,2048]{2,1,0:T(8,128)(2,1)S(1)} all-to-all(bf16[16,56,2048]{2,1,0:T(8,128)(2,1)} %bitcast.164), channel_id=1, replica_groups=mesh['exp'=8,'tp'=4] {'exp'}, dimensions={0} | all-to-all | bytes 7340032 | tf_op jit(solution)/shard_map/all_to_all | solution.py:200
  295.1 2.3 copy.154
  297.5 13.5 %fusion.53 = f32[2,1792,256]{2,1,0:T(8,128)} fusion(bf16[2,1792,2048]{2,1,0:T(8,128)(2,1)} %all-gather.7.cloned.1.call-done, bf16[2,2048,256]{2,1,0:T(8,128)(2,1)} %param.28), kind=kOutput, calls=%fused_computation.159 | convolution fusion | flops 3758096384 | bytes 20447232 | tf_op jit(solution)/shard_map/erd,edf->erf/dot_general | solution.py:176
  310.9 9.8 fusion.52
  320.8 68.7 %all-gather.9.cloned.1.call-done = bf16[2,1792,2048]{2,1,0:T(8,128)(2,1)} async-done(((bf16[2,448,2048]{2,1,0:T(8,128)(2,1)}), bf16[2,1792,2048]{2,1,0:T(8,128)(2,1)}) %all-gather.9.cloned.1.call-update) | async-done | bytes 14680080 | tf_op jit(solution)/shard_map/all_gather | solution.py:201
  389.5 15.6 %multiply_convert_fusion.1 = (bf16[2,1792,256]{2,1,0:T(8,128)(2,1)}, bf16[2,1792,256]{2,1,0:T(8,128)(2,1)}, bf16[2,1792,256]{2,1,0:T(8,128)(2,1)}) fusion(f32[2,1792,256]{2,1,0:T(8,128)} %fusion.52, f32[2,1792,256]{2,1,0:T(8,128)} %fusion.53, bf16[2,1792,2048]{2,1,0:T(8,128)(2,1)} %all-gather.9.cloned.1.call-done, bf16[2,256,2048]{2,1,0:T(8,128)(2,1)S(1)} %copy-done), kind=kOutput, calls=%fused_computation.22 | convolution fusion | flops 3771858944 | bytes 29622272 | tf_op jit(solution)/shard_map/erd,efd->erf/dot_general | solution.py:209
  405.0 8.7 convolution_convert_fusion
  415.3 19.2 %fusion.54 = f32[2,1792,2048]{2,1,0:T(8,128)} fusion(bf16[2,1792,256]{2,1,0:T(8,128)(2,1)} %get-tuple-element.33, bf16[2,2048,256]{2,1,0:T(8,128)(2,1)S(1)} %copy-done.34), kind=kOutput, calls=%fused_computation.160 | convolution fusion | flops 3758096384 | bytes 33292288 | tf_op jit(solution)/shard_map/erf,edf->erd/dot_general | solution.py:221
  434.6 17.7 %add_convert_fusion = bf16[2,1792,2048]{2,1,0:T(8,128)(2,1)} fusion(f32[2,1792,2048]{2,1,0:T(8,128)} %fusion.54, bf16[2,1792,256]{2,1,0:T(8,128)(2,1)S(1)} %copy-done.43, bf16[2,2048,256]{2,1,0:T(8,128)(2,1)S(1)} %copy-done.35), kind=kOutput, calls=%fused_computation.5 | convolution fusion | flops 3772776448 | bytes 47972352 | tf_op jit(solution)/shard_map/erf,edf->erd/dot_general | solution.py:223
  452.3 74.5 %reduce-scatter.7.cloned.1.call-done = bf16[2,448,2048]{2,1,0:T(8,128)(2,1)} async-done(((bf16[2,1792,2048]{2,1,0:T(8,128)(2,1)}), bf16[2,448,2048]{2,1,0:T(8,128)(2,1)}) %reduce-scatter.7.cloned.1.call-update) | async-done | bytes 3670032 | tf_op jit(solution)/shard_map/reduce_scatter | solution.py:181
  526.8 7.6 copy.151
  534.4 5.5 all-to-all-start.1
  539.9 102.3 %reduce-scatter.9.cloned.1.call-done = bf16[2,448,2048]{2,1,0:T(8,128)(2,1)} async-done(((bf16[2,1792,2048]{2,1,0:T(8,128)(2,1)}), bf16[2,448,2048]{2,1,0:T(8,128)(2,1)}) %reduce-scatter.9.cloned.1.call-update) | async-done | bytes 3670032 | tf_op jit(solution)/shard_map/reduce_scatter | solution.py:224
  642.3 7.6 copy.155
  649.9 5.5 all-to-all-start.3
  655.9 3.7 copy.152
  659.6 2.3 concatenate.33
  661.9 11.3 gather_fusion.1
  673.2 5.8 fusion.1
  679.2 58.3 %all-to-all-done.3 = bf16[2,448,2048]{2,0,1:T(2,128)(2,1)} async-done(((bf16[2,448,2048]{2,0,1:T(2,128)(2,1)}), bf16[2,448,2048]{2,0,1:T(2,128)(2,1)}, u32[]{:S(2)}, u32[]{:S(2)}) %all-to-all-start.3) | async-done | bytes 3670048 | tf_op jit(solution)/shard_map/all_to_all | solution.py:227
  737.5 3.7 copy.156
  741.1 2.3 concatenate.35
  743.4 11.3 gather_fusion.3
  754.8 5.2 convert_reduce_fusion
  762.6 20.6 %all-gather.11.cloned.1.call-done = bf16[512,2048]{1,0:T(8,128)(2,1)} async-done(((bf16[128,2048]{1,0:T(8,128)(2,1)}), bf16[512,2048]{1,0:T(8,128)(2,1)}) %all-gather.11.cloned.1.call-update) | async-done | bytes 2097168 | tf_op jit(solution)/shard_map/all_gather | solution.py:243
  783.2 3.6 convolution_convert_fusion.6
  786.9 1.6 fusion.16
  797.4 2.6 copy.164
  800.1 2.5 copy.169
  804.2 3.1 fusion.55
  809.7 2.7 add_convert_fusion.1
  812.5 4.4 convolution_convert_fusion.1
  816.9 2.6 convolution_convert_fusion.2
  819.5 2.6 convolution_convert_fusion.3
  822.2 2.6 convolution_convert_fusion.4
  824.9 11.0 fusion.58
  835.9 11.0 fusion.57
  847.0 5.7 fusion.59
  853.7 22.3 %all-reduce.5 = (bf16[512]{0:T(512)(128)(2,1)S(1)}, bf16[512]{0:T(512)(128)(2,1)S(1)}) all-reduce(bf16[512]{0:T(512)(128)(2,1)S(1)} %get-tuple-element.37, bf16[512]{0:T(512)(128)(2,1)S(1)} %get-tuple-element.35), channel_id=1, replica_groups=mesh['exp'=8,'tp'=4] {'exp'}, use_global_device_ids=true, to_apply=%region_35.36 | all-reduce | flops 1024 | bytes 4096 | tf_op jit(solution)/shard_map/psum | solution.py:305
  878.7 3.3 fusion.22
  882.0 40.7 %all-reduce.4 = (f32[2048]{0:T(1024)}, f32[2048]{0:T(1024)}) all-reduce(f32[2048]{0:T(1024)S(1)} %get-tuple-element.18, f32[2048]{0:T(1024)S(1)} %get-tuple-element.16), channel_id=1, replica_groups=mesh['exp'=8,'tp'=4] {'exp','tp'}, use_global_device_ids=true, to_apply=%region_29.30 | all-reduce | flops 4096 | bytes 32768 | tf_op jit(solution)/shard_map/psum | solution.py:308
  922.7 200.3 %all-reduce.12.cloned.1.call-done = (bf16[2048,512]{1,0:T(8,128)(2,1)}, bf16[2048,512]{1,0:T(8,128)(2,1)}, bf16[2048,512]{1,0:T(8,128)(2,1)}, bf16[512,2048]{1,0:T(8,128)(2,1)}) async-done(((bf16[2048,512]{1,0:T(8,128)(2,1)}, bf16[2048,512]{1,0:T(8,128)(2,1)}, bf16[2048,512]{1,0:T(8,128)(2,1)}, bf16[512,2048]{1,0:T(8,128)(2,1)}), (bf16[2048,512]{1,0:T(8,128)(2,1)}, bf16[2048,512]{1,0:T(8,128)(2,1)}, ...) | async-done | bytes 8388624 | tf_op jit(solution)/shard_map/psum | solution.py:301
  1123.0 4.3 convert_element_type.207
  1127.4 2.6 convert_element_type.209
  1130.0 2.7 convert_element_type.211
  1132.7 2.5 convert_element_type.213
  1135.3 115.1 %all-reduce.10.cloned.1.call-done = f32[2048,16]{0,1:T(8,128)} async-done(((f32[2048,16]{0,1:T(8,128)}), f32[2048,16]{0,1:T(8,128)}) %all-reduce.10.cloned.1.call-update) | async-done | bytes 131088 | tf_op jit(solution)/shard_map/psum | solution.py:308
  (253 shorter events, 43.5 us)
Async XLA Ops:
  7.2 382.3 %copy-start = (bf16[2,256,2048]{2,1,0:T(8,128)(2,1)S(1)}, bf16[2,256,2048]{2,1,0:T(8,128)(2,1)}, u32[]{:S(2)}) copy-start(bf16[2,256,2048]{2,1,0:T(8,128)(2,1)} %param.29) | copy-start | bytes 6291460
  7.2 29.5 %all-gather.5.cloned.1.call-start = ((), (), s32[]{:S(2)}) async-start(), calls=%async_computation.8 | async-start | bytes 2621440 | tf_op jit(solution)/shard_map/all_gather | solution.py:96
  11.2 82.1 %reduce-scatter.5.cloned.1.call-start = ((), (), s32[]{:S(2)}) async-start(), calls=%async_computation.9 | async-start | bytes 2621440 | tf_op jit(solution)/shard_map/reduce_scatter | solution.py:143
  15.7 34.2 %copy-start.31 = (f32[512,64]{1,0:T(8,128)}, f32[512,64]{1,0:T(8,128)S(1)}, u32[]{:S(2)}) copy-start(f32[512,64]{1,0:T(8,128)S(1)} %get-tuple-element.57) | copy-start | bytes 393220
  40.2 5.9 copy-start.23
  40.2 7.4 copy-start.52
  41.6 6.1 copy-start.62
  41.6 6.1 copy-start.64
  46.1 4.6 copy-start.54
  47.7 3.1 copy-start.8
  52.2 5.1 copy-start.2
  52.2 5.1 copy-start.57
  52.2 3.1 copy-start.36
  52.3 3.7 copy-start.71
  58.3 3.4 copy-start.73
  59.1 2.9 copy-start.59
  59.1 34.3 %copy-start.4 = (bf16[128,2048]{1,0:T(8,128)(2,1)S(1)}, bf16[128,2048]{1,0:T(8,128)(2,1)}, u32[]{:S(2)}) copy-start(bf16[128,2048]{1,0:T(8,128)(2,1)} %param.16) | copy-start | bytes 1572868
  59.1 35.6 %copy-start.50 = (f32[2048]{0:T(1024)S(1)}, f32[2048]{0:T(1024)}, u32[]{:S(2)}) copy-start(f32[2048]{0:T(1024)} %param.25) | copy-start | bytes 24580
  61.7 235.7 %all-gather.7.cloned.1.call-start = ((), (), s32[]{:S(2)}) async-start(), calls=%async_computation.10 | async-start | bytes 18350080 | tf_op jit(solution)/shard_map/all_gather | solution.py:64
  94.7 7.1 copy-start.66
  191.5 197.9 %all-gather.9.cloned.1.call-start = ((), (), s32[]{:S(2)}) async-start(), calls=%async_computation.12 | async-start | bytes 18350080 | tf_op jit(solution)/shard_map/all_gather | solution.py:201
  297.4 229.4 %reduce-scatter.7.cloned.1.call-start = ((), (), s32[]{:S(2)}) async-start(), calls=%async_computation.11 | async-start | bytes 18350080 | tf_op jit(solution)/shard_map/reduce_scatter | solution.py:181
  297.5 13.5 %copy-start.33 = (bf16[2,2048,256]{2,1,0:T(8,128)(2,1)S(1)}, bf16[2,2048,256]{2,1,0:T(8,128)(2,1)}, u32[]{:S(2)}) copy-start(bf16[2,2048,256]{2,1,0:T(8,128)(2,1)} %param.27) | copy-start | bytes 6291460
  413.8 228.5 %reduce-scatter.9.cloned.1.call-start = ((), (), s32[]{:S(2)}) async-start(), calls=%async_computation.13 | async-start | bytes 18350080 | tf_op jit(solution)/shard_map/reduce_scatter | solution.py:224
  415.3 19.2 %copy-start.35 = (bf16[2,2048,256]{2,1,0:T(8,128)(2,1)S(1)}, bf16[2,2048,256]{2,1,0:T(8,128)(2,1)}, u32[]{:S(2)}) copy-start(bf16[2,2048,256]{2,1,0:T(8,128)(2,1)} %param.28) | copy-start | bytes 6291460
  415.3 19.2 %copy-start.43 = (bf16[2,1792,256]{2,1,0:T(8,128)(2,1)S(1)}, bf16[2,1792,256]{2,1,0:T(8,128)(2,1)}, u32[]{:S(2)}) copy-start(bf16[2,1792,256]{2,1,0:T(8,128)(2,1)} %get-tuple-element.32) | copy-start | bytes 5505028
  534.4 115.5 %all-to-all-start.1 = ((bf16[2,448,2048]{2,0,1:T(2,128)(2,1)}), bf16[2,448,2048]{2,0,1:T(2,128)(2,1)}, u32[]{:S(2)}, u32[]{:S(2)}) async-start(bf16[2,448,2048]{2,0,1:T(2,128)(2,1)} %copy.151), calls=%async_computation.3 | async-start | bytes 7340032 | tf_op jit(solution)/shard_map/all_to_all | solution.py:184
  649.9 87.6 %all-to-all-start.3 = ((bf16[2,448,2048]{2,0,1:T(2,128)(2,1)}), bf16[2,448,2048]{2,0,1:T(2,128)(2,1)}, u32[]{:S(2)}, u32[]{:S(2)}) async-start(bf16[2,448,2048]{2,0,1:T(2,128)(2,1)} %copy.155), calls=%async_computation.6 | async-start | bytes 7340032 | tf_op jit(solution)/shard_map/all_to_all | solution.py:227
  655.4 127.8 %all-gather.11.cloned.1.call-start = ((), (), s32[]{:S(2)}) async-start(), calls=%async_computation.14 | async-start | bytes 2621440 | tf_op jit(solution)/shard_map/all_gather | solution.py:243
  754.8 5.2 copy-start.5
  754.8 5.2 copy-start.7
  754.8 5.2 copy-start.51
  754.8 5.2 copy-start.67
  754.8 6.3 copy-start.13
  760.0 2.5 copy-start.58
  760.0 2.5 copy-start.61
  762.3 114.9 %reduce-scatter.11.cloned.1.call-start = ((), (), s32[]{:S(2)}) async-start(), calls=%async_computation.15 | async-start | bytes 2621440 | tf_op jit(solution)/shard_map/reduce_scatter | solution.py:290
  783.2 3.7 copy-start.3
  790.7 2.2 copy-start.32
  790.8 2.2 copy-start.45
  797.4 5.2 copy-start.25
  804.2 3.2 copy-start.27
  804.2 3.2 copy-start.24
  804.2 3.2 copy-start.26
  804.2 3.6 copy-start.42
  809.7 2.8 copy-start.74
  812.4 310.6 %all-reduce.12.cloned.1.call-start = ((), (), s32[]{:S(2)}) async-start(), calls=%async_computation.17 | async-start | bytes 16777216 | tf_op jit(solution)/shard_map/psum | solution.py:301
  812.5 4.4 copy-start.72
  816.9 2.7 copy-start.30
  819.5 2.7 copy-start.28
  824.8 425.5 %all-reduce.10.cloned.1.call-start = ((), (), s32[]{:S(2)}) async-start(), calls=%async_computation.16 | async-start | bytes 262144 | tf_op jit(solution)/shard_map/psum | solution.py:308
  824.9 22.0 %slice-start = ((s8[14680064]{0:T(1024)(128)(4,1)}), s8[4194304]{0:T(1024)(128)(4,1)S(1)}, s32[]{:S(2)}) async-start(s8[14680064]{0:T(1024)(128)(4,1)} %bitcast.161), calls=%async_computation.18 | async-start | bytes 8388608
  824.9 22.0 %slice-start.1 = ((s8[14680064]{0:T(1024)(128)(4,1)}), s8[4194304]{0:T(1024)(128)(4,1)S(1)}, s32[]{:S(2)}) async-start(s8[14680064]{0:T(1024)(128)(4,1)} %bitcast.161), calls=%async_computation.19 | async-start | bytes 8388608
  835.9 11.0 copy-start.6
  835.9 11.0 slice-start.2
  835.9 11.1 slice-start.3
  847.0 5.7 copy-start.12
  847.0 30.2 %copy-start.56 = (f32[2048]{0:T(1024)S(1)}, f32[2048]{0:T(1024)}, u32[]{:S(2)}) copy-start(f32[2048]{0:T(1024)} %param.18) | copy-start | bytes 24580
  847.0 30.2 %copy-start.69 = (f32[128]{0:T(128)S(1)}, f32[128]{0:T(128)}, u32[]{:S(2)}) copy-start(f32[128]{0:T(128)} %copy-done.68) | copy-start | bytes 1540
  847.0 31.7 %copy-start.14 = (bf16[128,2048]{1,0:T(8,128)(2,1)S(1)}, bf16[128,2048]{1,0:T(8,128)(2,1)}, u32[]{:S(2)}) copy-start(bf16[128,2048]{1,0:T(8,128)(2,1)} %param.17) | copy-start | bytes 1572868
  1123.0 4.4 copy-start.40
  1127.4 2.6 copy-start.39
  1130.0 2.7 copy-start.38
  1130.0 121.9 %copy-start.1 = (bf16[2,256,2048]{2,1,0:T(8,128)(2,1)S(1)}, bf16[2,256,2048]{2,1,0:T(8,128)(2,1)}, u32[]{:S(2)}) copy-start(bf16[2,256,2048]{2,1,0:T(8,128)(2,1)} %param.29) | copy-start | bytes 6291460
  (27 other events, 40.5 us)
Sparse Core Ops, SparseCore 0:
  11.4 25.2 all-gather.4
  61.8 31.4 reduce-scatter.4
  191.6 92.0 all-gather.6
  297.5 91.9 all-gather.8
  413.9 112.8 reduce-scatter.6
  529.4 112.8 reduce-scatter.8
  762.4 20.6 all-gather.10
  812.5 31.4 reduce-scatter.10
  849.2 273.8 all-reduce.11
  1129.0 121.2 all-reduce.9
where the time goes:
time: 1270 us; the launch traced here: 1260 us
  waiting for transfers between devices  682 us (54%)
  blocking collectives  236 us (19%)
  matrix products  157 us (12%)
  local copies, waits for them, and re-layouts  97.1 us (8%)
  other arithmetic  58.7 us (5%)
  between operations  15.7 us (1%)
    psum x1, waiting for transfers between devices, body(): lax.psum(query_weight_grad.astype(jnp.bfloat16), 'exp').astype(jnp.float32)  200 us
    psum x1, waiting for transfers between devices, body(): lax.psum((attention_gain_grad, mixture_gain_grad, router_grad), ('exp', '...  115 us
    reduce_scatter x1, waiting for transfers between devices, body(): lax.psum_scatter(grad_in_part.astype(jnp.bfloat16), 'tp', scatter_dimensi...  102 us
    all_to_all x1, blocking collectives, body(): lax.all_to_all(outgoing, 'exp', split_axis=0, concat_axis=1, tiled=True)  87.5 us
    all_to_all x1, blocking collectives, body(): lax.all_to_all(grad_outgoing, 'exp', split_axis=0, concat_axis=1, tiled=T...  85 us
    reduce_scatter x1, waiting for transfers between devices, body(): lax.psum_scatter(partial_out.astype(jnp.bfloat16), 'tp', scatter_dimensio...  74.5 us
    all_gather x1, waiting for transfers between devices, body(): grad_expert = lax.all_gather(grad_arrived, 'tp', axis=1, tiled=True)  68.7 us
    all_to_all x1, waiting for transfers between devices, body(): lax.all_to_all(grad_in, 'exp', split_axis=1, concat_axis=0, tiled=True)  58.3 us
  transfers between devices with their start and end apart: 12, of which 9 were waited for; matrix products, arithmetic and copies ran while one was open for 15% of the time, Pallas kernels for 0%

commit v1 on v0

v1 whole, which is shorter than its diff:
```python
import functools
import math

import jax
import jax.numpy as jnp
from jax import lax
from jax.experimental import pallas as pl
from jax.experimental.pallas import tpu as pltpu
from jax.sharding import PartitionSpec as P

HD = 128


EPS = 1e-05
HIGH = lax.Precision.HIGHEST


def inverse_rms(values):
    return lax.rsqrt(jnp.mean(values * values, axis=-1, keepdims=True) + EPS)


def norm_backward(grad_normed, normalized_input, factor):
    return factor * (
        grad_normed
        - normalized_input * jnp.mean(grad_normed * normalized_input, axis=-1, keepdims=True)
    )


def contract_rows(first_arg, second_arg):
    return lax.dot_general(
        first_arg, second_arg, (((0,), (0,)), ((), ())), preferred_element_type=jnp.float32
    )


def contract_cols(first_arg, second_arg):
    return lax.dot_general(
        first_arg, second_arg, (((1,), (1,)), ((), ())), preferred_element_type=jnp.float32
    )


def positions_of(segment_row):
    earlier = jnp.sum((segment_row[None, :] < segment_row[:, None]).astype(jnp.int32), axis=1)
    return jnp.arange(segment_row.shape[0], dtype=jnp.int32) - earlier


def rope_tables(positions):
    half_dim = HD // 2
    inverse_freq = 10000.0 ** (-2.0 * jnp.arange(half_dim).astype(jnp.float32) / HD)
    angles = positions.astype(jnp.float32)[:, None] * inverse_freq[None, :]
    cos, sin = jnp.cos(angles), jnp.sin(angles)
    return jnp.concatenate([cos, cos], axis=1), jnp.concatenate([-sin, sin], axis=1)


def rotate(values, cos_table, sin_table):
    return values * cos_table + pltpu.roll(values, HD // 2, 1) * sin_table


def masked_scores(query_rot, key_rot, info):
    scores = contract_cols(query_rot, key_rot) * (1.0 / math.sqrt(HD))
    seg_col, row_col, seg_row, row_row = info
    allowed = (seg_col == seg_row) & (row_row <= row_col)
    return jnp.where(allowed, scores, -1e30)


def attend_kernel(
    rows_ref,
    query_weight,
    key_weight,
    value_weight,
    query_norm,
    key_norm,
    cos_ref,
    sin_ref,
    seg_col,
    row_col,
    seg_row,
    row_row,
    query_ref,
    key_ref,
    query_rot_ref,
    key_rot_ref,
    value_ref,
    attended_ref,
    total_ref,
):
    rows = rows_ref[...]
    cos_table, sin_table = cos_ref[...], sin_ref[...]
    info = (seg_col[...], row_col[...], seg_row[...], row_row[...])
    query_ref[...] = jnp.dot(rows, query_weight[...], preferred_element_type=jnp.float32)
    key_ref[...] = jnp.dot(rows, key_weight[...], preferred_element_type=jnp.float32)
    value_ref[...] = jnp.dot(
        rows, value_weight[...], preferred_element_type=jnp.float32
    ).astype(jnp.bfloat16)
    for head in range(query_ref.shape[1] // HD):
        span = slice(head * HD, (head + 1) * HD)
        queries, keys = query_ref[:, span], key_ref[:, span]
        query_rot = rotate(
            queries * inverse_rms(queries) * query_norm[:, span], cos_table, sin_table
        ).astype(jnp.bfloat16)
        key_rot = rotate(
            keys * inverse_rms(keys) * key_norm[:, span], cos_table, sin_table
        ).astype(jnp.bfloat16)
        query_rot_ref[:, span] = query_rot
        key_rot_ref[:, span] = key_rot
        scores = masked_scores(query_rot, key_rot, info)
        peak = jnp.max(scores, axis=-1, keepdims=True)
        shifted = jnp.exp(scores - peak)
        denominator = jnp.sum(shifted, axis=-1, keepdims=True)
        weights = (shifted / denominator).astype(jnp.bfloat16)
        attended_ref[:, span] = jnp.dot(
            weights, value_ref[:, span], preferred_element_type=jnp.float32
        ).astype(jnp.bfloat16)
        total_ref[head] = peak + jnp.log(denominator)


def attend_back_kernel(
    which_ref,
    row_grad_ref,
    output_weight,
    query_ref,
    key_ref,
    query_rot_ref,
    key_rot_ref,
    value_ref,
    total_ref,
    query_norm,
    key_norm,
    cos_ref,
    sin_ref,
    seg_col,
    row_col,
    seg_row,
    row_row,
    grad_query_ref,
    grad_key_ref,
    grad_value_ref,
    query_norm_grad,
    key_norm_grad,
):
    cos_table, sin_table = cos_ref[...], -sin_ref[...]
    info = (seg_col[...], row_col[...], seg_row[...], row_row[...])
    inv_sqrt = 1.0 / math.sqrt(HD)
    grad_attended = contract_cols(row_grad_ref[...], output_weight[...]).astype(jnp.bfloat16)

    def finish(grad_rot, raw, gain, out_ref, gain_ref, span):
        grad_norm = rotate(grad_rot, cos_table, sin_table)
        scale = inverse_rms(raw)
        hat = raw * scale
        gain_ref[:, span] = jnp.sum(grad_norm * hat, axis=0, keepdims=True)
        out_ref[:, span] = norm_backward(grad_norm * gain, hat, scale).astype(jnp.bfloat16)

    for head in range(query_ref.shape[1] // HD):
        span = slice(head * HD, (head + 1) * HD)
        query_rot, key_rot = query_rot_ref[:, span], key_rot_ref[:, span]
        grad_head = grad_attended[:, span]
        probs = jnp.exp(masked_scores(query_rot, key_rot, info) - total_ref[head])
        grad_weights = contract_cols(grad_head, value_ref[:, span])
        inner = jnp.sum(grad_weights * probs, axis=-1, keepdims=True)
        grad_scores = (probs * (grad_weights - inner)).astype(jnp.bfloat16)
        grad_value_ref[:, span] = contract_rows(probs.astype(jnp.bfloat16), grad_head).astype(
            jnp.bfloat16
        )
        grad_query_rot = (
            jnp.dot(grad_scores, key_rot, preferred_element_type=jnp.float32) * inv_sqrt
        )
        grad_key_rot = contract_rows(grad_scores, query_rot) * inv_sqrt
        finish(
            grad_query_rot,
            query_ref[:, span],
            query_norm[:, span],
            grad_query_ref,
            query_norm_grad,
            span,
        )
        finish(
            grad_key_rot, key_ref[:, span], key_norm[:, span], grad_key_ref, key_norm_grad, span
        )


def head_specs(length, width, model_width, wide):
    whole = pl.BlockSpec((length, model_width), lambda i: (0, 0))
    across = pl.BlockSpec((model_width, wide), lambda i: (0, i))
    down = pl.BlockSpec((wide, model_width), lambda i: (i, 0))
    heads = pl.BlockSpec((length, wide), lambda i: (0, i))
    gain = pl.BlockSpec((1, wide), lambda i: (0, i))
    total = pl.BlockSpec((wide // HD, length, 1), lambda i: (i, 0, 0))
    table = pl.BlockSpec((length, HD), lambda i: (0, 0))
    col = pl.BlockSpec((length, 1), lambda i: (0, 0))
    row = pl.BlockSpec((1, length), lambda i: (0, 0))
    return whole, across, down, heads, gain, total, [table, table, col, col, row, row]


def attend(rows, weights, gains, tables):
    length, model_width = rows.shape
    width = weights[0].shape[1]
    wide = min(2 * HD, width)
    whole, across, _, heads, gain, total, table_specs = head_specs(
        length, width, model_width, wide
    )
    low = jnp.bfloat16
    types = [jnp.float32, jnp.float32, low, low, low, low]
    return pl.pallas_call(
        attend_kernel,
        grid=(width // wide,),
        in_specs=[whole, across, across, across, gain, gain] + table_specs,
        out_specs=[heads] * 6 + [total],
        out_shape=[jax.ShapeDtypeStruct((length, width), t) for t in types]
        + [jax.ShapeDtypeStruct((width // HD, length, 1), jnp.float32)],
        cost_estimate=pl.CostEstimate(
            flops=6 * length * width * (model_width + length),
            bytes_accessed=2 * model_width * (length + 3 * width),
            transcendentals=width // HD * length * length,
        ),
        name="attend",
    )(rows, *weights, *gains, *tables)


def attend_back(which, row_grad, output_weight, saved, gains, tables, wide):
    length, model_width = row_grad.shape
    low = jnp.bfloat16
    whole = pl.BlockSpec((length, model_width), lambda i, w: (0, 0))
    down = pl.BlockSpec((wide, model_width), lambda i, w: (w[0], 0))
    heads = pl.BlockSpec((length, wide), lambda i, w: (0, w[0]))
    gain = pl.BlockSpec((1, wide), lambda i, w: (0, w[0]))
    total = pl.BlockSpec((wide // HD, length, 1), lambda i, w: (w[0], 0, 0))
    table = pl.BlockSpec((length, HD), lambda i, w: (0, 0))
    col = pl.BlockSpec((length, 1), lambda i, w: (0, 0))
    row = pl.BlockSpec((1, length), lambda i, w: (0, 0))
    out = pl.BlockSpec((length, wide), lambda i, w: (0, 0))
    gain_out = pl.BlockSpec((1, wide), lambda i, w: (0, 0))
    return pl.pallas_call(
        attend_back_kernel,
        grid_spec=pltpu.PrefetchScalarGridSpec(
            num_scalar_prefetch=1,
            grid=(1,),
            in_specs=[whole, down]
            + [heads] * 5
            + [total, gain, gain, table, table, col, col, row, row],
            out_specs=[out] * 3 + [gain_out] * 2,
        ),
        out_shape=[jax.ShapeDtypeStruct((length, wide), low)] * 3
        + [jax.ShapeDtypeStruct((1, wide), jnp.float32)] * 2,
        cost_estimate=pl.CostEstimate(
            flops=2 * length * wide * (model_width + 5 * length),
            bytes_accessed=2 * model_width * (length + wide) + 16 * length * wide,
            transcendentals=wide // HD * length * length,
        ),
        name="attend_back",
    )(which, row_grad, output_weight, *saved, *gains, *tables)


AXES = ("exp", "tp")


def after(value, others):
    return lax.optimization_barrier((value, others))[0]


class Links:
    def __init__(self, n_exp, n_tp):
        self.n_exp, self.n_tp, self.n_z = n_exp, n_tp, n_exp // 2

    def send(self, value, place):
        pairs = []
        for z in range(self.n_z):
            for x in range(2):
                for y in range(2):
                    for c in range(2):
                        z2, x2, y2, c2 = place(z, x, y, c)
                        pairs.append(((z * 2 + x) * 4 + y * 2 + c, (z2 * 2 + x2) * 4 + y2 * 2 + c2))
        return lax.ppermute(value, AXES, pairs)

    def core(self, value):
        return self.send(value, lambda z, x, y, c: (z, x, y, 1 - c))

    def flip_x(self, value):
        return self.send(value, lambda z, x, y, c: (z, 1 - x, y, c))

    def flip_y(self, value):
        return self.send(value, lambda z, x, y, c: (z, x, 1 - y, c))

    def first(self, value):
        return self.send(value, lambda z, x, y, c: (z, x ^ (1 - c), y ^ c, c))

    def second(self, value):
        return self.send(value, lambda z, x, y, c: (z, x ^ c, y ^ (1 - c), c))

    def along_z(self, value, steps):
        return self.send(value, lambda z, x, y, c: ((z + steps) % self.n_z, x, y, c))

    def flip_z(self, value, bit):
        return self.send(value, lambda z, x, y, c: (z ^ bit, x, y, c))

    def spread(self, block, axis=0):
        near = jnp.concatenate([block, self.first(block)], axis=axis)
        plane = jnp.concatenate([near, self.second(near)], axis=axis)
        return plane, self.core(plane)

    def collect(self, plane, partner, kind):
        total = plane.astype(jnp.float32) + self.core(partner.astype(kind)).astype(jnp.float32)
        half = total.shape[0] // 2
        total = total[:half] + self.second(total[half:].astype(kind)).astype(jnp.float32)
        half = half // 2
        return total[:half] + self.first(total[half:].astype(kind)).astype(jnp.float32)

    def tp_rows(self, block):
        far = self.flip_y(block)
        return jnp.concatenate([block, self.core(block), far, self.core(far)], axis=0)

    def tp_sum(self, part):
        rows = part.shape[0] // 4
        sent = jnp.concatenate([part[rows : 2 * rows], part[3 * rows :]], axis=0)
        got = self.core(sent.astype(jnp.bfloat16)).astype(jnp.float32)
        far = part[2 * rows : 3 * rows] + got[rows:]
        return part[:rows] + got[:rows] + self.flip_y(far.astype(jnp.bfloat16)).astype(jnp.float32)

    def sum_exp(self, value):
        value = value + self.flip_x(value)
        for bit in range(self.n_z.bit_length() - 1):
            value = value + self.flip_z(value, 1 << bit)
        return value

    def sum_tp(self, value):
        value = value + self.core(value)
        return value + self.flip_y(value)


def gather_expert_rows(local_rows):
    return lax.all_gather(local_rows, "tp", axis=1, tiled=True)


def moe_slots(
    mixture_in, probabilities, grad_out, routes, capacity, gate_weight, up_weight, down_weight
):
    tok_rows, model_width = mixture_in.shape
    top_count = routes.shape[1]
    experts_all = probabilities.shape[1]
    expert_ids = jnp.arange(experts_all, dtype=jnp.int32)
    chosen = (routes[:, :, None] == expert_ids[None, None, :]).astype(jnp.float32)
    gate_values = jnp.sum(chosen * probabilities[:, None, :], axis=-1)
    assigned = routes.reshape(-1)
    matches = (assigned[:, None] == expert_ids[None, :]).astype(jnp.int32)
    earlier = jnp.sum(jnp.cumsum(matches, axis=0) * matches, axis=1) - 1
    slot_ids = jnp.where(earlier < capacity, assigned * capacity + earlier, experts_all * capacity)
    assign_count = tok_rows * top_count
    owners = (
        jnp.full((experts_all * capacity + 1,), assign_count, jnp.int32)
        .at[slot_ids]
        .set(jnp.arange(assign_count, dtype=jnp.int32))[:-1]
    )
    source_rows = owners // top_count
    input_pad = jnp.concatenate([mixture_in, jnp.zeros((1, model_width), jnp.bfloat16)], axis=0)
    outgoing = input_pad[source_rows].reshape(experts_all, capacity, model_width)
    arrived = lax.all_to_all(outgoing, "exp", split_axis=0, concat_axis=1, tiled=True)
    expert_in = gather_expert_rows(arrived)
    gate_pre = jnp.einsum(
        "erd,edf->erf", expert_in, gate_weight, preferred_element_type=jnp.float32
    )
    up_pre = jnp.einsum("erd,edf->erf", expert_in, up_weight, preferred_element_type=jnp.float32)
    hidden = (jax.nn.silu(gate_pre) * up_pre).astype(jnp.bfloat16)
    partial_out = jnp.einsum(
        "erf,efd->erd", hidden, down_weight, preferred_element_type=jnp.float32
    )
    returned = lax.psum_scatter(
        partial_out.astype(jnp.bfloat16), "tp", scatter_dimension=1, tiled=True
    )
    combined = lax.all_to_all(returned, "exp", split_axis=1, concat_axis=0, tiled=True)
    output_pad = jnp.concatenate(
        [combined.reshape(-1, model_width), jnp.zeros((1, model_width), jnp.bfloat16)], axis=0
    )
    expert_out = output_pad[slot_ids].astype(jnp.float32).reshape(tok_rows, top_count, model_width)
    mixture = jnp.sum(gate_values[:, :, None] * expert_out, axis=1)
    grad_gate = jnp.sum(grad_out[:, None, :] * expert_out, axis=-1)
    grad_sent = (
        (gate_values[:, :, None] * grad_out[:, None, :])
        .reshape(assign_count, model_width)
        .astype(jnp.bfloat16)
    )
    grad_pad = jnp.concatenate([grad_sent, jnp.zeros((1, model_width), jnp.bfloat16)], axis=0)
    grad_outgoing = grad_pad[owners].reshape(experts_all, capacity, model_width)
    grad_arrived = lax.all_to_all(grad_outgoing, "exp", split_axis=0, concat_axis=1, tiled=True)
    grad_expert = lax.all_gather(grad_arrived, "tp", axis=1, tiled=True)
    gate_pre = jnp.einsum(
        "erd,edf->erf", expert_in, gate_weight, preferred_element_type=jnp.float32
    )
    up_pre = jnp.einsum("erd,edf->erf", expert_in, up_weight, preferred_element_type=jnp.float32)
    gate_sig = jax.nn.sigmoid(gate_pre)
    gate_act = gate_pre * gate_sig
    hidden = (gate_act * up_pre).astype(jnp.bfloat16)
    grad_hidden = jnp.einsum(
        "erd,efd->erf", grad_expert, down_weight, preferred_element_type=jnp.float32
    )
    down_grad = jnp.einsum("erf,erd->efd", hidden, grad_expert, preferred_element_type=jnp.float32)
    grad_gate_pre = (grad_hidden * up_pre * gate_sig * (1.0 + gate_pre * (1.0 - gate_sig))).astype(
        jnp.bfloat16
    )
    grad_up_pre = (grad_hidden * gate_act).astype(jnp.bfloat16)
    gate_grad = jnp.einsum(
        "erd,erf->edf", expert_in, grad_gate_pre, preferred_element_type=jnp.float32
    )
    up_grad = jnp.einsum("erd,erf->edf", expert_in, grad_up_pre, preferred_element_type=jnp.float32)
    grad_in_part = jnp.einsum(
        "erf,edf->erd", grad_gate_pre, gate_weight, preferred_element_type=jnp.float32
    ) + jnp.einsum("erf,edf->erd", grad_up_pre, up_weight, preferred_element_type=jnp.float32)
    grad_in = lax.psum_scatter(
        grad_in_part.astype(jnp.bfloat16), "tp", scatter_dimension=1, tiled=True
    )
    grad_home = lax.all_to_all(grad_in, "exp", split_axis=1, concat_axis=0, tiled=True)
    home_pad = jnp.concatenate(
        [grad_home.reshape(-1, model_width), jnp.zeros((1, model_width), jnp.bfloat16)], axis=0
    )
    grad_assigned = home_pad[slot_ids].astype(jnp.float32).reshape(tok_rows, top_count, model_width)
    weighted = probabilities * jnp.sum(chosen * grad_gate[:, :, None], axis=1)
    return mixture, jnp.sum(grad_assigned, axis=1), weighted, gate_grad, up_grad, down_grad


def kept_experts(routes, experts_all, capacity):
    tok_rows = routes.shape[0]
    expert_ids = jnp.arange(experts_all, dtype=jnp.int32)
    member = jnp.sum((routes[:, :, None] == expert_ids[None, None, :]).astype(jnp.float32), axis=1)
    row = jnp.arange(tok_rows, dtype=jnp.int32)
    before = (row[None, :] < row[:, None]).astype(jnp.bfloat16)
    rank = jnp.dot(before, member.astype(jnp.bfloat16), preferred_element_type=jnp.float32)
    return jnp.where(rank < capacity, member, 0.0)


def expert_kernel(
    carried,
    tile,
    place,
    near_ref,
    far_ref,
    grad_near_ref,
    grad_far_ref,
    kept_ref,
    router_ref,
    gate_hbm,
    up_hbm,
    down_hbm,
    *refs,
):
    (
        mix_hbm,
        part_hbm,
        sum_ref,
        rows_all,
        grad_all,
        hidden_all,
        gate_all,
        up_all,
        rows,
        grads,
        gate_w,
        up_w,
        down_w,
        mix,
        part,
        hidden_v,
        gate_v,
        up_v,
        sem_in,
        sem_out,
    ) = refs[carried:]
    local_experts, _, hidden_width = gate_w.shape
    spans = [slice(e * hidden_width, (e + 1) * hidden_width) for e in range(local_experts)]
    loads = {}
    plan = [(("x", 0), near_ref, rows.at[0])]
    for e in range(local_experts):
        plan.append((("g", e), gate_hbm.at[e], gate_w.at[e]))
        plan.append((("u", e), up_hbm.at[e], up_w.at[e]))
        if e == 0:
            plan.append((("c", 0), grad_near_ref, grads.at[0]))
        plan.append((("d", e), down_hbm.at[spans[e], :], down_w.at[spans[e], :]))
    plan.append((("x", 1), far_ref, rows.at[1]))
    plan.append((("c", 1), grad_far_ref, grads.at[1]))
    for n, (key, source, target) in enumerate(plan):
        loads[key] = pltpu.make_async_copy(source, target, sem_in.at[n])
        loads[key].start()
    stores = []

    def store(source, target):
        copy = pltpu.make_async_copy(source, target, sem_out.at[len(stores)])
        copy.start()
        stores.append(copy)

    for t in range(2):
        at = pl.ds(place + t * tile, tile)
        loads["x", t].wait()
        store(rows.at[t], rows_all.at[at, :])
        x = rows[t]
        logits = jnp.dot(x, router_ref[...], preferred_element_type=jnp.float32)
        shifted = jnp.exp(logits - jnp.max(logits, axis=-1, keepdims=True))
        kept = kept_ref[t * tile : (t + 1) * tile, :]
        gates = shifted[:, :local_experts] / jnp.sum(shifted, axis=-1, keepdims=True) * kept
        sums = []
        total = None
        for e in range(local_experts):
            gate = gates[:, e : e + 1]
            if t == 0:
                loads["g", e].wait()
            gate_pre = jnp.dot(x, gate_w[e], preferred_element_type=jnp.float32)
            if t == 0:
                loads["u", e].wait()
            up_pre = jnp.dot(x, up_w[e], preferred_element_type=jnp.float32)
            if e == 0:
                loads["c", t].wait()
                store(grads.at[t], grad_all.at[at, :])
            if t == 0:
                loads["d", e].wait()
            back = contract_cols(grads[t], down_w[spans[e], :]) * gate
            sig = jax.nn.sigmoid(gate_pre)
            act = gate_pre * sig
            hidden = (act * up_pre).astype(jnp.bfloat16).astype(jnp.float32)
            sums.append(jnp.sum(hidden * back, axis=-1, keepdims=True))
            hidden_v[t, :, spans[e]] = (hidden * gate).astype(jnp.bfloat16)
            grad_gate = (back * up_pre * sig * (1.0 + gate_pre * (1.0 - sig))).astype(
                jnp.bfloat16
            )
            grad_up = (back * act).astype(jnp.bfloat16)
            gate_v[t, e] = grad_gate
            up_v[t, e] = grad_up
            piece = contract_cols(grad_gate, gate_w[e]) + contract_cols(grad_up, up_w[e])
            total = piece if total is None else total + piece
        part[t] = total.astype(jnp.bfloat16)
        store(part.at[t], part_hbm.at[pl.ds(t * tile, tile), :])
        for e in range(local_experts):
            store(gate_v.at[t, e], gate_all.at[e, at, :])
            store(up_v.at[t, e], up_all.at[e, at, :])
        store(hidden_v.at[t], hidden_all.at[at, :])
        sum_ref[t * tile : (t + 1) * tile, :] = jnp.concatenate(sums, axis=1)
        mix[t] = jnp.dot(
            hidden_v[t], down_w[...], preferred_element_type=jnp.float32
        ).astype(jnp.bfloat16)
        store(mix.at[t], mix_hbm.at[pl.ds(t * tile, tile), :])
    for copy in stores:
        copy.wait()


def run_experts(
    place, count, rows, grads, kept, router, gate_weight, up_weight, down_flat, carried
):
    tile, model_width = rows[0].shape
    local_experts, _, hidden_width = gate_weight.shape
    flat = local_experts * hidden_width
    tok_count = 2 * tile
    whole = tok_count * count
    low = jnp.bfloat16
    hbm = pl.BlockSpec(memory_space=pl.ANY)
    vmem = pl.BlockSpec(memory_space=pltpu.VMEM)
    out = pl.pallas_call(
        functools.partial(expert_kernel, len(carried), tile, place * tok_count),
        in_specs=[hbm] * 4 + [vmem] * 2 + [hbm] * (3 + len(carried)),
        out_specs=[hbm, hbm, vmem] + [hbm] * 5,
        out_shape=[
            jax.ShapeDtypeStruct((tok_count, model_width), low),
            jax.ShapeDtypeStruct((tok_count, model_width), low),
            jax.ShapeDtypeStruct((tok_count, local_experts), jnp.float32),
            jax.ShapeDtypeStruct((whole, model_width), low),
            jax.ShapeDtypeStruct((whole, model_width), low),
            jax.ShapeDtypeStruct((whole, flat), low),
            jax.ShapeDtypeStruct((local_experts, whole, hidden_width), low),
            jax.ShapeDtypeStruct((local_experts, whole, hidden_width), low),
        ],
        scratch_shapes=[
            pltpu.VMEM((2, tile, model_width), low),
            pltpu.VMEM((2, tile, model_width), low),
            pltpu.VMEM(gate_weight.shape, low),
            pltpu.VMEM(up_weight.shape, low),
            pltpu.VMEM(down_flat.shape, low),
            pltpu.VMEM((2, tile, model_width), low),
            pltpu.VMEM((2, tile, model_width), low),
            pltpu.VMEM((2, tile, flat), low),
            pltpu.VMEM((2, local_experts, tile, hidden_width), low),
            pltpu.VMEM((2, local_experts, tile, hidden_width), low),
            pltpu.SemaphoreType.DMA((4 + 3 * local_experts,)),
            pltpu.SemaphoreType.DMA((2 * (5 + 2 * local_experts),)),
        ],
        input_output_aliases={9 + i: 3 + i for i in range(len(carried))},
        cost_estimate=pl.CostEstimate(
            flops=16 * tok_count * model_width * flat,
            bytes_accessed=12 * model_width * (tok_count + flat),
            transcendentals=tok_count * flat,
        ),
        name="experts",
    )(*rows, *grads, kept, router, gate_weight, up_weight, down_flat, *carried)
    return out[:3], list(out[3:])


class HalfSum:
    def __init__(self, links, value):
        self.links, self.value = links, value
        self.bits = [1 << b for b in range(links.n_z.bit_length() - 1)]

    def stages(self):
        return 2 * len(self.bits)

    def go(self, stage, ties=()):
        links, value, count = self.links, self.value, len(self.bits)
        z = lax.axis_index("exp") // 2
        if stage < count:
            bit = self.bits[stage]
            upper = (z // bit) % 2
            half = value.shape[0] // 2
            kept = lax.dynamic_slice_in_dim(value, upper * half, half, axis=0)
            sent = lax.dynamic_slice_in_dim(value, (1 - upper) * half, half, axis=0)
            got = links.flip_z(after(sent.astype(jnp.bfloat16), ties), bit)
            value = kept + got.astype(jnp.float32)
            if stage == count - 1:
                value = value.astype(jnp.bfloat16)
        else:
            bit = self.bits[2 * count - 1 - stage]
            got = links.flip_z(after(value, ties), bit)
            value = jnp.where(
                (z // bit) % 2 == 0,
                jnp.concatenate([value, got], axis=0),
                jnp.concatenate([got, value], axis=0),
            )
        self.value = value
        return got


class Spread:
    def __init__(self, links, block, order):
        self.links, self.order = links, order
        self.blocks, self.near, self.far, self.other = {0: block}, {}, {}, {}

    def go_z(self, k, ties=()):
        self.blocks[k] = self.links.along_z(after(self.blocks[0], ties), self.order[k])
        return self.blocks[k]

    def go_near(self, k, ties=()):
        block = after(self.blocks[k], ties)
        self.near[k] = jnp.concatenate([block, self.links.first(block)], axis=0)
        return self.near[k]

    def go_far(self, k, ties=()):
        self.far[k] = self.links.second(after(self.near[k], ties))
        return self.far[k]

    def go_core(self, k, ties=()):
        near, far = after((self.near[k], self.far[k]), ties)
        self.other[k] = (self.links.core(near), self.links.core(far))
        return self.other[k]

    def plane(self, k, side):
        return self.other[k] if side else (self.near[k], self.far[k])


class Gathering:
    def __init__(self, links, order):
        self.links, self.order, self.terms = links, order, {}

    def total(self, k, first, last):
        wide = [t[first:last].astype(jnp.float32) for t in self.terms[k]]
        return functools.reduce(jnp.add, wide)

    def go_core(self, k, own, partner, ties=()):
        self.terms[k] = [own, self.links.core(after(partner, ties))]
        return self.terms[k][-1]

    def go_second(self, k, ties=()):
        rows = self.terms[k][0].shape[0]
        sent = self.total(k, rows // 2, rows).astype(jnp.bfloat16)
        self.terms[k].append(self.links.second(after(sent, ties)))
        return self.terms[k][-1]

    def go_first(self, k, ties=()):
        rows = self.terms[k][0].shape[0]
        sent = self.total(k, rows // 4, rows // 2).astype(jnp.bfloat16)
        self.terms[k].append(self.links.first(after(sent, ties)))
        return self.terms[k][-1]

    def go_z(self, k, ties=()):
        rows = self.terms[k][0].shape[0]
        sent = self.total(k, 0, rows // 4)
        if k:
            sent = self.links.along_z(after(sent.astype(jnp.bfloat16), ties), -self.order[k])
        self.terms[k] = [sent]
        return sent

    def home(self):
        return functools.reduce(
            jnp.add, [self.terms[k][0].astype(jnp.float32) for k in range(len(self.order))]
        )


def moe_dense(
    links,
    order,
    attention_in,
    mixture_in,
    grads,
    kept_chunks,
    router_weight,
    gate_weight,
    up_weight,
    down_weight,
):
    tok_rows, model_width = mixture_in.shape
    local_experts, _, hidden_width = gate_weight.shape
    experts_all = router_weight.shape[1]
    first_expert = lax.axis_index("exp") * local_experts
    down_flat = down_weight.reshape(local_experts * hidden_width, model_width)
    router = jnp.roll(router_weight, -first_expert, axis=1)
    n_z = links.n_z
    kept_own = [
        [lax.dynamic_slice_in_dim(k, first_expert, local_experts, axis=1) for k in kept_chunks[r]]
        for r in order
    ]
    rows = Spread(links, mixture_in, order)
    back = Gathering(links, order)
    mix = Gathering(links, order)
    carried = []
    own, partner = [None] * n_z, [None] * n_z

    def experts(k, side, ties):
        nonlocal carried
        result, carried = run_experts(
            2 * k + side,
            2 * n_z,
            rows.plane(k, side),
            grads.plane(k, side),
            after(kept_own[k][side], ties),
            router,
            gate_weight,
            up_weight,
            down_flat,
            carried,
        )
        return result

    rows.go_near(0)
    rows.go_z(1)
    grads.go_core(0)
    grads.go_core(1)
    rows.go_far(0)
    held = [grads.go_near(2)]
    for k in range(n_z):
        own[k] = experts(k, 0, held)
        held = [rows.go_core(k)]
        if k + 1 < n_z:
            held.append(rows.go_near(k + 1))
        if k + 2 < n_z:
            held.append(rows.go_z(k + 2, [rows.blocks[k + 1]]))
            if k == 0:
                held.append(grads.go_far(2))
                grads.go_core(2)
            elif k == 1:
                held.append(grads.go_far(3))
                grads.go_core(3)
        if k >= 2:
            held.append(back.go_first(k - 2))
        if k >= 1:
            held.append(back.go_core(k - 1, own[k - 1][1], partner[k - 1][1]))
        partner[k] = experts(k, 1, held)
        held = []
        if k + 1 < n_z:
            rows.go_far(k + 1)
        if k == 0:
            held.append(grads.go_near(3))
        if k >= 2:
            held.append(back.go_z(k - 2))
        if k >= 1:
            held.append(back.go_second(k - 1))
    step_one = [
        back.go_core(n_z - 1, own[n_z - 1][1], partner[n_z - 1][1]),
        back.go_first(n_z - 2),
    ]
    rows_all, grad_all, hidden_all, gate_all, up_all = carried
    step_two = [
        back.go_second(n_z - 1),
        back.go_z(n_z - 2),
        mix.go_core(0, own[0][0], partner[0][0], step_one),
        mix.go_core(1, own[1][0], partner[1][0], step_one),
    ]
    gate_all = after(gate_all, step_one)
    gate_grad = jnp.stack([contract_rows(rows_all, gate_all[e]) for e in range(local_experts)])
    step_three = [
        back.go_first(n_z - 1),
        mix.go_core(2, own[2][0], partner[2][0], step_two),
        mix.go_core(3, own[3][0], partner[3][0], step_two),
    ]
    up_all = after(up_all, step_two)
    up_grad = jnp.stack([contract_rows(rows_all, up_all[e]) for e in range(local_experts)])
    back.go_z(n_z - 1)
    early_x = links.flip_x(after(attention_in, step_three))
    mix.go_second(0, [early_x])
    hidden_all = after(hidden_all, step_three)
    down_grad = contract_rows(hidden_all, grad_all).reshape(
        local_experts, hidden_width, model_width
    )
    full = []
    for parts in (own, partner):
        planes = []
        for k in range(n_z):
            local = parts[k][2].reshape(-1, tok_rows, local_experts).transpose(0, 2, 1)
            zero = jnp.zeros((local.shape[0], experts_all, tok_rows), jnp.float32)
            planes.append(lax.dynamic_update_slice_in_dim(zero, local, first_expert, axis=1))
        full.append(jnp.stack(planes, axis=1))
    small = links.collect(full[0], full[1], jnp.float32)[0]
    weighted = small[0]
    for k in range(1, n_z):
        weighted = weighted + links.along_z(small[k], -order[k])
    input_grad = after(back.home(), [mix.terms[0][-1]])
    return mix, early_x, input_grad, weighted.T, gate_grad, up_grad, down_grad


def body(
    mesh_sizes,
    tokens,
    cotangent,
    attention_gain,
    query_weight,
    key_weight,
    value_weight,
    output_weight,
    query_norm,
    key_norm,
    mixture_gain,
    router_weight,
    gate_weight,
    up_weight,
    down_weight,
    routes,
    segments,
):
    tok_rows, model_width = tokens.shape
    top_count = routes.shape[1]
    experts_all = router_weight.shape[1]
    capacity = tok_rows * top_count * 7 // (8 * experts_all)
    local_width = query_weight.shape[1]
    n_exp, n_tp = mesh_sizes
    dense = experts_all <= 2 * top_count and n_tp == 4 and n_exp % 2 == 0
    links = Links(n_exp, n_tp)
    grad_out = cotangent.astype(jnp.float32)
    if dense:
        kept = kept_experts(routes, experts_all, capacity).T.astype(jnp.bfloat16)
        kept_z = jnp.stack([kept] + [links.along_z(kept, r) for r in range(1, n_exp // 2)])
        kept_planes = links.spread(kept_z[None])
        kept_chunks = [
            [
                plane[:, r].transpose(0, 2, 1).reshape(-1, experts_all).astype(jnp.float32)
                for plane in kept_planes
            ]
            for r in range(n_exp // 2)
        ]
        order = [0, 1, 3, 2] if n_exp == 8 else list(range(n_exp // 2))
        grads = Spread(links, cotangent, order)
        held = [grads.go_near(0), grads.go_z(1)]
    else:
        held = []
    inputs = tokens.astype(jnp.float32)
    scale_one = inverse_rms(inputs)
    normed_one = inputs * scale_one
    attention_in = (normed_one * attention_gain).astype(jnp.bfloat16)
    segment_row = segments[0]
    tp_order = lax.axis_index("tp") ^ jnp.arange(n_tp, dtype=jnp.int32)
    positions = positions_of(segment_row).reshape(n_tp, tok_rows)[tp_order].reshape(-1)
    segment_rel = segment_row.reshape(n_tp, tok_rows)[tp_order].reshape(-1)
    row_rel = (
        tp_order[:, None] * tok_rows + jnp.arange(tok_rows, dtype=jnp.int32)[None, :]
    ).reshape(-1)
    tables = (
        *rope_tables(positions),
        segment_rel[:, None],
        row_rel[:, None],
        segment_rel[None, :],
        row_rel[None, :],
    )
    gains = (query_norm[None, :], key_norm[None, :])
    gathered_rows = links.tp_rows(attention_in)
    rows_held = after(gathered_rows, held)
    if dense:
        held = [
            grads.go_far(0, [gathered_rows]),
            grads.go_near(1, [grads.far[0]]),
            grads.go_z(2, [grads.blocks[1]]),
        ]
    *saved, attended, log_totals = attend(
        rows_held, (query_weight, key_weight, value_weight), gains, tables
    )
    partial_block = jnp.dot(after(attended, held), output_weight, preferred_element_type=jnp.float32)
    held = [grads.go_far(1), grads.go_z(3, [grads.blocks[2]])] if dense else []
    attention_block = after(links.tp_sum(partial_block), held)
    middle = inputs + attention_block
    scale_two = inverse_rms(middle)
    normed_two = middle * scale_two
    mixture_in = (normed_two * mixture_gain).astype(jnp.bfloat16)
    logits = jnp.dot(mixture_in, router_weight, preferred_element_type=jnp.float32)
    probabilities = jax.nn.softmax(logits, axis=-1)
    if dense:
        mix, early_x, grad_expert_in, weighted, gate_grad, up_grad, down_grad = moe_dense(
            links,
            order,
            attention_in,
            mixture_in,
            grads,
            kept_chunks,
            router_weight,
            gate_weight,
            up_weight,
            down_weight,
        )
    else:
        mixture, grad_expert_in, weighted, gate_grad, up_grad, down_grad = moe_slots(
            mixture_in,
            probabilities,
            grad_out,
            routes,
            capacity,
            gate_weight,
            up_weight,
            down_weight,
        )
        early_x = links.flip_x(attention_in)
    grad_logits = weighted - probabilities * jnp.sum(weighted, axis=-1, keepdims=True)
    router_grad = jnp.dot(mixture_in.astype(jnp.float32).T, grad_logits, precision=HIGH)
    grad_mixture_in = grad_expert_in + jnp.dot(
        grad_logits, router_weight.astype(jnp.float32).T, precision=HIGH
    )
    mixture_gain_grad = jnp.sum(grad_mixture_in * normed_two, axis=0)
    grad_middle = grad_out + norm_backward(grad_mixture_in * mixture_gain, normed_two, scale_two)
    grad_attention = grad_middle.astype(jnp.bfloat16)
    row_grad = links.tp_rows(grad_attention)
    wide = local_width // 2
    side = lax.axis_index("exp") % 2
    peer_attention = links.flip_x(grad_attention)
    attended_other = lax.dynamic_slice_in_dim(attended, (1 - side) * wide, wide, axis=1)
    peer_rows = links.tp_rows(after(early_x, row_grad))
    held = [peer_attention, peer_rows]
    if dense:
        held.append(mix.go_first(0))
    results = [None, None]
    for turn in range(2):
        which = 1 - side if turn == 0 else side
        ties = [r[0] for r in results[:turn]]
        if turn == 1:
            ties += held
        results[turn] = attend_back(
            after(which.astype(jnp.int32)[None], ties),
            row_grad,
            output_weight,
            (*saved, log_totals),
            gains,
            tables,
            wide,
        )
    other = jnp.concatenate(results[0][:3], axis=1)
    peer_grads = links.flip_x(after(other, held))
    attended_peer = links.flip_x(after(attended_other, held))
    peer_row_grad = links.tp_rows(after(peer_attention, held))
    own_grads = jnp.concatenate(results[1][:3], axis=1)

    def in_order(own_part, other_part, axis):
        return jnp.where(
            side == 0,
            jnp.concatenate([own_part, other_part], axis=axis),
            jnp.concatenate([other_part, own_part], axis=axis),
        )

    grad_queries, grad_keys, grad_values, query_norm_grad, key_norm_grad = [
        in_order(results[1][i], results[0][i], 1) for i in range(5)
    ]
    query_norm_grad, key_norm_grad = query_norm_grad[0], key_norm_grad[0]
    total_grad = contract_cols(grad_queries, query_weight)
    total_grad = total_grad + contract_cols(grad_keys, key_weight)
    total_grad = total_grad + contract_cols(grad_values, value_weight)
    held = [peer_row_grad, attended_peer]
    grad_attention_in = links.tp_sum(after(total_grad, held))
    attended_own = lax.dynamic_slice_in_dim(attended, side * wide, wide, axis=1)
    own_parts = [attended_own] + [gathered_rows] * 3
    peer_parts = [attended_peer] + [peer_rows] * 3
    own_ends = [row_grad] + [own_grads[:, i * wide : (i + 1) * wide] for i in range(3)]
    peer_ends = [peer_row_grad] + [peer_grads[:, i * wide : (i + 1) * wide] for i in range(3)]
    pieces = [
        HalfSum(links, contract_rows(p, q) + contract_rows(r, s))
        for p, q, r, s in zip(own_parts, own_ends, peer_parts, peer_ends)
    ]
    stages = pieces[0].stages()
    big_sums = [None] * 4
    if dense:
        mix_steps = (
            [lambda t, k=k: mix.go_second(k, t) for k in range(1, links.n_z)]
            + [lambda t, k=k: mix.go_first(k, t) for k in range(1, links.n_z)]
            + [lambda t, k=k: mix.go_z(k, t) for k in range(links.n_z)]
        )
    else:
        mix_steps = []
    last = [None] * stages
    ties = []
    for step in range(stages + 4):
        moved = []
        for p in range(4):
            stage = step - p
            if 0 <= stage < stages:
                moved.append(pieces[p].go(stage, ties))
            elif stage == stages:
                whole = pieces[p].value
                moved.append(links.flip_x(after(whole, ties)))
                big_sums[p] = (whole, moved[-1])
        for _ in range(2):
            if mix_steps:
                moved.append(mix_steps.pop(0)(ties))
        ties = moved
    big_sums = [
        in_order(whole, got, axis).astype(jnp.float32)
        for (whole, got), axis in zip(big_sums, (0, 1, 1, 1))
    ]
    output_weight_grad, query_weight_grad, key_weight_grad, value_weight_grad = big_sums
    if dense:
        while mix_steps:
            mix_steps.pop(0)([])
        mixture = mix.home()
    output = (middle + mixture).astype(jnp.bfloat16)
    attention_gain_grad = jnp.sum(grad_attention_in * normed_one, axis=0)
    tokens_grad = grad_middle + norm_backward(
        grad_attention_in * attention_gain, normed_one, scale_one
    )
    if dense:
        early = jnp.concatenate([mixture_gain_grad, router_grad.reshape(-1)])
        early = links.sum_tp(links.sum_exp(early))
        late = jnp.concatenate([query_norm_grad, key_norm_grad, attention_gain_grad])
        late = links.sum_exp(late)
        norm_sums = (late[:local_width], late[local_width : 2 * local_width])
        gain_sum = links.sum_tp(late[2 * local_width :])
        shared_sums = (
            gain_sum,
            early[:model_width],
            early[model_width:].reshape(model_width, experts_all),
        )
    else:
        norm_sums = [
            lax.psum(value.astype(jnp.bfloat16), "exp").astype(jnp.float32)
            for value in (query_norm_grad, key_norm_grad)
        ]
        shared_sums = lax.psum((attention_gain_grad, mixture_gain_grad, router_grad), AXES)
    return (
        output,
        tokens_grad,
        shared_sums[0],
        query_weight_grad,
        key_weight_grad,
        value_weight_grad,
        output_weight_grad,
        norm_sums[0],
        norm_sums[1],
        shared_sums[1],
        shared_sums[2],
        gate_grad,
        up_grad,
        down_grad,
    )


def solution(mesh):
    return jax.shard_map(
        functools.partial(body, (mesh.shape["exp"], mesh.shape["tp"])),
        mesh=mesh,
        in_specs=(
            P(("exp", "tp"), None),
            P(("exp", "tp"), None),
            P(),
            P(None, "tp"),
            P(None, "tp"),
            P(None, "tp"),
            P("tp", None),
            P("tp"),
            P("tp"),
            P(),
            P(),
            P("exp", None, "tp"),
            P("exp", None, "tp"),
            P("exp", "tp", None),
            P(("exp", "tp"), None),
            P("exp", None),
        ),
        out_specs=(
            P(("exp", "tp"), None),
            P(("exp", "tp"), None),
            P(),
            P(None, "tp"),
            P(None, "tp"),
            P(None, "tp"),
            P("tp", None),
            P("tp"),
            P("tp"),
            P(),
            P(),
            P("exp", None, "tp"),
            P("exp", None, "tp"),
            P("exp", "tp", None),
        ),
        check_vma=False,
    )
```

time: 1270 us -> 823 us (0.65)
  waiting for transfers between devices: 682 us -> 309 us
  blocking collectives: 236 us -> 0 us
  Pallas kernels: 0 us -> 166 us
  starting transfers between devices: 12.2 us -> 117 us
  matrix products: 157 us -> 60.5 us
  other arithmetic: 58.7 us -> 116 us
  local copies, waits for them, and re-layouts: 97.1 us -> 42.2 us
    psum x2 -> x0, waiting for transfers between devices: 315 us -> none  [the longest x1 200 us: body(): lax.psum(query_weight_grad.astype(jnp.bfloat16), 'exp').astype(jnp.float32)]
    ppermute x0 -> x130, waiting for transfers between devices: none -> 309 us  [send(): return lax.ppermute(value, AXES, pairs)]
    reduce_scatter x4 -> x0, waiting for transfers between devices: 198 us -> none  [the longest x1 102 us: body(): lax.psum_scatter(grad_in_part.astype(jnp.bfloat16), 'tp', scatter_dimensi...]
    all_to_all x2 -> x0, blocking collectives: 172 us -> none  [the longest x1 87.5 us: body(): lax.all_to_all(outgoing, 'exp', split_axis=0, concat_axis=1, tiled=True)]
    pallas_call x0 -> x11, Pallas kernels: none -> 166 us  [the longest x8 135 us: run_experts(): pl.pallas_call(functools.partial(expert_kernel, len(carried), tile, place...]
    dot_general x19 -> x2, matrix products: 131 us -> 2.63 us  [the longest x1 2.49 us: body(): jnp.dot(after(attended, held), output_weight, preferred_element_type=jnp....]
    ppermute x0 -> x130, starting transfers between devices: none -> 117 us  [send(): return lax.ppermute(value, AXES, pairs)]
    all_gather x4 -> x0, waiting for transfers between devices: 110 us -> none  [the longest x1 68.7 us: body(): grad_expert = lax.all_gather(grad_arrived, 'tp', axis=1, tiled=True)]
  transfers between devices with their start and end apart: 12 -> 130, of which waited for: 9 -> 50; matrix products, arithmetic and copies ran while one was open for 15% -> 25% of each run, Pallas kernels for 0% -> 18%
where the time goes in v1:
time: 823 us; the launch traced here: 813 us
  waiting for transfers between devices  309 us (38%)
  Pallas kernels  166 us (20%)
  starting transfers between devices  117 us (14%)
  other arithmetic  116 us (14%)
  matrix products  60.5 us (7%)
  local copies, waits for them, and re-layouts  42.2 us (5%)
    ppermute x130, waiting for transfers between devices, send(): return lax.ppermute(value, AXES, pairs)  309 us
    pallas_call x8, Pallas kernels, run_experts(): pl.pallas_call(functools.partial(expert_kernel, len(carried), tile, place...  135 us
    ppermute x130, starting transfers between devices, send(): return lax.ppermute(value, AXES, pairs)  117 us
    dot_general x13, matrix products, contract_rows(): lax.dot_general(first_arg, second_arg, (((0,), (0,)), ((), ())), preferre...  50.2 us
    pallas_call x2, Pallas kernels, attend_back(): pl.pallas_call(attend_back_kernel, grid_spec=pltpu.PrefetchScalarGridSpec...  17.7 us
  transfers between devices with their start and end apart: 130, of which 50 were waited for; matrix products, arithmetic and copies ran while one was open for 25% of the time, Pallas kernels for 18%

profile of v1, /device:TPU:0, one launch (start us, length us, event | category | flops | bytes accessed | tf_op | source)
XLA Modules:
  0.0 813.2 jit_solution(2372626167032606687)
XLA Ops:
  3.1 3.0 collective-permute-start.1
  10.2 8.7 %collective-permute-done.1 = bf16[128,2048]{1,0:T(8,128)(2,1)S(1)} collective-permute-done((bf16[128,2048]{1,0:T(8,128)(2,1)S(1)}, bf16[128,2048]{1,0:T(8,128)(2,1)S(1)}, u32[]{:S(2)}, u32[]{:S(2)}) %collective-permute-start.1) | collective-permute-done | bytes 524320 | tf_op jit(solution)/shard_map/ppermute | solution.py:271
  29.8 3.6 collective-permute-start.7
  33.4 4.3 collective-permute-done.5.grad_far_ref
  39.7 12.7 %attend.1 = (f32[512,512]{1,0:T(8,128)}, f32[512,512]{1,0:T(8,128)}, bf16[512,512]{1,0:T(8,128)(2,1)}, bf16[512,512]{1,0:T(8,128)(2,1)}, bf16[512,512]{1,0:T(8,1...) custom-call(bf16[512,2048]{1,0:T(8,128)(2,1)} %pad_maximum_fusion.2.rows_ref, bf16[2048,512]{1,0:T(8,128)(2,1)} %query_weight.1, ...), custom_call_target="tpu_custom_call" | custom-call | flops 4026531840 | bytes 8388608 | tf_op jit(solution)/shard_map/attend/pallas_call | solution.py:202
  79.1 8.1 collective-permute-done.9
  88.8 16.2 %collective-permute-done.11 = bf16[128,2048]{1,0:T(8,128)(2,1)S(1)} collective-permute-done((bf16[128,2048]{1,0:T(8,128)(2,1)S(1)}, bf16[128,2048]{1,0:T(8,128)(2,1)S(1)}, u32[]{:S(2)}, u32[]{:S(2)}) %collective-permute-start.11) | collective-permute-done | bytes 524320 | tf_op jit(solution)/shard_map/ppermute | solution.py:271
  110.9 4.7 collective-permute-done.12
  121.2 5.4 collective-permute-done.25
  131.5 3.6 collective-permute-done.34
  136.3 5.4 collective-permute-done.13.far_ref
  141.7 4.5 collective-permute-done.26
  148.8 16.7 %experts.8 = (bf16[512,2048]{1,0:T(8,128)(2,1)}, bf16[512,2048]{1,0:T(8,128)(2,1)}, f32[512,2]{1,0:T(8,128)}, bf16[4096,2048]{1,0:T(8,128)(2,1)}, bf16[4096,2048...) custom-call(bf16[256,2048]{1,0:T(8,128)(2,1)} %pad_maximum_fusion.6.nea, ...), custom_call_target="tpu_custom_call" | custom-call | flops 8589934592 | bytes 25165824 | tf_op jit(solution)/shard_map/experts/pallas_call | solution.py:550
  169.1 16.9 %experts.9 = (bf16[512,2048]{1,0:T(8,128)(2,1)}, bf16[512,2048]{1,0:T(8,128)(2,1)}, f32[512,2]{1,0:T(8,128)}, bf16[4096,2048]{1,0:T(8,128)(2,1)}, bf16[4096,2048...) custom-call(bf16[256,2048]{1,0:T(8,128)(2,1)} %collective-permute-do, ...), custom_call_target="tpu_custom_call", output_to_operand_aliasing={{3}: (9, {}), {4}: (10, {}), {5}: (11, {}), {6}: (12, {}), ... | custom-call | flops 8589934592 | bytes 25165824 | tf_op jit(solution)/shard_map/experts/pallas_call | solution.py:550
  199.3 10.2 %collective-permute-done.30 = bf16[128,2048]{1,0:T(8,128)(2,1)} collective-permute-done((bf16[128,2048]{1,0:T(8,128)(2,1)}, bf16[128,2048]{1,0:T(8,128)(2,1)}, u32[]{:S(2)}, u32[]{:S(2)}) %collective-permute-start.30) | collective-permute-done | bytes 524320 | tf_op jit(solution)/shard_map/ppermute | solution.py:271
  215.2 17.0 %experts.10 = (bf16[512,2048]{1,0:T(8,128)(2,1)}, bf16[512,2048]{1,0:T(8,128)(2,1)}, f32[512,2]{1,0:T(8,128)}, bf16[4096,2048]{1,0:T(8,128)(2,1)}, bf16[4096,204...) custom-call(bf16[256,2048]{1,0:T(8,128)(2,1)} %pad_maximum_fusion.8., ...), custom_call_target="tpu_custom_call", output_to_operand_aliasing={{3}: (9, {}), {4}: (10, {}), {5}: (11, {}), {6}: (12, {}), ... | custom-call | flops 8589934592 | bytes 25165824 | tf_op jit(solution)/shard_map/experts/pallas_call | solution.py:550
  232.8 2.9 add_convert_fusion.6
  237.9 17.2 %experts.11 = (bf16[512,2048]{1,0:T(8,128)(2,1)}, bf16[512,2048]{1,0:T(8,128)(2,1)}, f32[512,2]{1,0:T(8,128)}, bf16[4096,2048]{1,0:T(8,128)(2,1)}, bf16[4096,204...) custom-call(bf16[256,2048]{1,0:T(8,128)(2,1)} %collective-permute-do, ...), custom_call_target="tpu_custom_call", output_to_operand_aliasing={{3}: (9, {}), {4}: (10, {}), {5}: (11, {}), {6}: (12, {}), ... | custom-call | flops 8589934592 | bytes 25165824 | tf_op jit(solution)/shard_map/experts/pallas_call | solution.py:550
  256.9 5.2 collective-permute-done.53
  266.1 16.9 %experts.12 = (bf16[512,2048]{1,0:T(8,128)(2,1)}, bf16[512,2048]{1,0:T(8,128)(2,1)}, f32[512,2]{1,0:T(8,128)}, bf16[4096,2048]{1,0:T(8,128)(2,1)}, bf16[4096,204...) custom-call(bf16[256,2048]{1,0:T(8,128)(2,1)} %pad_maximum_fusion.11, ...), custom_call_target="tpu_custom_call", output_to_operand_aliasing={{3}: (9, {}), {4}: (10, {}), {5}: (11, {}), {6}: (12, {}), ... | custom-call | flops 8589934592 | bytes 25165824 | tf_op jit(solution)/shard_map/experts/pallas_call | solution.py:550
  284.8 2.9 add_convert_fusion.7
  288.4 16.8 %experts.13 = (bf16[512,2048]{1,0:T(8,128)(2,1)}, bf16[512,2048]{1,0:T(8,128)(2,1)}, f32[512,2]{1,0:T(8,128)}, bf16[4096,2048]{1,0:T(8,128)(2,1)}, bf16[4096,204...) custom-call(bf16[256,2048]{1,0:T(8,128)(2,1)} %collective-permute-do, ...), custom_call_target="tpu_custom_call", output_to_operand_aliasing={{3}: (9, {}), {4}: (10, {}), {5}: (11, {}), {6}: (12, {}), ... | custom-call | flops 8589934592 | bytes 25165824 | tf_op jit(solution)/shard_map/experts/pallas_call | solution.py:550
  311.6 17.1 %experts.14 = (bf16[512,2048]{1,0:T(8,128)(2,1)}, bf16[512,2048]{1,0:T(8,128)(2,1)}, f32[512,2]{1,0:T(8,128)}, bf16[4096,2048]{1,0:T(8,128)(2,1)}, bf16[4096,204...) custom-call(bf16[256,2048]{1,0:T(8,128)(2,1)} %pad_maximum_fusion.9., ...), custom_call_target="tpu_custom_call", output_to_operand_aliasing={{3}: (9, {}), {4}: (10, {}), {5}: (11, {}), {6}: (12, {}), ... | custom-call | flops 8589934592 | bytes 25165824 | tf_op jit(solution)/shard_map/experts/pallas_call | solution.py:550
  329.9 17.0 %experts.15 = (bf16[512,2048]{1,0:T(8,128)(2,1)}, bf16[512,2048]{1,0:T(8,128)(2,1)}, f32[512,2]{1,0:T(8,128)}, bf16[4096,2048]{1,0:T(8,128)(2,1)}, bf16[4096,204...) custom-call(bf16[256,2048]{1,0:T(8,128)(2,1)} %collective-permute-do, ...), custom_call_target="tpu_custom_call", output_to_operand_aliasing={{3}: (9, {}), {4}: (10, {}), {5}: (11, {}), {6}: (12, {}), ... | custom-call | flops 8589934592 | bytes 25165824 | tf_op jit(solution)/shard_map/experts/pallas_call | solution.py:550
  353.2 12.4 %collective-permute-done.73 = f32[2,4,16,128]{3,2,1,0:T(8,128)S(1)} collective-permute-done((f32[2,4,16,128]{3,2,1,0:T(8,128)S(1)}, f32[2,4,16,128]{3,2,1,0:T(8,128)S(1)}, u32[]{:S(2)}, u32[]{:S(2)}) %collective-permute-start.73) | collective-permute-done | bytes 65568 | tf_op jit(solution)/shard_map/ppermute | solution.py:271
  366.3 3.3 collective-permute-done.74
  384.2 2.8 add_convert_fusion.18
  387.0 3.8 collective-permute-start.62
  394.2 10.3 %convolution_bitcast_fusion.3 = f32[1,2048,256]{2,1,0:T(8,128)} fusion(bf16[4096,2048]{1,0:T(8,128)(2,1)} %get-tuple-element.318, bf16[2,4096,256]{2,1,0:T(8,128)(2,1)S(1)} %copy-done.1), kind=kOutput, calls=%fused_computation.8 | convolution fusion | flops 4294967296 | bytes 20971520 | tf_op jit(solution)/shard_map/dot_general | solution.py:30
  404.5 3.8 collective-permute-done.60
  410.5 6.6 convolution_bitcast_fusion.2
  417.1 4.7 pad_maximum_fusion
  424.7 6.6 convolution_bitcast_fusion.1
  433.1 6.8 convolution_bitcast_fusion
  439.9 4.0 pad_maximum_fusion.1
  452.6 7.0 collective-permute-done.66
  465.9 8.5 %collective-permute-done.67 = bf16[256,2048]{1,0:T(8,128)(2,1)S(1)} collective-permute-done((bf16[256,2048]{1,0:T(8,128)(2,1)S(1)}, bf16[256,2048]{1,0:T(8,128)(2,1)S(1)}, u32[]{:S(2)}, u32[]{:S(2)}) %collective-permute-start.67) | collective-permute-done | bytes 1048608 | tf_op jit(solution)/shard_map/ppermute | solution.py:271
  478.9 3.2 collective-permute-done.125
  482.8 14.1 %collective-permute-done.79 = bf16[128,2048]{1,0:T(8,128)(2,1)S(1)} collective-permute-done((bf16[128,2048]{1,0:T(8,128)(2,1)}, bf16[128,2048]{1,0:T(8,128)(2,1)S(1)}, u32[]{:S(2)}, u32[]{:S(2)}) %collective-permute-start.79) | collective-permute-done | bytes 524320 | tf_op jit(solution)/shard_map/ppermute | solution.py:271
  499.0 3.0 collective-permute-start.127
  505.9 3.1 collective-permute-done.127
  509.2 3.0 pad_maximum_fusion.3.row_grad_ref
  516.1 8.9 %attend_back.2 = (bf16[512,256]{1,0:T(8,128)(2,1)}, bf16[512,256]{1,0:T(8,128)(2,1)}, bf16[512,256]{1,0:T(8,128)(2,1)}, f32[1,256]{1,0:T(1,128)}, f32[1,256]{1,0:T(1,128)}) custom-call(s32[1]{0:T(128)} %bitcast.72.which_ref, bf16[512,2048]{1,0:T(8,128)(2,1)} %pad_maximum_fusion.3.row_grad_ref, bf16[512,2048]{1,0:T(8,128)(2,1)} %output_weight.3, ...), custom_call_target="tpu_custom_call" | custom-call | flops 1207959552 | bytes 5242880 | tf_op jit(solution)/shard_map/attend_back/pallas_call | solution.py:231
  533.6 8.7 %attend_back.3 = (bf16[512,256]{1,0:T(8,128)(2,1)}, bf16[512,256]{1,0:T(8,128)(2,1)}, bf16[512,256]{1,0:T(8,128)(2,1)}, f32[1,256]{1,0:T(1,128)}, f32[1,256]{1,0:T(1,128)}) custom-call(s32[1]{0:T(128)} %bitcast.71.which_ref, bf16[512,2048]{1,0:T(8,128)(2,1)} %pad_maximum_fusion.3.row_grad_ref, bf16[512,2048]{1,0:T(8,128)(2,1)} %output_weight.3, ...), custom_call_target="tpu_custom_call" | custom-call | flops 1207959552 | bytes 5242880 | tf_op jit(solution)/shard_map/attend_back/pallas_call | solution.py:231
  543.6 3.2 fusion.35
  553.2 8.3 %collective-permute-done.93 = bf16[512,768]{1,0:T(8,128)(2,1)S(1)} collective-permute-done((bf16[512,768]{1,0:T(8,128)(2,1)}, bf16[512,768]{1,0:T(8,128)(2,1)S(1)}, u32[]{:S(2)}, u32[]{:S(2)}) %collective-permute-start.93) | collective-permute-done | bytes 786464 | tf_op jit(solution)/shard_map/ppermute | solution.py:271
  572.1 11.8 %collective-permute-done.89 = bf16[128,2048]{1,0:T(8,128)(2,1)S(1)} collective-permute-done((bf16[128,2048]{1,0:T(8,128)(2,1)S(1)}, bf16[128,2048]{1,0:T(8,128)(2,1)S(1)}, u32[]{:S(2)}, u32[]{:S(2)}) %collective-permute-start.89) | collective-permute-done | bytes 524320 | tf_op jit(solution)/shard_map/ppermute | solution.py:271
  589.3 7.3 collective-permute-done.92
  598.4 5.0 collective-permute-done.94
  607.4 3.3 collective-permute-start.98
  610.7 2.9 collective-permute-start.96
  613.6 5.0 collective-permute-done.109
  624.9 6.8 collective-permute-done.96
  642.0 31.7 %collective-permute-done.103 = bf16[512,256]{1,0:T(8,128)(2,1)S(1)} collective-permute-done((bf16[512,256]{1,0:T(8,128)(2,1)S(1)}, bf16[512,256]{1,0:T(8,128)(2,1)S(1)}, u32[]{:S(2)}, u32[]{:S(2)}) %collective-permute-start.103) | collective-permute-done | bytes 262176 | tf_op jit(solution)/shard_map/ppermute | solution.py:271
  686.1 19.2 %collective-permute-done.117 = bf16[512,256]{1,0:T(8,128)(2,1)S(1)} collective-permute-done((bf16[512,256]{1,0:T(8,128)(2,1)S(1)}, bf16[512,256]{1,0:T(8,128)(2,1)S(1)}, u32[]{:S(2)}, u32[]{:S(2)}) %collective-permute-start.117) | collective-permute-done | bytes 262176 | tf_op jit(solution)/shard_map/ppermute | solution.py:271
  708.0 8.2 %collective-permute-done.106 = bf16[128,2048]{1,0:T(8,128)(2,1)S(1)} collective-permute-done((bf16[128,2048]{1,0:T(8,128)(2,1)S(1)}, bf16[128,2048]{1,0:T(8,128)(2,1)S(1)}, u32[]{:S(2)}, u32[]{:S(2)}) %collective-permute-start.106) | collective-permute-done | bytes 524320 | tf_op jit(solution)/shard_map/ppermute | solution.py:271
  716.1 16.3 %collective-permute-done.107 = bf16[128,2048]{1,0:T(8,128)(2,1)S(1)} collective-permute-done((bf16[128,2048]{1,0:T(8,128)(2,1)S(1)}, bf16[128,2048]{1,0:T(8,128)(2,1)S(1)}, u32[]{:S(2)}, u32[]{:S(2)}) %collective-permute-start.107) | collective-permute-done | bytes 524320 | tf_op jit(solution)/shard_map/ppermute | solution.py:271
  737.5 10.6 %fusion.82 = f32[512,2048]{1,0:T(8,128)} fusion(bf16[4096,512]{1,0:T(8,128)(2,1)S(1)} %copy-done, bf16[4096,2048]{1,0:T(8,128)(2,1)S(1)} %bitcast.202), kind=kOutput, calls=%fused_computation.257 | convolution fusion | flops 8589934592 | bytes 25165824 | tf_op jit(solution)/shard_map/dot_general | solution.py:30
  754.0 3.7 collective-permute-done.112
  768.2 6.6 collective-permute-done.123
  775.1 11.0 %collective-permute-done.122 = bf16[2048,256]{1,0:T(8,128)(2,1)S(1)} collective-permute-done((bf16[2048,256]{1,0:T(8,128)(2,1)S(1)}, bf16[2048,256]{1,0:T(8,128)(2,1)S(1)}, u32[]{:S(2)}, u32[]{:S(2)}) %collective-permute-start.122) | collective-permute-done | bytes 1048608 | tf_op jit(solution)/shard_map/ppermute | solution.py:271
  787.9 2.9 fusion.3
  790.8 4.9 fusion
  798.4 11.8 %collective-permute-done.124 = bf16[2048,256]{1,0:T(8,128)(2,1)S(1)} collective-permute-done((bf16[2048,256]{1,0:T(8,128)(2,1)S(1)}, bf16[2048,256]{1,0:T(8,128)(2,1)S(1)}, u32[]{:S(2)}, u32[]{:S(2)}) %collective-permute-start.124) | collective-permute-done | bytes 1048608 | tf_op jit(solution)/shard_map/ppermute | solution.py:271
  (624 shorter events, 268.4 us)
Async XLA Ops:
  7.7 22.1 %collective-permute-start.4 = (bf16[128,2048]{1,0:T(8,128)(2,1)}, bf16[128,2048]{1,0:T(8,128)(2,1)}, u32[]{:S(2)}, u32[]{:S(2)}) collective-permute-start(bf16[128,2048]{1,0:T(8,128)(2,1)} %param.17), channel_id=1, source_target_pairs={{0,8},{1,9},{2,10},{3,11},{4,12},{5,13},{6,14},{7,15},{8,16},{9,17... | collective-permute-start | bytes 1572872 | tf_op jit(solution)/shard_map/ppermute | solution.py:271
  29.8 25.5 %collective-permute-start.7 = (bf16[128,2048]{1,0:T(8,128)(2,1)S(1)}, bf16[128,2048]{1,0:T(8,128)(2,1)S(1)}, u32[]{:S(2)}, u32[]{:S(2)}) collective-permute-start(bf16[128,2048]{1,0:T(8,128)(2,1)S(1)} %copy-done.23), channel_id=1, source_target_pairs={{0,24},{1,25},{2,26},{3,27},{4,28},{5,29},{6,30},{7,31},{8,0},{9,1... | collective-permute-start | bytes 1572872 | tf_op jit(solution)/shard_map/ppermute | solution.py:271
  60.7 44.2 %collective-permute-start.10 = (bf16[256,2048]{1,0:T(8,128)(2,1)}, bf16[256,2048]{1,0:T(8,128)(2,1)}, u32[]{:S(2)}, u32[]{:S(2)}) collective-permute-start(bf16[256,2048]{1,0:T(8,128)(2,1)} %constant_dynamic-update-slice_fusion.grad_near_ref), channel_id=1, source_target_pairs={{0,2},{1,5},{2,0},{3,7},{4,6},{5,1},{6,4},{7,3},{8,10},{9,13},{10,... | collective-permute-start | bytes 3145736 | tf_op jit(solution)/shard_map/ppermute | solution.py:271
  64.2 23.0 %collective-permute-start.9 = (bf16[128,2048]{1,0:T(8,128)(2,1)}, bf16[128,2048]{1,0:T(8,128)(2,1)}, u32[]{:S(2)}, u32[]{:S(2)}) collective-permute-start(bf16[128,2048]{1,0:T(8,128)(2,1)} %fusion.27), channel_id=1, source_target_pairs={{0,2},{1,3},{2,0},{3,1},{4,6},{5,7},{6,4},{7,5},{8,10},{9,11},{10,... | collective-permute-start | bytes 1572872 | tf_op jit(solution)/shard_map/ppermute | solution.py:271
  76.6 32.5 %collective-permute-start.18 = (bf16[2,4,16,128]{3,2,1,0:T(8,128)(2,1)S(1)}, bf16[2,4,16,128]{3,2,1,0:T(8,128)(2,1)S(1)}, u32[]{:S(2)}, u32[]{:S(2)}) collective-permute-start(bf16[2,4,16,128]{3,2,1,0:T(8,128)(2,1)S(1)} %pad_maximum_fusion.19), channel_id=1, source_target_pairs={{0,2},{1,5},{2,0},{3,7},{4,6},{5,1},{6,4},{7,3},{8,10},{9,13},{10,... | collective-permute-start | bytes 98312 | tf_op jit(solution)/shard_map/ppermute | solution.py:271
  78.2 26.8 %collective-permute-start.11 = (bf16[128,2048]{1,0:T(8,128)(2,1)S(1)}, bf16[128,2048]{1,0:T(8,128)(2,1)S(1)}, u32[]{:S(2)}, u32[]{:S(2)}) collective-permute-start(bf16[128,2048]{1,0:T(8,128)(2,1)S(1)} %copy-done.23), channel_id=1, source_target_pairs={{0,16},{1,17},{2,18},{3,19},{4,20},{5,21},{6,22},{7,23},{8,24},{9,... | collective-permute-start | bytes 1572872 | tf_op jit(solution)/shard_map/ppermute | solution.py:271
  116.7 25.0 %collective-permute-start.13 = (bf16[256,2048]{1,0:T(8,128)(2,1)}, bf16[256,2048]{1,0:T(8,128)(2,1)}, u32[]{:S(2)}, u32[]{:S(2)}) collective-permute-start(bf16[256,2048]{1,0:T(8,128)(2,1)} %pad_maximum_fusion.6.near_ref), channel_id=1, source_target_pairs={{0,2},{1,5},{2,0},{3,7},{4,6},{5,1},{6,4},{7,3},{8,10},{9,13},{10,... | collective-permute-start | bytes 3145736 | tf_op jit(solution)/shard_map/ppermute | solution.py:271
  130.2 35.3 %collective-permute-start.28 = (bf16[256,2048]{1,0:T(8,128)(2,1)S(1)}, bf16[256,2048]{1,0:T(8,128)(2,1)}, u32[]{:S(2)}, u32[]{:S(2)}) collective-permute-start(bf16[256,2048]{1,0:T(8,128)(2,1)S(1)} %pad_maximum_fusion.7.grad_near_ref), channel_id=1, source_target_pairs={{0,2},{1,5},{2,0},{3,7},{4,6},{5,1},{6,4},{7,3},{8,10},{9,13},{10,... | collective-permute-start | bytes 3145736 | tf_op jit(solution)/shard_map/ppermute | solution.py:271
  135.0 34.1 %collective-permute-start.22 = (bf16[256,2048]{1,0:T(8,128)(2,1)}, bf16[256,2048]{1,0:T(8,128)(2,1)}, u32[]{:S(2)}, u32[]{:S(2)}) collective-permute-start(bf16[256,2048]{1,0:T(8,128)(2,1)} %copy-done.34), channel_id=1, source_target_pairs={{0,1},{1,0},{2,3},{3,2},{4,5},{5,4},{6,7},{7,6},{8,9},{9,8},{10,11... | collective-permute-start | bytes 3145736 | tf_op jit(solution)/shard_map/ppermute | solution.py:271
  141.7 27.4 %collective-permute-start.23 = (bf16[256,2048]{1,0:T(8,128)(2,1)}, bf16[256,2048]{1,0:T(8,128)(2,1)}, u32[]{:S(2)}, u32[]{:S(2)}) collective-permute-start(bf16[256,2048]{1,0:T(8,128)(2,1)} %collective-permute-done.5.grad_far_ref), channel_id=1, source_target_pairs={{0,1},{1,0},{2,3},{3,2},{4,5},{5,4},{6,7},{7,6},{8,9},{9,8},{10,11... | collective-permute-start | bytes 3145736 | tf_op jit(solution)/shard_map/ppermute | solution.py:271
  165.5 32.7 %collective-permute-start.35 = (bf16[256,2048]{1,0:T(8,128)(2,1)S(1)}, bf16[256,2048]{1,0:T(8,128)(2,1)}, u32[]{:S(2)}, u32[]{:S(2)}) collective-permute-start(bf16[256,2048]{1,0:T(8,128)(2,1)S(1)} %pad_maximum_fusion.10.grad_near_ref), channel_id=1, source_target_pairs={{0,2},{1,5},{2,0},{3,7},{4,6},{5,1},{6,4},{7,3},{8,10},{9,13},{10,... | collective-permute-start | bytes 3145736 | tf_op jit(solution)/shard_map/ppermute | solution.py:271
  166.2 45.6 %collective-permute-start.38 = (bf16[256,2048]{1,0:T(8,128)(2,1)}, bf16[256,2048]{1,0:T(8,128)(2,1)}, u32[]{:S(2)}, u32[]{:S(2)}) collective-permute-start(bf16[256,2048]{1,0:T(8,128)(2,1)} %pad_maximum_fusion.8.near_ref), channel_id=1, source_target_pairs={{0,2},{1,5},{2,0},{3,7},{4,6},{5,1},{6,4},{7,3},{8,10},{9,13},{10,... | collective-permute-start | bytes 3145736 | tf_op jit(solution)/shard_map/ppermute | solution.py:271
  169.1 25.2 %collective-permute-start.29 = (bf16[128,2048]{1,0:T(8,128)(2,1)S(1)}, bf16[128,2048]{1,0:T(8,128)(2,1)}, u32[]{:S(2)}, u32[]{:S(2)}) collective-permute-start(bf16[128,2048]{1,0:T(8,128)(2,1)S(1)} %multiply_convert_fusion), channel_id=1, source_target_pairs={{0,16},{1,17},{2,18},{3,19},{4,20},{5,21},{6,22},{7,23},{8,24},{9,... | collective-permute-start | bytes 1572872 | tf_op jit(solution)/shard_map/ppermute | solution.py:271
  186.0 46.2 %collective-permute-start.44 = (bf16[512,2048]{1,0:T(8,128)(2,1)}, bf16[512,2048]{1,0:T(8,128)(2,1)}, u32[]{:S(2)}, u32[]{:S(2)}) collective-permute-start(bf16[512,2048]{1,0:T(8,128)(2,1)} %get-tuple-element.208), channel_id=1, source_target_pairs={{0,1},{1,0},{2,3},{3,2},{4,5},{5,4},{6,7},{7,6},{8,9},{9,8},{10,11... | collective-permute-start | bytes 6291464 | tf_op jit(solution)/shard_map/ppermute | solution.py:271
  188.5 25.7 %collective-permute-start.48 = (bf16[256,2048]{1,0:T(8,128)(2,1)}, bf16[256,2048]{1,0:T(8,128)(2,1)}, u32[]{:S(2)}, u32[]{:S(2)}) collective-permute-start(bf16[256,2048]{1,0:T(8,128)(2,1)} %pad_maximum_fusion.11.near_ref), channel_id=1, source_target_pairs={{0,2},{1,5},{2,0},{3,7},{4,6},{5,1},{6,4},{7,3},{8,10},{9,13},{10,... | collective-permute-start | bytes 3145736 | tf_op jit(solution)/shard_map/ppermute | solution.py:271
  198.2 38.8 %collective-permute-start.41 = (bf16[256,2048]{1,0:T(8,128)(2,1)}, bf16[256,2048]{1,0:T(8,128)(2,1)}, u32[]{:S(2)}, u32[]{:S(2)}) collective-permute-start(bf16[256,2048]{1,0:T(8,128)(2,1)} %constant_dynamic-update-slice_fusion.grad_near_ref), channel_id=1, source_target_pairs={{0,1},{1,0},{2,3},{3,2},{4,5},{5,4},{6,7},{7,6},{8,9},{9,8},{10,11... | collective-permute-start | bytes 3145736 | tf_op jit(solution)/shard_map/ppermute | solution.py:271
  209.5 28.4 %collective-permute-start.42 = (bf16[256,2048]{1,0:T(8,128)(2,1)}, bf16[256,2048]{1,0:T(8,128)(2,1)}, u32[]{:S(2)}, u32[]{:S(2)}) collective-permute-start(bf16[256,2048]{1,0:T(8,128)(2,1)} %collective-permute-done.10.grad_far_ref), channel_id=1, source_target_pairs={{0,1},{1,0},{2,3},{3,2},{4,5},{5,4},{6,7},{7,6},{8,9},{9,8},{10,11... | collective-permute-start | bytes 3145736 | tf_op jit(solution)/shard_map/ppermute | solution.py:271
  211.8 23.9 %collective-permute-start.39 = (bf16[256,2048]{1,0:T(8,128)(2,1)}, bf16[256,2048]{1,0:T(8,128)(2,1)}, u32[]{:S(2)}, u32[]{:S(2)}) collective-permute-start(bf16[256,2048]{1,0:T(8,128)(2,1)} %pad_maximum_fusion.8.near_ref), channel_id=1, source_target_pairs={{0,1},{1,0},{2,3},{3,2},{4,5},{5,4},{6,7},{7,6},{8,9},{9,8},{10,11... | collective-permute-start | bytes 3145736 | tf_op jit(solution)/shard_map/ppermute | solution.py:271
  214.2 22.2 %collective-permute-start.40 = (bf16[256,2048]{1,0:T(8,128)(2,1)}, bf16[256,2048]{1,0:T(8,128)(2,1)}, u32[]{:S(2)}, u32[]{:S(2)}) collective-permute-start(bf16[256,2048]{1,0:T(8,128)(2,1)} %collective-permute-done.38.far_ref), channel_id=1, source_target_pairs={{0,1},{1,0},{2,3},{3,2},{4,5},{5,4},{6,7},{7,6},{8,9},{9,8},{10,11... | collective-permute-start | bytes 3145736 | tf_op jit(solution)/shard_map/ppermute | solution.py:271
  232.2 55.5 %collective-permute-start.51 = (bf16[256,2048]{1,0:T(8,128)(2,1)S(1)}, bf16[256,2048]{1,0:T(8,128)(2,1)}, u32[]{:S(2)}, u32[]{:S(2)}) collective-permute-start(bf16[256,2048]{1,0:T(8,128)(2,1)S(1)} %pad_maximum_fusion.7.grad_near_ref), channel_id=1, source_target_pairs={{0,1},{1,0},{2,3},{3,2},{4,5},{5,4},{6,7},{7,6},{8,9},{9,8},{10,11... | collective-permute-start | bytes 3145736 | tf_op jit(solution)/shard_map/ppermute | solution.py:271
  236.4 28.2 %collective-permute-start.49 = (bf16[256,2048]{1,0:T(8,128)(2,1)}, bf16[256,2048]{1,0:T(8,128)(2,1)}, u32[]{:S(2)}, u32[]{:S(2)}) collective-permute-start(bf16[256,2048]{1,0:T(8,128)(2,1)} %pad_maximum_fusion.11.near_ref), channel_id=1, source_target_pairs={{0,1},{1,0},{2,3},{3,2},{4,5},{5,4},{6,7},{7,6},{8,9},{9,8},{10,11... | collective-permute-start | bytes 3145736 | tf_op jit(solution)/shard_map/ppermute | solution.py:271
  237.0 25.1 %collective-permute-start.53 = (bf16[256,2048]{1,0:T(8,128)(2,1)}, bf16[256,2048]{1,0:T(8,128)(2,1)}, u32[]{:S(2)}, u32[]{:S(2)}) collective-permute-start(bf16[256,2048]{1,0:T(8,128)(2,1)} %add_convert_fusion.6), channel_id=1, source_target_pairs={{0,2},{1,5},{2,0},{3,7},{4,6},{5,1},{6,4},{7,3},{8,10},{9,13},{10,... | collective-permute-start | bytes 3145736 | tf_op jit(solution)/shard_map/ppermute | solution.py:271
  255.1 29.6 %collective-permute-start.45 = (bf16[512,2048]{1,0:T(8,128)(2,1)}, bf16[512,2048]{1,0:T(8,128)(2,1)}, u32[]{:S(2)}, u32[]{:S(2)}) collective-permute-start(bf16[512,2048]{1,0:T(8,128)(2,1)} %get-tuple-element.215), channel_id=1, source_target_pairs={{0,1},{1,0},{2,3},{3,2},{4,5},{5,4},{6,7},{7,6},{8,9},{9,8},{10,11... | collective-permute-start | bytes 6291464 | tf_op jit(solution)/shard_map/ppermute | solution.py:271
  255.5 32.9 %collective-permute-start.52 = (bf16[256,2048]{1,0:T(8,128)(2,1)}, bf16[256,2048]{1,0:T(8,128)(2,1)}, u32[]{:S(2)}, u32[]{:S(2)}) collective-permute-start(bf16[256,2048]{1,0:T(8,128)(2,1)} %collective-permute-done.28.grad_far_ref), channel_id=1, source_target_pairs={{0,1},{1,0},{2,3},{3,2},{4,5},{5,4},{6,7},{7,6},{8,9},{9,8},{10,11... | collective-permute-start | bytes 3145736 | tf_op jit(solution)/shard_map/ppermute | solution.py:271
  262.1 22.0 %collective-permute-start.50 = (bf16[256,2048]{1,0:T(8,128)(2,1)}, bf16[256,2048]{1,0:T(8,128)(2,1)}, u32[]{:S(2)}, u32[]{:S(2)}) collective-permute-start(bf16[256,2048]{1,0:T(8,128)(2,1)} %collective-permute-done.48.far_ref), channel_id=1, source_target_pairs={{0,1},{1,0},{2,3},{3,2},{4,5},{5,4},{6,7},{7,6},{8,9},{9,8},{10,11... | collective-permute-start | bytes 3145736 | tf_op jit(solution)/shard_map/ppermute | solution.py:271
  284.1 45.7 %collective-permute-start.36 = (bf16[256,2048]{1,0:T(8,128)(2,1)S(1)}, bf16[256,2048]{1,0:T(8,128)(2,1)}, u32[]{:S(2)}, u32[]{:S(2)}) collective-permute-start(bf16[256,2048]{1,0:T(8,128)(2,1)S(1)} %pad_maximum_fusion.10.grad_near_ref), channel_id=1, source_target_pairs={{0,1},{1,0},{2,3},{3,2},{4,5},{5,4},{6,7},{7,6},{8,9},{9,8},{10,11... | collective-permute-start | bytes 3145736 | tf_op jit(solution)/shard_map/ppermute | solution.py:271
  284.2 45.6 %collective-permute-start.37 = (bf16[256,2048]{1,0:T(8,128)(2,1)}, bf16[256,2048]{1,0:T(8,128)(2,1)}, u32[]{:S(2)}, u32[]{:S(2)}) collective-permute-start(bf16[256,2048]{1,0:T(8,128)(2,1)} %collective-permute-done.35.grad_far_ref), channel_id=1, source_target_pairs={{0,1},{1,0},{2,3},{3,2},{4,5},{5,4},{6,7},{7,6},{8,9},{9,8},{10,11... | collective-permute-start | bytes 3145736 | tf_op jit(solution)/shard_map/ppermute | solution.py:271
  284.7 25.4 %collective-permute-start.32 = (bf16[256,2048]{1,0:T(8,128)(2,1)}, bf16[256,2048]{1,0:T(8,128)(2,1)}, u32[]{:S(2)}, u32[]{:S(2)}) collective-permute-start(bf16[256,2048]{1,0:T(8,128)(2,1)} %pad_maximum_fusion.9.near_ref), channel_id=1, source_target_pairs={{0,1},{1,0},{2,3},{3,2},{4,5},{5,4},{6,7},{7,6},{8,9},{9,8},{10,11... | collective-permute-start | bytes 3145736 | tf_op jit(solution)/shard_map/ppermute | solution.py:271
  305.2 24.6 %collective-permute-start.55 = (bf16[512,2048]{1,0:T(8,128)(2,1)}, bf16[512,2048]{1,0:T(8,128)(2,1)}, u32[]{:S(2)}, u32[]{:S(2)}) collective-permute-start(bf16[512,2048]{1,0:T(8,128)(2,1)} %get-tuple-element.233), channel_id=1, source_target_pairs={{0,1},{1,0},{2,3},{3,2},{4,5},{5,4},{6,7},{7,6},{8,9},{9,8},{10,11... | collective-permute-start | bytes 6291464 | tf_op jit(solution)/shard_map/ppermute | solution.py:271
  307.1 22.7 %collective-permute-start.33 = (bf16[256,2048]{1,0:T(8,128)(2,1)}, bf16[256,2048]{1,0:T(8,128)(2,1)}, u32[]{:S(2)}, u32[]{:S(2)}) collective-permute-start(bf16[256,2048]{1,0:T(8,128)(2,1)} %collective-permute-done.31.far_ref), channel_id=1, source_target_pairs={{0,1},{1,0},{2,3},{3,2},{4,5},{5,4},{6,7},{7,6},{8,9},{9,8},{10,11... | collective-permute-start | bytes 3145736 | tf_op jit(solution)/shard_map/ppermute | solution.py:271
  350.0 22.1 %collective-permute-start.57 = (bf16[256,2048]{1,0:T(8,128)(2,1)S(1)}, bf16[256,2048]{1,0:T(8,128)(2,1)S(1)}, u32[]{:S(2)}, u32[]{:S(2)}) collective-permute-start(bf16[256,2048]{1,0:T(8,128)(2,1)S(1)} %add_convert_fusion.5), channel_id=1, source_target_pairs={{0,2},{1,5},{2,0},{3,7},{4,6},{5,1},{6,4},{7,3},{8,10},{9,13},{10,... | collective-permute-start | bytes 3145736 | tf_op jit(solution)/shard_map/ppermute | solution.py:271
  366.2 24.6 %collective-permute-start.56 = (bf16[512,2048]{1,0:T(8,128)(2,1)}, bf16[512,2048]{1,0:T(8,128)(2,1)}, u32[]{:S(2)}, u32[]{:S(2)}) collective-permute-start(bf16[512,2048]{1,0:T(8,128)(2,1)} %get-tuple-element.246), channel_id=1, source_target_pairs={{0,1},{1,0},{2,3},{3,2},{4,5},{5,4},{6,7},{7,6},{8,9},{9,8},{10,11... | collective-permute-start | bytes 6291464 | tf_op jit(solution)/shard_map/ppermute | solution.py:271
  378.4 68.2 %collective-permute-start.70 = (bf16[128,2048]{1,0:T(8,128)(2,1)}, bf16[128,2048]{1,0:T(8,128)(2,1)S(1)}, u32[]{:S(2)}, u32[]{:S(2)}) collective-permute-start(bf16[128,2048]{1,0:T(8,128)(2,1)} %add_convert_fusion.15), channel_id=1, source_target_pairs={{0,24},{1,25},{2,26},{3,27},{4,28},{5,29},{6,30},{7,31},{8,0},{9,1... | collective-permute-start | bytes 1572872 | tf_op jit(solution)/shard_map/ppermute | solution.py:271
  387.0 37.1 %collective-permute-start.62 = (bf16[128,2048]{1,0:T(8,128)(2,1)}, bf16[128,2048]{1,0:T(8,128)(2,1)S(1)}, u32[]{:S(2)}, u32[]{:S(2)}) collective-permute-start(bf16[128,2048]{1,0:T(8,128)(2,1)} %add_convert_fusion.18), channel_id=1, source_target_pairs={{0,8},{1,9},{2,10},{3,11},{4,12},{5,13},{6,14},{7,15},{8,16},{9,17... | collective-permute-start | bytes 1572872 | tf_op jit(solution)/shard_map/ppermute | solution.py:271
  390.8 33.3 %collective-permute-start.63 = (bf16[512,2048]{1,0:T(8,128)(2,1)}, bf16[512,2048]{1,0:T(8,128)(2,1)S(1)}, u32[]{:S(2)}, u32[]{:S(2)}) collective-permute-start(bf16[512,2048]{1,0:T(8,128)(2,1)} %get-tuple-element.252), channel_id=1, source_target_pairs={{0,1},{1,0},{2,3},{3,2},{4,5},{5,4},{6,7},{7,6},{8,9},{9,8},{10,11... | collective-permute-start | bytes 6291464 | tf_op jit(solution)/shard_map/ppermute | solution.py:271
  390.8 33.4 %collective-permute-start.59 = (bf16[512,2048]{1,0:T(8,128)(2,1)}, bf16[512,2048]{1,0:T(8,128)(2,1)}, u32[]{:S(2)}, u32[]{:S(2)}) collective-permute-start(bf16[512,2048]{1,0:T(8,128)(2,1)} %get-tuple-element.248), channel_id=1, source_target_pairs={{0,1},{1,0},{2,3},{3,2},{4,5},{5,4},{6,7},{7,6},{8,9},{9,8},{10,11... | collective-permute-start | bytes 6291464 | tf_op jit(solution)/shard_map/ppermute | solution.py:271
  424.1 24.9 %collective-permute-start.71 = (bf16[128,2048]{1,0:T(8,128)(2,1)}, bf16[128,2048]{1,0:T(8,128)(2,1)}, u32[]{:S(2)}, u32[]{:S(2)}) collective-permute-start(bf16[128,2048]{1,0:T(8,128)(2,1)} %add_convert_fusion.14), channel_id=1, source_target_pairs={{0,16},{1,17},{2,18},{3,19},{4,20},{5,21},{6,22},{7,23},{8,24},{9,... | collective-permute-start | bytes 1572872 | tf_op jit(solution)/shard_map/ppermute | solution.py:271
  424.1 21.5 %collective-permute-start.64 = (bf16[512,2048]{1,0:T(8,128)(2,1)}, bf16[512,2048]{1,0:T(8,128)(2,1)}, u32[]{:S(2)}, u32[]{:S(2)}) collective-permute-start(bf16[512,2048]{1,0:T(8,128)(2,1)} %get-tuple-element.253), channel_id=1, source_target_pairs={{0,1},{1,0},{2,3},{3,2},{4,5},{5,4},{6,7},{7,6},{8,9},{9,8},{10,11... | collective-permute-start | bytes 6291464 | tf_op jit(solution)/shard_map/ppermute | solution.py:271
  462.0 40.0 %collective-permute-start.90 = (bf16[256,2048]{1,0:T(8,128)(2,1)S(1)}, bf16[256,2048]{1,0:T(8,128)(2,1)S(1)}, u32[]{:S(2)}, u32[]{:S(2)}) collective-permute-start(bf16[256,2048]{1,0:T(8,128)(2,1)S(1)} %add_convert_fusion.1), channel_id=1, source_target_pairs={{0,2},{1,5},{2,0},{3,7},{4,6},{5,1},{6,4},{7,3},{8,10},{9,13},{10,... | collective-permute-start | bytes 3145736 | tf_op jit(solution)/shard_map/ppermute | solution.py:271
  478.9 30.2 %collective-permute-start.78 = (bf16[128,2048]{1,0:T(8,128)(2,1)}, bf16[128,2048]{1,0:T(8,128)(2,1)S(1)}, u32[]{:S(2)}, u32[]{:S(2)}) collective-permute-start(bf16[128,2048]{1,0:T(8,128)(2,1)} %get-tuple-element.373), channel_id=1, source_target_pairs={{0,1},{1,0},{2,3},{3,2},{4,5},{5,4},{6,7},{7,6},{8,9},{9,8},{10,11... | collective-permute-start | bytes 1572872 | tf_op jit(solution)/shard_map/ppermute | solution.py:271
  504.5 26.7 %collective-permute-start.81 = (bf16[128,2048]{1,0:T(8,128)(2,1)}, bf16[128,2048]{1,0:T(8,128)(2,1)}, u32[]{:S(2)}, u32[]{:S(2)}) collective-permute-start(bf16[128,2048]{1,0:T(8,128)(2,1)} %get-tuple-element.373), channel_id=1, source_target_pairs={{0,4},{1,5},{2,6},{3,7},{4,0},{5,1},{6,2},{7,3},{8,12},{9,13},{10,... | collective-permute-start | bytes 1572872 | tf_op jit(solution)/shard_map/ppermute | solution.py:271
  532.8 34.9 %collective-permute-start.85 = (bf16[512,256]{1,0:T(8,128)(2,1)}, bf16[512,256]{1,0:T(8,128)(2,1)}, u32[]{:S(2)}, u32[]{:S(2)}) collective-permute-start(bf16[512,256]{1,0:T(8,128)(2,1)} %constant_dynamic-slice_fusion), channel_id=1, source_target_pairs={{0,4},{1,5},{2,6},{3,7},{4,0},{5,1},{6,2},{7,3},{8,12},{9,13},{10,... | collective-permute-start | bytes 786440 | tf_op jit(solution)/shard_map/ppermute | solution.py:271
  572.0 24.7 %collective-permute-start.108 = (bf16[256,2048]{1,0:T(8,128)(2,1)S(1)}, bf16[256,2048]{1,0:T(8,128)(2,1)S(1)}, u32[]{:S(2)}, u32[]{:S(2)}) collective-permute-start(bf16[256,2048]{1,0:T(8,128)(2,1)S(1)} %pad_maximum_fusion.12), channel_id=1, source_target_pairs={{0,1},{1,0},{2,3},{3,2},{4,5},{5,4},{6,7},{7,6},{8,9},{9,8},{10,11... | collective-permute-start | bytes 3145736 | tf_op jit(solution)/shard_map/ppermute | solution.py:271
  597.0 21.6 %collective-permute-start.109 = (bf16[128,2048]{1,0:T(8,128)(2,1)S(1)}, bf16[128,2048]{1,0:T(8,128)(2,1)S(1)}, u32[]{:S(2)}, u32[]{:S(2)}) collective-permute-start(bf16[128,2048]{1,0:T(8,128)(2,1)S(1)} %fusion.25), channel_id=1, source_target_pairs={{0,2},{1,3},{2,0},{3,1},{4,6},{5,7},{6,4},{7,5},{8,10},{9,11},{10,... | collective-permute-start | bytes 1572872 | tf_op jit(solution)/shard_map/ppermute | solution.py:271
  607.4 24.5 %collective-permute-start.99 = (bf16[128,2048]{1,0:T(8,128)(2,1)S(1)}, bf16[128,2048]{1,0:T(8,128)(2,1)S(1)}, u32[]{:S(2)}, u32[]{:S(2)}) collective-permute-start(bf16[128,2048]{1,0:T(8,128)(2,1)S(1)} %copy-done.42), channel_id=1, source_target_pairs={{0,4},{1,3},{2,6},{3,1},{4,0},{5,7},{6,2},{7,5},{8,12},{9,11},{10,... | collective-permute-start | bytes 1572872 | tf_op jit(solution)/shard_map/ppermute | solution.py:271
  607.4 24.5 %collective-permute-start.98 = (bf16[1024,256]{1,0:T(8,128)(2,1)S(1)}, bf16[1024,256]{1,0:T(8,128)(2,1)S(1)}, u32[]{:S(2)}, u32[]{:S(2)}) collective-permute-start(bf16[1024,256]{1,0:T(8,128)(2,1)S(1)} %dynamic-slice_convert_fusion.1), channel_id=1, source_target_pairs={{0,8},{1,9},{2,10},{3,11},{4,12},{5,13},{6,14},{7,15},{8,0},{9,1},... | collective-permute-start | bytes 1572872 | tf_op jit(solution)/shard_map/ppermute | solution.py:271
  633.4 40.6 %collective-permute-start.102 = (bf16[128,2048]{1,0:T(8,128)(2,1)S(1)}, bf16[128,2048]{1,0:T(8,128)(2,1)S(1)}, u32[]{:S(2)}, u32[]{:S(2)}) collective-permute-start(bf16[128,2048]{1,0:T(8,128)(2,1)S(1)} %maximum_select_fusion.8), channel_id=1, source_target_pairs={{0,8},{1,9},{2,10},{3,11},{4,12},{5,13},{6,14},{7,15},{8,0},{9,1},... | collective-permute-start | bytes 1572872 | tf_op jit(solution)/shard_map/ppermute | solution.py:271
  635.3 39.0 %collective-permute-start.101 = (bf16[128,2048]{1,0:T(8,128)(2,1)S(1)}, bf16[128,2048]{1,0:T(8,128)(2,1)S(1)}, u32[]{:S(2)}, u32[]{:S(2)}) collective-permute-start(bf16[128,2048]{1,0:T(8,128)(2,1)S(1)} %add_convert_fusion.13), channel_id=1, source_target_pairs={{0,24},{1,25},{2,26},{3,27},{4,28},{5,29},{6,30},{7,31},{8,0},{9,1... | collective-permute-start | bytes 1572872 | tf_op jit(solution)/shard_map/ppermute | solution.py:271
  637.0 40.0 %collective-permute-start.105 = (bf16[1024,256]{1,0:T(8,128)(2,1)S(1)}, bf16[1024,256]{1,0:T(8,128)(2,1)S(1)}, u32[]{:S(2)}, u32[]{:S(2)}) collective-permute-start(bf16[1024,256]{1,0:T(8,128)(2,1)S(1)} %dynamic-slice_convert_fusion), channel_id=1, source_target_pairs={{0,8},{1,9},{2,10},{3,11},{4,12},{5,13},{6,14},{7,15},{8,0},{9,1},... | collective-permute-start | bytes 1572872 | tf_op jit(solution)/shard_map/ppermute | solution.py:271
  637.5 36.5 %collective-permute-start.104 = (bf16[512,256]{1,0:T(8,128)(2,1)S(1)}, bf16[512,256]{1,0:T(8,128)(2,1)S(1)}, u32[]{:S(2)}, u32[]{:S(2)}) collective-permute-start(bf16[512,256]{1,0:T(8,128)(2,1)S(1)} %dynamic-slice_convert_fusion.5), channel_id=1, source_target_pairs={{0,16},{1,17},{2,18},{3,19},{4,20},{5,21},{6,22},{7,23},{8,24},{9,... | collective-permute-start | bytes 786440 | tf_op jit(solution)/shard_map/ppermute | solution.py:271
  637.8 35.9 %collective-permute-start.103 = (bf16[512,256]{1,0:T(8,128)(2,1)S(1)}, bf16[512,256]{1,0:T(8,128)(2,1)S(1)}, u32[]{:S(2)}, u32[]{:S(2)}) collective-permute-start(bf16[512,256]{1,0:T(8,128)(2,1)S(1)} %add_convert_fusion.25), channel_id=1, source_target_pairs={{0,16},{1,17},{2,18},{3,19},{4,20},{5,21},{6,22},{7,23},{8,24},{9,... | collective-permute-start | bytes 786440 | tf_op jit(solution)/shard_map/ppermute | solution.py:271
  677.0 55.4 %collective-permute-start.116 = (bf16[256,2048]{1,0:T(8,128)(2,1)S(1)}, bf16[256,2048]{1,0:T(8,128)(2,1)S(1)}, u32[]{:S(2)}, u32[]{:S(2)}) collective-permute-start(bf16[256,2048]{1,0:T(8,128)(2,1)S(1)} %maximum_select_fusion.5), channel_id=1, source_target_pairs={{0,4},{1,5},{2,6},{3,7},{4,0},{5,1},{6,2},{7,3},{8,12},{9,13},{10,... | collective-permute-start | bytes 3145736 | tf_op jit(solution)/shard_map/ppermute | solution.py:271
  679.6 25.9 %collective-permute-start.118 = (bf16[512,256]{1,0:T(8,128)(2,1)S(1)}, bf16[512,256]{1,0:T(8,128)(2,1)S(1)}, u32[]{:S(2)}, u32[]{:S(2)}) collective-permute-start(bf16[512,256]{1,0:T(8,128)(2,1)S(1)} %dynamic-slice_convert_fusion.4), channel_id=1, source_target_pairs={{0,16},{1,17},{2,18},{3,19},{4,20},{5,21},{6,22},{7,23},{8,24},{9,... | collective-permute-start | bytes 786440 | tf_op jit(solution)/shard_map/ppermute | solution.py:271
  680.2 25.0 %collective-permute-start.117 = (bf16[512,256]{1,0:T(8,128)(2,1)S(1)}, bf16[512,256]{1,0:T(8,128)(2,1)S(1)}, u32[]{:S(2)}, u32[]{:S(2)}) collective-permute-start(bf16[512,256]{1,0:T(8,128)(2,1)S(1)} %add_convert_fusion.24), channel_id=1, source_target_pairs={{0,16},{1,17},{2,18},{3,19},{4,20},{5,21},{6,22},{7,23},{8,24},{9,... | collective-permute-start | bytes 786440 | tf_op jit(solution)/shard_map/ppermute | solution.py:271
  682.6 24.1 %collective-permute-start.115 = (bf16[1024,256]{1,0:T(8,128)(2,1)S(1)}, bf16[1024,256]{1,0:T(8,128)(2,1)S(1)}, u32[]{:S(2)}, u32[]{:S(2)}) collective-permute-start(bf16[1024,256]{1,0:T(8,128)(2,1)S(1)} %maximum_select_fusion.15), channel_id=1, source_target_pairs={{0,8},{1,9},{2,10},{3,11},{4,12},{5,13},{6,14},{7,15},{8,0},{9,1},... | collective-permute-start | bytes 1572872 | tf_op jit(solution)/shard_map/ppermute | solution.py:271
  684.0 32.1 %collective-permute-start.106 = (bf16[128,2048]{1,0:T(8,128)(2,1)S(1)}, bf16[128,2048]{1,0:T(8,128)(2,1)S(1)}, u32[]{:S(2)}, u32[]{:S(2)}) collective-permute-start(bf16[128,2048]{1,0:T(8,128)(2,1)S(1)} %add_convert_fusion.10), channel_id=1, source_target_pairs={{0,8},{1,9},{2,10},{3,11},{4,12},{5,13},{6,14},{7,15},{8,16},{9,17... | collective-permute-start | bytes 1572872 | tf_op jit(solution)/shard_map/ppermute | solution.py:271
  705.3 27.2 %collective-permute-start.107 = (bf16[128,2048]{1,0:T(8,128)(2,1)S(1)}, bf16[128,2048]{1,0:T(8,128)(2,1)S(1)}, u32[]{:S(2)}, u32[]{:S(2)}) collective-permute-start(bf16[128,2048]{1,0:T(8,128)(2,1)S(1)} %add_convert_fusion.9), channel_id=1, source_target_pairs={{0,16},{1,17},{2,18},{3,19},{4,20},{5,21},{6,22},{7,23},{8,24},{9,... | collective-permute-start | bytes 1572872 | tf_op jit(solution)/shard_map/ppermute | solution.py:271
  705.5 42.5 %collective-permute-start.129 = (f32[34816]{0:T(1024)S(1)}, f32[34816]{0:T(1024)S(1)}, u32[]{:S(2)}, u32[]{:S(2)}) collective-permute-start(f32[34816]{0:T(1024)S(1)} %add.556), channel_id=1, source_target_pairs={{0,2},{1,3},{2,0},{3,1},{4,6},{5,7},{6,4},{7,5},{8,10},{9,11},{10,... | collective-permute-start | bytes 417800 | tf_op jit(solution)/shard_map/ppermute | solution.py:271
  706.7 45.5 %collective-permute-start.111 = (f32[3072]{0:T(1024)}, f32[3072]{0:T(1024)}, u32[]{:S(2)}, u32[]{:S(2)}) collective-permute-start(f32[3072]{0:T(1024)} %fusion.70), channel_id=1, source_target_pairs={{0,8},{1,9},{2,10},{3,11},{4,12},{5,13},{6,14},{7,15},{8,0},{9,1},... | collective-permute-start | bytes 36872 | tf_op jit(solution)/shard_map/ppermute | solution.py:271
  733.4 24.2 %collective-permute-start.121 = (bf16[512,256]{1,0:T(8,128)(2,1)S(1)}, bf16[512,256]{1,0:T(8,128)(2,1)}, u32[]{:S(2)}, u32[]{:S(2)}) collective-permute-start(bf16[512,256]{1,0:T(8,128)(2,1)S(1)} %add_convert_fusion.23), channel_id=1, source_target_pairs={{0,16},{1,17},{2,18},{3,19},{4,20},{5,21},{6,22},{7,23},{8,24},{9,... | collective-permute-start | bytes 786440 | tf_op jit(solution)/shard_map/ppermute | solution.py:271
  733.4 25.5 %collective-permute-start.120 = (bf16[1024,256]{1,0:T(8,128)(2,1)S(1)}, bf16[1024,256]{1,0:T(8,128)(2,1)}, u32[]{:S(2)}, u32[]{:S(2)}) collective-permute-start(bf16[1024,256]{1,0:T(8,128)(2,1)S(1)} %maximum_select_fusion.16), channel_id=1, source_target_pairs={{0,8},{1,9},{2,10},{3,11},{4,12},{5,13},{6,14},{7,15},{8,0},{9,1},... | collective-permute-start | bytes 1572872 | tf_op jit(solution)/shard_map/ppermute | solution.py:271
  736.0 24.8 %collective-permute-start.119 = (bf16[2048,256]{1,0:T(8,128)(2,1)}, bf16[2048,256]{1,0:T(8,128)(2,1)}, u32[]{:S(2)}, u32[]{:S(2)}) collective-permute-start(bf16[2048,256]{1,0:T(8,128)(2,1)} %maximum_select_fusion.4), channel_id=1, source_target_pairs={{0,4},{1,5},{2,6},{3,7},{4,0},{5,1},{6,2},{7,3},{8,12},{9,13},{10,... | collective-permute-start | bytes 3145736 | tf_op jit(solution)/shard_map/ppermute | solution.py:271
  761.1 25.0 %collective-permute-start.122 = (bf16[2048,256]{1,0:T(8,128)(2,1)S(1)}, bf16[2048,256]{1,0:T(8,128)(2,1)S(1)}, u32[]{:S(2)}, u32[]{:S(2)}) collective-permute-start(bf16[2048,256]{1,0:T(8,128)(2,1)S(1)} %maximum_select_fusion.6), channel_id=1, source_target_pairs={{0,4},{1,5},{2,6},{3,7},{4,0},{5,1},{6,2},{7,3},{8,12},{9,13},{10,... | collective-permute-start | bytes 3145736 | tf_op jit(solution)/shard_map/ppermute | solution.py:271
  786.1 24.1 %collective-permute-start.124 = (bf16[2048,256]{1,0:T(8,128)(2,1)S(1)}, bf16[2048,256]{1,0:T(8,128)(2,1)S(1)}, u32[]{:S(2)}, u32[]{:S(2)}) collective-permute-start(bf16[2048,256]{1,0:T(8,128)(2,1)S(1)} %maximum_select_fusion.7), channel_id=1, source_target_pairs={{0,4},{1,5},{2,6},{3,7},{4,0},{5,1},{6,2},{7,3},{8,12},{9,13},{10,... | collective-permute-start | bytes 3145736 | tf_op jit(solution)/shard_map/ppermute | solution.py:271
  (168 other events, 2437.7 us)

commit v2 on v1

--- a/solution.py
+++ b/solution.py
@@ -1,4 +1,5 @@
 import functools
+import itertools
 import math
 
 import jax
@@ -207,7 +208,7 @@
         out_shape=[jax.ShapeDtypeStruct((length, width), t) for t in types]
         + [jax.ShapeDtypeStruct((width // HD, length, 1), jnp.float32)],
         cost_estimate=pl.CostEstimate(
-            flops=6 * length * width * (model_width + length),
+            flops=18 * length * width * (model_width + length),
             bytes_accessed=2 * model_width * (length + 3 * width),
             transcendentals=width // HD * length * length,
         ),
@@ -241,7 +242,7 @@
         out_shape=[jax.ShapeDtypeStruct((length, wide), low)] * 3
         + [jax.ShapeDtypeStruct((1, wide), jnp.float32)] * 2,
         cost_estimate=pl.CostEstimate(
-            flops=2 * length * wide * (model_width + 5 * length),
+            flops=8 * length * wide * (model_width + 5 * length),
             bytes_accessed=2 * model_width * (length + wide) + 16 * length * wide,
             transcendentals=wide // HD * length * length,
         ),
@@ -290,6 +291,11 @@
 
     def flip_z(self, value, bit):
         return self.send(value, lambda z, x, y, c: (z ^ bit, x, y, c))
+
+    def plane_groups(self):
+        return [
+            [(z * 2 + x) * 4 + t for x in range(2) for t in range(4)] for z in range(self.n_z)
+        ]
 
     def spread(self, block, axis=0):
         near = jnp.concatenate([block, self.first(block)], axis=axis)
@@ -426,23 +432,17 @@
 
 def expert_kernel(
     carried,
-    tile,
     place,
-    near_ref,
-    far_ref,
-    grad_near_ref,
-    grad_far_ref,
-    kept_ref,
-    router_ref,
-    gate_hbm,
-    up_hbm,
-    down_hbm,
+    ids_ref,
     *refs,
 ):
+    blocks, refs = refs[:8], refs[8:]
+    grads_hbm, kept_ref, router_ref, gate_hbm, up_hbm, down_hbm = refs[:6]
     (
-        mix_hbm,
-        part_hbm,
+        own_part,
+        other_part,
         sum_ref,
+        mix_all,
         rows_all,
         grad_all,
         hidden_all,
@@ -450,139 +450,171 @@
         up_all,
         rows,
         grads,
-        gate_w,
-        up_w,
+        weights,
         down_w,
         mix,
         part,
         hidden_v,
-        gate_v,
-        up_v,
+        back_v,
         sem_in,
         sem_out,
-    ) = refs[carried:]
-    local_experts, _, hidden_width = gate_w.shape
-    spans = [slice(e * hidden_width, (e + 1) * hidden_width) for e in range(local_experts)]
-    loads = {}
-    plan = [(("x", 0), near_ref, rows.at[0])]
-    for e in range(local_experts):
-        plan.append((("g", e), gate_hbm.at[e], gate_w.at[e]))
-        plan.append((("u", e), up_hbm.at[e], up_w.at[e]))
-        if e == 0:
-            plan.append((("c", 0), grad_near_ref, grads.at[0]))
-        plan.append((("d", e), down_hbm.at[spans[e], :], down_w.at[spans[e], :]))
-    plan.append((("x", 1), far_ref, rows.at[1]))
-    plan.append((("c", 1), grad_far_ref, grads.at[1]))
-    for n, (key, source, target) in enumerate(plan):
-        loads[key] = pltpu.make_async_copy(source, target, sem_in.at[n])
-        loads[key].start()
-    stores = []
+    ) = refs[6 + carried :]
+    local_experts, _, width = gate_hbm.shape
+    block = blocks[0].shape[0]
+    tile = 2 * block
+    loads, stores = [], []
+
+    def load(source, target):
+        copy = pltpu.make_async_copy(source, target, sem_in.at[len(loads)])
+        copy.start()
+        loads.append(copy)
+        return copy
 
     def store(source, target):
         copy = pltpu.make_async_copy(source, target, sem_out.at[len(stores)])
         copy.start()
         stores.append(copy)
 
-    for t in range(2):
-        at = pl.ds(place + t * tile, tile)
-        loads["x", t].wait()
-        store(rows.at[t], rows_all.at[at, :])
-        x = rows[t]
+    def load_rows(t):
+        return [
+            load(blocks[2 * t + i], rows.at[pl.ds(t * tile + i * block, block), :])
+            for i in range(2)
+        ]
+
+    def load_grads(t):
+        copies = []
+        for i in range(2):
+            at = pl.multiple_of(ids_ref[0, place // block + 2 * t + i] * block, block)
+            copies.append(
+                load(
+                    grads_hbm.at[pl.ds(at, block), :],
+                    grads.at[pl.ds(t * tile + i * block, block), :],
+                )
+            )
+        return copies
+
+    row_loads = [load_rows(0)]
+    weight_loads = []
+    for e in range(local_experts):
+        weight_loads.append(
+            [
+                load(gate_hbm.at[e], weights.at[:, pl.ds(2 * e * width, width)]),
+                load(up_hbm.at[e], weights.at[:, pl.ds((2 * e + 1) * width, width)]),
+            ]
+        )
+        if e == 0:
+            grad_loads = [load_grads(0)]
+            down_load = load(down_hbm, down_w)
+    for t in range(1, 4):
+        row_loads.append(load_rows(t))
+        grad_loads.append(load_grads(t))
+
+    for t in range(4):
+        at = pl.ds(t * tile, tile)
+        span = slice(t * tile, (t + 1) * tile)
+        whole = pl.ds(place + t * tile, tile)
+        half = pl.ds((t % 2) * tile, tile)
+        for copy in row_loads[t]:
+            copy.wait()
+        store(rows.at[at, :], rows_all.at[whole, :])
+        x = rows[span, :]
         logits = jnp.dot(x, router_ref[...], preferred_element_type=jnp.float32)
         shifted = jnp.exp(logits - jnp.max(logits, axis=-1, keepdims=True))
-        kept = kept_ref[t * tile : (t + 1) * tile, :]
-        gates = shifted[:, :local_experts] / jnp.sum(shifted, axis=-1, keepdims=True) * kept
+        gates = shifted[:, :local_experts] / jnp.sum(shifted, axis=-1, keepdims=True)
+        gates = gates * kept_ref[span, :]
         sums = []
-        total = None
         for e in range(local_experts):
+            low, mid, high = 2 * e * width, (2 * e + 1) * width, (2 * e + 2) * width
+            here = slice(e * width, (e + 1) * width)
             gate = gates[:, e : e + 1]
             if t == 0:
-                loads["g", e].wait()
-            gate_pre = jnp.dot(x, gate_w[e], preferred_element_type=jnp.float32)
-            if t == 0:
-                loads["u", e].wait()
-            up_pre = jnp.dot(x, up_w[e], preferred_element_type=jnp.float32)
+                for copy in weight_loads[e]:
+                    copy.wait()
+            pre = jnp.dot(x, weights[:, low:high], preferred_element_type=jnp.float32)
+            gate_pre, up_pre = pre[:, :width], pre[:, width:]
             if e == 0:
-                loads["c", t].wait()
-                store(grads.at[t], grad_all.at[at, :])
-            if t == 0:
-                loads["d", e].wait()
-            back = contract_cols(grads[t], down_w[spans[e], :]) * gate
+                for copy in grad_loads[t]:
+                    copy.wait()
+                store(grads.at[at, :], grad_all.at[whole, :])
+                if t == 0:
+                    down_load.wait()
+            back = contract_cols(grads[span, :], down_w[here, :]) * gate
             sig = jax.nn.sigmoid(gate_pre)
             act = gate_pre * sig
             hidden = (act * up_pre).astype(jnp.bfloat16).astype(jnp.float32)
             sums.append(jnp.sum(hidden * back, axis=-1, keepdims=True))
-            hidden_v[t, :, spans[e]] = (hidden * gate).astype(jnp.bfloat16)
-            grad_gate = (back * up_pre * sig * (1.0 + gate_pre * (1.0 - sig))).astype(
-                jnp.bfloat16
+            hidden_v[span, here] = (hidden * gate).astype(jnp.bfloat16)
+            back_v[span, low:mid] = (
+                back * up_pre * sig * (1.0 + gate_pre * (1.0 - sig))
+            ).astype(jnp.bfloat16)
+            back_v[span, mid:high] = (back * act).astype(jnp.bfloat16)
+            store(back_v.at[at, pl.ds(low, width)], gate_all.at[e, whole, :])
+            store(back_v.at[at, pl.ds(mid, width)], up_all.at[e, whole, :])
+        store(hidden_v.at[at, :], hidden_all.at[whole, :])
+        sum_ref[span, :] = jnp.concatenate(sums, axis=1)
+        part[span, :] = contract_cols(back_v[span, :], weights[...]).astype(jnp.bfloat16)
+        store(part.at[at, :], (own_part if t < 2 else other_part).at[half, :])
+        mix[span, :] = jnp.dot(
+            hidden_v[span, :], down_w[...], preferred_element_type=jnp.float32
+        ).astype(jnp.bfloat16)
+        for i in range(2):
+            home = pl.multiple_of(ids_ref[1, place // block + 2 * t + i] * block, block)
+            store(
+                mix.at[pl.ds(t * tile + i * block, block), :], mix_all.at[pl.ds(home, block), :]
             )
-            grad_up = (back * act).astype(jnp.bfloat16)
-            gate_v[t, e] = grad_gate
-            up_v[t, e] = grad_up
-            piece = contract_cols(grad_gate, gate_w[e]) + contract_cols(grad_up, up_w[e])
-            total = piece if total is None else total + piece
-        part[t] = total.astype(jnp.bfloat16)
-        store(part.at[t], part_hbm.at[pl.ds(t * tile, tile), :])
-        for e in range(local_experts):
-            store(gate_v.at[t, e], gate_all.at[e, at, :])
-            store(up_v.at[t, e], up_all.at[e, at, :])
-        store(hidden_v.at[t], hidden_all.at[at, :])
-        sum_ref[t * tile : (t + 1) * tile, :] = jnp.concatenate(sums, axis=1)
-        mix[t] = jnp.dot(
-            hidden_v[t], down_w[...], preferred_element_type=jnp.float32
-        ).astype(jnp.bfloat16)
-        store(mix.at[t], mix_hbm.at[pl.ds(t * tile, tile), :])
     for copy in stores:
         copy.wait()
 
 
 def run_experts(
-    place, count, rows, grads, kept, router, gate_weight, up_weight, down_flat, carried
+    place, count, ids, blocks, grads, kept, router, gate_weight, up_weight, down_flat, carried
 ):
-    tile, model_width = rows[0].shape
-    local_experts, _, hidden_width = gate_weight.shape
-    flat = local_experts * hidden_width
-    tok_count = 2 * tile
+    block, model_width = blocks[0].shape
+    local_experts, _, width = gate_weight.shape
+    flat = local_experts * width
+    tok_count = 8 * block
     whole = tok_count * count
     low = jnp.bfloat16
     hbm = pl.BlockSpec(memory_space=pl.ANY)
     vmem = pl.BlockSpec(memory_space=pltpu.VMEM)
+    plane = jax.ShapeDtypeStruct((tok_count // 2, model_width), low)
     out = pl.pallas_call(
-        functools.partial(expert_kernel, len(carried), tile, place * tok_count),
-        in_specs=[hbm] * 4 + [vmem] * 2 + [hbm] * (3 + len(carried)),
-        out_specs=[hbm, hbm, vmem] + [hbm] * 5,
-        out_shape=[
-            jax.ShapeDtypeStruct((tok_count, model_width), low),
-            jax.ShapeDtypeStruct((tok_count, model_width), low),
+        functools.partial(expert_kernel, len(carried), place * tok_count),
+        in_specs=[pl.BlockSpec(memory_space=pltpu.SMEM)]
+        + [hbm] * 9
+        + [vmem] * 2
+        + [hbm] * (3 + len(carried)),
+        out_specs=[hbm] * 2 + [vmem] + [hbm] * 6,
+        out_shape=[plane] * 2
+        + [
             jax.ShapeDtypeStruct((tok_count, local_experts), jnp.float32),
             jax.ShapeDtypeStruct((whole, model_width), low),
             jax.ShapeDtypeStruct((whole, model_width), low),
+            jax.ShapeDtypeStruct((whole, model_width), low),
             jax.ShapeDtypeStruct((whole, flat), low),
-            jax.ShapeDtypeStruct((local_experts, whole, hidden_width), low),
-            jax.ShapeDtypeStruct((local_experts, whole, hidden_width), low),
+            jax.ShapeDtypeStruct((local_experts, whole, width), low),
+            jax.ShapeDtypeStruct((local_experts, whole, width), low),
         ],
         scratch_shapes=[
-            pltpu.VMEM((2, tile, model_width), low),
-            pltpu.VMEM((2, tile, model_width), low),
-            pltpu.VMEM(gate_weight.shape, low),
-            pltpu.VMEM(up_weight.shape, low),
+            pltpu.VMEM((tok_count, model_width), low),
+            pltpu.VMEM((tok_count, model_width), low),
+            pltpu.VMEM((model_width, 2 * flat), low),
             pltpu.VMEM(down_flat.shape, low),
-            pltpu.VMEM((2, tile, model_width), low),
-            pltpu.VMEM((2, tile, model_width), low),
-            pltpu.VMEM((2, tile, flat), low),
-            pltpu.VMEM((2, local_experts, tile, hidden_width), low),
-            pltpu.VMEM((2, local_experts, tile, hidden_width), low),
-            pltpu.SemaphoreType.DMA((4 + 3 * local_experts,)),
-            pltpu.SemaphoreType.DMA((2 * (5 + 2 * local_experts),)),
+            pltpu.VMEM((tok_count, model_width), low),
+            pltpu.VMEM((tok_count, model_width), low),
+            pltpu.VMEM((tok_count, flat), low),
+            pltpu.VMEM((tok_count, 2 * flat), low),
+            pltpu.SemaphoreType.DMA((17 + 2 * local_experts,)),
+            pltpu.SemaphoreType.DMA((4 * (6 + 2 * local_experts),)),
         ],
-        input_output_aliases={9 + i: 3 + i for i in range(len(carried))},
+        input_output_aliases={15 + i: 3 + i for i in range(len(carried))},
         cost_estimate=pl.CostEstimate(
-            flops=16 * tok_count * model_width * flat,
+            flops=25 * tok_count * model_width * flat,
             bytes_accessed=12 * model_width * (tok_count + flat),
             transcendentals=tok_count * flat,
         ),
         name="experts",
-    )(*rows, *grads, kept, router, gate_weight, up_weight, down_flat, *carried)
+    )(ids, *blocks, grads, kept, router, gate_weight, up_weight, down_flat, *carried)
     return out[:3], list(out[3:])
 
 
@@ -621,29 +653,52 @@
 
 class Spread:
     def __init__(self, links, block, order):
-        self.links, self.order = links, order
-        self.blocks, self.near, self.far, self.other = {0: block}, {}, {}, {}
+        self.links, self.order, self.own = links, order, block
+        self.blocks, self.near, self.far, self.other = {}, {}, {}, {}
 
     def go_z(self, k, ties=()):
-        self.blocks[k] = self.links.along_z(after(self.blocks[0], ties), self.order[k])
-        return self.blocks[k]
+        block = self.own
+        if self.order[k]:
+            block = self.links.along_z(after(block, ties), self.order[k])
+        self.blocks[k] = block
+        return block
 
     def go_near(self, k, ties=()):
         block = after(self.blocks[k], ties)
-        self.near[k] = jnp.concatenate([block, self.links.first(block)], axis=0)
+        self.near[k] = [self.links.first(block), self.links.second(block)]
         return self.near[k]
 
     def go_far(self, k, ties=()):
-        self.far[k] = self.links.second(after(self.near[k], ties))
+        self.far[k] = self.links.second(after(self.near[k][0], ties))
         return self.far[k]
 
     def go_core(self, k, ties=()):
-        near, far = after((self.near[k], self.far[k]), ties)
-        self.other[k] = (self.links.core(near), self.links.core(far))
+        plane = after(self.plane(k), ties)
+        self.other[k] = [self.links.core(block) for block in plane]
         return self.other[k]
 
-    def plane(self, k, side):
-        return self.other[k] if side else (self.near[k], self.far[k])
+    def plane(self, k):
+        return [self.blocks[k], *self.near[k], self.far[k]]
+
+    def eight(self, k):
+        return self.plane(k) + self.other[k]
+
+
+def source_ids(links, order):
+    n_z = links.n_z
+    table, homes = [], []
+    for z, x, y, c in itertools.product(range(n_z), range(2), range(2), range(2)):
+        row, home = [], []
+        for k, r in enumerate(order):
+            for core in (c, 1 - c):
+                for dx, dy in [(0, 0), (1 - core, core), (core, 1 - core), (1, 1)]:
+                    member = (x ^ dx) * 4 + (y ^ dy) * 2 + core
+                    row.append(member if k == 0 else member * (n_z - 1) + k - 1)
+                    home.append((z - r) % n_z * 8 + member)
+        table.append(row)
+        homes.append(home)
+    here = lax.axis_index(AXES)
+    return jnp.asarray([table, homes], jnp.int32)[:, here]
 
 
 class Gathering:
@@ -673,7 +728,7 @@
     def go_z(self, k, ties=()):
         rows = self.terms[k][0].shape[0]
         sent = self.total(k, 0, rows // 4)
-        if k:
+        if self.order[k]:
             sent = self.links.along_z(after(sent.astype(jnp.bfloat16), ties), -self.order[k])
         self.terms[k] = [sent]
         return sent
@@ -703,106 +758,107 @@
     down_flat = down_weight.reshape(local_experts * hidden_width, model_width)
     router = jnp.roll(router_weight, -first_expert, axis=1)
     n_z = links.n_z
+    ids = source_ids(links, order)
     kept_own = [
-        [lax.dynamic_slice_in_dim(k, first_expert, local_experts, axis=1) for k in kept_chunks[r]]
+        lax.dynamic_slice_in_dim(
+            jnp.concatenate(kept_chunks[r]), first_expert, local_experts, axis=1
+        )
         for r in order
     ]
     rows = Spread(links, mixture_in, order)
     back = Gathering(links, order)
-    mix = Gathering(links, order)
     carried = []
-    own, partner = [None] * n_z, [None] * n_z
-
-    def experts(k, side, ties):
+    done = [None] * n_z
+
+    def experts(k, ties):
         nonlocal carried
-        result, carried = run_experts(
-            2 * k + side,
-            2 * n_z,
-            rows.plane(k, side),
-            grads.plane(k, side),
-            after(kept_own[k][side], ties),
+        done[k], carried = run_experts(
+            k,
+            n_z,
+            ids,
+            rows.eight(k),
+            grads[k],
+            after(kept_own[k], ties),
             router,
             gate_weight,
             up_weight,
             down_flat,
             carried,
         )
-        return result
-
+
+    rows.go_z(0)
+    held = [rows.go_z(1)]
+    held.append(rows.go_z(2, held))
+    held.append(rows.go_z(3, held))
     rows.go_near(0)
-    rows.go_z(1)
-    grads.go_core(0)
-    grads.go_core(1)
     rows.go_far(0)
-    held = [grads.go_near(2)]
+    rows.go_core(0)
+    held += rows.go_near(1, [rows.blocks[1]])
+    pin = rows.near[1]
     for k in range(n_z):
-        own[k] = experts(k, 0, held)
-        held = [rows.go_core(k)]
-        if k + 1 < n_z:
-            held.append(rows.go_near(k + 1))
-        if k + 2 < n_z:
-            held.append(rows.go_z(k + 2, [rows.blocks[k + 1]]))
-            if k == 0:
-                held.append(grads.go_far(2))
-                grads.go_core(2)
-            elif k == 1:
-                held.append(grads.go_far(3))
-                grads.go_core(3)
-        if k >= 2:
-            held.append(back.go_first(k - 2))
-        if k >= 1:
-            held.append(back.go_core(k - 1, own[k - 1][1], partner[k - 1][1]))
-        partner[k] = experts(k, 1, held)
+        experts(k, held)
         held = []
         if k + 1 < n_z:
-            rows.go_far(k + 1)
+            rows.go_far(k + 1, pin)
+        if k + 2 < n_z:
+            held += rows.go_near(k + 2, pin)
+        pin = [done[k][2]]
+        if k + 1 < n_z:
+            rows.go_core(k + 1, pin)
         if k == 0:
-            held.append(grads.go_near(3))
-        if k >= 2:
-            held.append(back.go_z(k - 2))
-        if k >= 1:
-            held.append(back.go_second(k - 1))
+            held.append(back.go_core(0, done[0][0], done[0][1]))
+        elif k == 1:
+            held.append(back.go_second(0, [done[0][2]]))
+        elif k == 2:
+            held.append(back.go_core(1, done[1][0], done[1][1], [done[1][2]]))
+            held.append(back.go_first(0, [done[1][2]]))
+    mix_all = carried[0]
+    step_zero = [
+        back.go_second(1, [done[2][2]]),
+        back.go_core(2, done[2][0], done[2][1], [done[2][2]]),
+        back.go_z(0, [done[2][2]]),
+    ]
     step_one = [
-        back.go_core(n_z - 1, own[n_z - 1][1], partner[n_z - 1][1]),
-        back.go_first(n_z - 2),
+        back.go_core(3, done[3][0], done[3][1]),
+        back.go_second(2, step_zero),
+        back.go_first(1, step_zero),
     ]
-    rows_all, grad_all, hidden_all, gate_all, up_all = carried
     step_two = [
-        back.go_second(n_z - 1),
-        back.go_z(n_z - 2),
-        mix.go_core(0, own[0][0], partner[0][0], step_one),
-        mix.go_core(1, own[1][0], partner[1][0], step_one),
+        back.go_second(3, step_one),
+        back.go_first(2, step_one),
+        back.go_z(1, step_one),
     ]
-    gate_all = after(gate_all, step_one)
-    gate_grad = jnp.stack([contract_rows(rows_all, gate_all[e]) for e in range(local_experts)])
-    step_three = [
-        back.go_first(n_z - 1),
-        mix.go_core(2, own[2][0], partner[2][0], step_two),
-        mix.go_core(3, own[3][0], partner[3][0], step_two),
-    ]
-    up_all = after(up_all, step_two)
-    up_grad = jnp.stack([contract_rows(rows_all, up_all[e]) for e in range(local_experts)])
-    back.go_z(n_z - 1)
-    early_x = links.flip_x(after(attention_in, step_three))
-    mix.go_second(0, [early_x])
-    hidden_all = after(hidden_all, step_three)
-    down_grad = contract_rows(hidden_all, grad_all).reshape(
-        local_experts, hidden_width, model_width
+    early_x = links.flip_x(after(attention_in, step_two))
+    step_three = [back.go_first(3), back.go_z(2, step_two), early_x]
+    far_x = links.flip_y(after(early_x, step_three))
+    back.go_z(3)
+    input_grad = after(back.home(), far_x)
+    peer_rows = jnp.concatenate(
+        [early_x, links.core(early_x), far_x, links.core(far_x)], axis=0
     )
     full = []
-    for parts in (own, partner):
+    for half in range(2):
         planes = []
         for k in range(n_z):
-            local = parts[k][2].reshape(-1, tok_rows, local_experts).transpose(0, 2, 1)
+            local = done[k][2].reshape(2, -1, tok_rows, local_experts)[half].transpose(0, 2, 1)
             zero = jnp.zeros((local.shape[0], experts_all, tok_rows), jnp.float32)
             planes.append(lax.dynamic_update_slice_in_dim(zero, local, first_expert, axis=1))
         full.append(jnp.stack(planes, axis=1))
     small = links.collect(full[0], full[1], jnp.float32)[0]
-    weighted = small[0]
-    for k in range(1, n_z):
-        weighted = weighted + links.along_z(small[k], -order[k])
-    input_grad = after(back.home(), [mix.terms[0][-1]])
-    return mix, early_x, input_grad, weighted.T, gate_grad, up_grad, down_grad
+    weighted = functools.reduce(
+        jnp.add,
+        [links.along_z(small[k], -r) if r else small[k] for k, r in enumerate(order)],
+    )
+    return mix_all, peer_rows, input_grad, weighted.T, carried[1:]
+
+
+def expert_weight_grad(saved, which, ties):
+    rows_all, grad_all, hidden_all, gate_all, up_all = saved
+    if which == 2:
+        down_grad = contract_rows(after(hidden_all, ties), grad_all)
+        return down_grad.reshape(gate_all.shape[0], gate_all.shape[2], grad_all.shape[1])
+    parts = after((gate_all, up_all)[which], ties)
+    return jnp.stack([contract_rows(rows_all, parts[e]) for e in range(parts.shape[0])])
 
 
 def body(
@@ -830,7 +886,7 @@
     capacity = tok_rows * top_count * 7 // (8 * experts_all)
     local_width = query_weight.shape[1]
     n_exp, n_tp = mesh_sizes
-    dense = experts_all <= 2 * top_count and n_tp == 4 and n_exp % 2 == 0
+    dense = experts_all <= 2 * top_count and n_tp == 4 and n_exp == 8
     links = Links(n_exp, n_tp)
     grad_out = cotangent.astype(jnp.float32)
     if dense:
@@ -844,11 +900,12 @@
             ]
             for r in range(n_exp // 2)
         ]
-        order = [0, 1, 3, 2] if n_exp == 8 else list(range(n_exp // 2))
-        grads = Spread(links, cotangent, order)
-        held = [grads.go_near(0), grads.go_z(1)]
-    else:
-        held = []
+        order = [0, 2, 1, 3]
+        groups = links.plane_groups()
+        near_grads = lax.all_gather(
+            cotangent, AXES, axis=0, tiled=True, axis_index_groups=groups
+        )
+        moved = [links.along_z(cotangent, r) for r in order[1:]]
     inputs = tokens.astype(jnp.float32)
     scale_one = inverse_rms(inputs)
     normed_one = inputs * scale_one
@@ -869,19 +926,18 @@
     )
     gains = (query_norm[None, :], key_norm[None, :])
     gathered_rows = links.tp_rows(attention_in)
-    rows_held = after(gathered_rows, held)
+    *saved, attended, log_totals = attend(
+        gathered_rows, (query_weight, key_weight, value_weight), gains, tables
+    )
     if dense:
-        held = [
-            grads.go_far(0, [gathered_rows]),
-            grads.go_near(1, [grads.far[0]]),
-            grads.go_z(2, [grads.blocks[1]]),
-        ]
-    *saved, attended, log_totals = attend(
-        rows_held, (query_weight, key_weight, value_weight), gains, tables
-    )
-    partial_block = jnp.dot(after(attended, held), output_weight, preferred_element_type=jnp.float32)
-    held = [grads.go_far(1), grads.go_z(3, [grads.blocks[2]])] if dense else []
-    attention_block = after(links.tp_sum(partial_block), held)
+        far_grads = jnp.concatenate(after(moved, [attended, near_grads]), axis=0)
+        far_grads = lax.all_gather(
+            far_grads, AXES, axis=0, tiled=True, axis_index_groups=groups
+        )
+        grads = [near_grads] + [far_grads] * 3
+    attention_block = links.tp_sum(
+        jnp.dot(attended, output_weight, preferred_element_type=jnp.float32)
+    )
     middle = inputs + attention_block
     scale_two = inverse_rms(middle)
     normed_two = middle * scale_two
@@ -889,7 +945,7 @@
     logits = jnp.dot(mixture_in, router_weight, preferred_element_type=jnp.float32)
     probabilities = jax.nn.softmax(logits, axis=-1)
     if dense:
-        mix, early_x, grad_expert_in, weighted, gate_grad, up_grad, down_grad = moe_dense(
+        mix_all, peer_rows, grad_expert_in, weighted, expert_saved = moe_dense(
             links,
             order,
             attention_in,
@@ -912,7 +968,7 @@
             up_weight,
             down_weight,
         )
-        early_x = links.flip_x(attention_in)
+        peer_rows = links.tp_rows(links.flip_x(attention_in))
     grad_logits = weighted - probabilities * jnp.sum(weighted, axis=-1, keepdims=True)
     router_grad = jnp.dot(mixture_in.astype(jnp.float32).T, grad_logits, precision=HIGH)
     grad_mixture_in = grad_expert_in + jnp.dot(
@@ -924,12 +980,9 @@
     row_grad = links.tp_rows(grad_attention)
     wide = local_width // 2
     side = lax.axis_index("exp") % 2
-    peer_attention = links.flip_x(grad_attention)
-    attended_other = lax.dynamic_slice_in_dim(attended, (1 - side) * wide, wide, axis=1)
-    peer_rows = links.tp_rows(after(early_x, row_grad))
-    held = [peer_attention, peer_rows]
-    if dense:
-        held.append(mix.go_first(0))
+    own_cols = lax.dynamic_slice_in_dim(attended, side * wide, wide, axis=1)
+    other_cols = lax.dynamic_slice_in_dim(attended, (1 - side) * wide, wide, axis=1)
+    held = []
     results = [None, None]
     for turn in range(2):
         which = 1 - side if turn == 0 else side
@@ -946,9 +999,13 @@
             wide,
         )
     other = jnp.concatenate(results[0][:3], axis=1)
-    peer_grads = links.flip_x(after(other, held))
-    attended_peer = links.flip_x(after(attended_other, held))
-    peer_row_grad = links.tp_rows(after(peer_attention, held))
+    peer_grads = links.flip_x(other)
+    if dense:
+        mixture = lax.psum_scatter(
+            after(mix_all, peer_grads), AXES, scatter_dimension=0, tiled=True
+        )
+    other_half = contract_rows(other_cols, row_grad).astype(jnp.bfloat16)
+    other_half = links.flip_x(after(other_half, peer_grads))
     own_grads = jnp.concatenate(results[1][:3], axis=1)
 
     def in_order(own_part, other_part, axis):
@@ -965,68 +1022,72 @@
     total_grad = contract_cols(grad_queries, query_weight)
     total_grad = total_grad + contract_cols(grad_keys, key_weight)
     total_grad = total_grad + contract_cols(grad_values, value_weight)
-    held = [peer_row_grad, attended_peer]
-    grad_attention_in = links.tp_sum(after(total_grad, held))
-    attended_own = lax.dynamic_slice_in_dim(attended, side * wide, wide, axis=1)
-    own_parts = [attended_own] + [gathered_rows] * 3
-    peer_parts = [attended_peer] + [peer_rows] * 3
-    own_ends = [row_grad] + [own_grads[:, i * wide : (i + 1) * wide] for i in range(3)]
-    peer_ends = [peer_row_grad] + [peer_grads[:, i * wide : (i + 1) * wide] for i in range(3)]
-    pieces = [
-        HalfSum(links, contract_rows(p, q) + contract_rows(r, s))
-        for p, q, r, s in zip(own_parts, own_ends, peer_parts, peer_ends)
+    grad_attention_in = links.tp_sum(total_grad)
+    pieces = []
+    for i in range(3):
+        span = slice(i * wide, (i + 1) * wide)
+        total = contract_rows(gathered_rows, own_grads[:, span])
+        pieces.append(HalfSum(links, total + contract_rows(peer_rows, peer_grads[:, span])))
+    pieces.append(
+        HalfSum(links, contract_rows(own_cols, row_grad) + other_half.astype(jnp.float32))
+    )
+    ties = [pieces[0].go(0)]
+    attention_gain_grad = jnp.sum(grad_attention_in * normed_one, axis=0)
+    tokens_grad = grad_middle + norm_backward(
+        grad_attention_in * attention_gain, normed_one, scale_one
+    )
+    if dense:
+        sums = jnp.concatenate(
+            [
+                query_norm_grad,
+                key_norm_grad,
+                attention_gain_grad,
+                mixture_gain_grad,
+                router_grad.reshape(-1),
+            ]
+        )
+    flips = [
+        links.flip_x,
+        lambda v: links.flip_z(v, 1),
+        lambda v: links.flip_z(v, 2),
+        links.core,
+        links.flip_y,
     ]
     stages = pieces[0].stages()
     big_sums = [None] * 4
-    if dense:
-        mix_steps = (
-            [lambda t, k=k: mix.go_second(k, t) for k in range(1, links.n_z)]
-            + [lambda t, k=k: mix.go_first(k, t) for k in range(1, links.n_z)]
-            + [lambda t, k=k: mix.go_z(k, t) for k in range(links.n_z)]
-        )
-    else:
-        mix_steps = []
-    last = [None] * stages
-    ties = []
-    for step in range(stages + 4):
+    expert_grads = []
+    for step in range(stages + 3):
         moved = []
         for p in range(4):
-            stage = step - p
+            stage = step + 1 - p
             if 0 <= stage < stages:
                 moved.append(pieces[p].go(stage, ties))
             elif stage == stages:
                 whole = pieces[p].value
-                moved.append(links.flip_x(after(whole, ties)))
-                big_sums[p] = (whole, moved[-1])
-        for _ in range(2):
-            if mix_steps:
-                moved.append(mix_steps.pop(0)(ties))
+                got = links.flip_x(after(whole, ties))
+                big_sums[p] = in_order(whole, got, 1 if p < 3 else 0).astype(jnp.float32)
+                moved.append(big_sums[p])
+        if dense and step < 5:
+            got = flips[step](after(sums, ties))
+            if step > 2:
+                got = jnp.concatenate([jnp.zeros_like(got[: 2 * local_width]), got[2 * local_width :]])
+            sums = sums + got
+            moved.append(sums)
+        if dense and step in (1, 3, 5):
+            expert_grads.append(expert_weight_grad(expert_saved, step // 2, ties))
+            moved.append(expert_grads[-1])
         ties = moved
-    big_sums = [
-        in_order(whole, got, axis).astype(jnp.float32)
-        for (whole, got), axis in zip(big_sums, (0, 1, 1, 1))
-    ]
-    output_weight_grad, query_weight_grad, key_weight_grad, value_weight_grad = big_sums
+    query_weight_grad, key_weight_grad, value_weight_grad, output_weight_grad = big_sums
     if dense:
-        while mix_steps:
-            mix_steps.pop(0)([])
-        mixture = mix.home()
+        gate_grad, up_grad, down_grad = expert_grads
     output = (middle + mixture).astype(jnp.bfloat16)
-    attention_gain_grad = jnp.sum(grad_attention_in * normed_one, axis=0)
-    tokens_grad = grad_middle + norm_backward(
-        grad_attention_in * attention_gain, normed_one, scale_one
-    )
     if dense:
-        early = jnp.concatenate([mixture_gain_grad, router_grad.reshape(-1)])
-        early = links.sum_tp(links.sum_exp(early))
-        late = jnp.concatenate([query_norm_grad, key_norm_grad, attention_gain_grad])
-        late = links.sum_exp(late)
-        norm_sums = (late[:local_width], late[local_width : 2 * local_width])
-        gain_sum = links.sum_tp(late[2 * local_width :])
+        norm_sums = (sums[:local_width], sums[local_width : 2 * local_width])
+        sums = sums[2 * local_width :]
         shared_sums = (
-            gain_sum,
-            early[:model_width],
-            early[model_width:].reshape(model_width, experts_all),
+            sums[:model_width],
+            sums[model_width : 2 * model_width],
+            sums[2 * model_width :].reshape(model_width, experts_all),
         )
     else:
         norm_sums = [

time: 823 us -> 818 us (level)
  waiting for transfers between devices: 309 us -> 360 us
  other arithmetic: 116 us -> 67.7 us
  Pallas kernels: 166 us -> 123 us
  starting transfers between devices: 117 us -> 139 us
  between operations: 3.06 us -> 15.9 us
  matrix products: 60.5 us -> 72.2 us
  local copies, waits for them, and re-layouts: 42.2 us -> 30.5 us
    ppermute x130 -> x102, waiting for transfers between devices: 309 us -> 359 us  [send(): return lax.ppermute(value, AXES, pairs)]
    pallas_call x8 -> x4, Pallas kernels: 135 us -> 91.8 us  [run_experts(): pl.pallas_call(functools.partial(expert_kernel, len(carried), place * tok...]
    ppermute x130 -> x102, starting transfers between devices: 117 us -> 138 us  [send(): return lax.ppermute(value, AXES, pairs)]
    dot_general x13, matrix products: 50.2 us -> 61.3 us  [contract_rows(): lax.dot_general(first_arg, second_arg, (((0,), (0,)), ((), ())), preferre...]
    convert_element_type x8 -> x4, other arithmetic: 16.4 us -> 5.45 us  [go_first(): sent = self.total(k, rows // 4, rows // 2).astype(jnp.bfloat16)]
    concatenate x9 -> x5, other arithmetic: 11.5 us -> 1.29 us  [the longest x1 1.24 us: body(): far_grads = jnp.concatenate(after(moved, [attended, near_grads]), axis=0)]
    dynamic_slice x9 -> x0, local copies, waits for them, and re-layouts: 9.42 us -> none  [the longest x8 8.69 us: moe_dense(): lax.dynamic_slice_in_dim(k, first_expert, local_experts, axis=1)]
    convert_element_type x6 -> x3, other arithmetic: 12.4 us -> 4.14 us  [go_z(): sent.astype(jnp.bfloat16)]
  transfers between devices with their start and end apart: 130 -> 105, of which waited for: 50 -> 41; matrix products, arithmetic and copies ran while one was open for 25% -> 19% of each run, Pallas kernels for 18% -> 14%
where the time goes in v2:
time: 818 us; the launch traced here: 808 us
  waiting for transfers between devices  360 us (44%)
  starting transfers between devices  139 us (17%)
  Pallas kernels  123 us (15%)
  matrix products  72.2 us (9%)
  other arithmetic  67.7 us (8%)
  local copies, waits for them, and re-layouts  30.5 us (4%)
  between operations  15.9 us (2%)
    ppermute x102, waiting for transfers between devices, send(): return lax.ppermute(value, AXES, pairs)  359 us
    ppermute x102, starting transfers between devices, send(): return lax.ppermute(value, AXES, pairs)  138 us
    pallas_call x4, Pallas kernels, run_experts(): pl.pallas_call(functools.partial(expert_kernel, len(carried), place * tok...  91.8 us
    dot_general x13, matrix products, contract_rows(): lax.dot_general(first_arg, second_arg, (((0,), (0,)), ((), ())), preferre...  61.3 us
    pallas_call x2, Pallas kernels, attend_back(): pl.pallas_call(attend_back_kernel, grid_spec=pltpu.PrefetchScalarGridSpec...  17.5 us
  transfers between devices with their start and end apart: 105, of which 41 were waited for; matrix products, arithmetic and copies ran while one was open for 19% of the time, Pallas kernels for 14%

profile of v2, /device:TPU:0, one launch (start us, length us, event | category | flops | bytes accessed | tf_op | source)
XLA Modules:
  0.0 807.9 jit_solution(4282575828906233899)
XLA Ops:
  10.5 3.0 collective-permute-start.1
  15.1 2.6 collective-permute-start.30
  19.9 9.5 %collective-permute-done.1 = bf16[128,2048]{1,0:T(8,128)(2,1)} collective-permute-done((bf16[128,2048]{1,0:T(8,128)(2,1)S(1)}, bf16[128,2048]{1,0:T(8,128)(2,1)}, u32[]{:S(2)}, u32[]{:S(2)}) %collective-permute-start.1) | collective-permute-done | bytes 524320 | tf_op jit(solution)/shard_map/ppermute | solution.py:272
  33.8 2.9 pad_maximum_fusion.2.rows_ref
  36.7 13.3 %attend.1 = (f32[512,512]{1,0:T(8,128)}, f32[512,512]{1,0:T(8,128)}, bf16[512,512]{1,0:T(8,128)(2,1)}, bf16[512,512]{1,0:T(8,128)(2,1)}, bf16[512,512]{1,0:T(8,1...) custom-call(bf16[512,2048]{1,0:T(8,128)(2,1)} %pad_maximum_fusion.2.rows_ref, bf16[2048,512]{1,0:T(8,128)(2,1)} %query_weight.1, ...), custom_call_target="tpu_custom_call" | custom-call | flops 12079595520 | bytes 8388608 | tf_op jit(solution)/shard_map/attend/pallas_call | solution.py:203
  54.5 2.8 fusion.93
  63.3 11.1 %collective-permute-start.17 = (bf16[16,128]{1,0:T(8,128)(2,1)S(1)}, bf16[16,128]{1,0:T(8,128)(2,1)S(1)}, u32[]{:S(2)}, u32[]{:S(2)}) collective-permute-start(bf16[16,128]{1,0:T(8,128)(2,1)S(1)} %fusion.17), channel_id=1, source_target_pairs={{0,24},{1,25},{2,26},{3,27},{4,28},{5,29},{6,30},{7,31},{8,0},{9,1... | collective-permute-start | bytes 12296 | tf_op jit(solution)/shard_map/ppermute | solution.py:272
  81.2 17.3 %collective-permute-start.5 = (bf16[128,2048]{1,0:T(8,128)(2,1)S(1)}, bf16[128,2048]{1,0:T(8,128)(2,1)S(1)}, u32[]{:S(2)}, u32[]{:S(2)}) collective-permute-start(bf16[128,2048]{1,0:T(8,128)(2,1)S(1)} %multiply_convert_fusion.refs_0_), channel_id=1, source_target_pairs={{0,16},{1,17},{2,18},{3,19},{4,20},{5,21},{6,22},{7,23},{8,24},{9,... | collective-permute-start | bytes 1572872 | tf_op jit(solution)/shard_map/ppermute | solution.py:272
  99.6 2.9 collective-permute-done.18
  105.2 13.0 %collective-permute-done.5.refs_0_ = bf16[128,2048]{1,0:T(8,128)(2,1)S(1)} collective-permute-done((bf16[128,2048]{1,0:T(8,128)(2,1)S(1)}, bf16[128,2048]{1,0:T(8,128)(2,1)S(1)}, u32[]{:S(2)}, u32[]{:S(2)}) %collective-permute-start.5) | collective-permute-done | bytes 524320 | tf_op jit(solution)/shard_map/ppermute | solution.py:272
  124.1 36.4 %collective-permute-done.10.refs_3_ = bf16[128,2048]{1,0:T(8,128)(2,1)} collective-permute-done((bf16[128,2048]{1,0:T(8,128)(2,1)}, bf16[128,2048]{1,0:T(8,128)(2,1)}, u32[]{:S(2)}, u32[]{:S(2)}) %collective-permute-start.10) | collective-permute-done | bytes 524320 | tf_op jit(solution)/shard_map/ppermute | solution.py:272
  161.6 4.6 collective-permute-start.7
  167.3 10.4 %collective-permute-done.7.refs_0_ = bf16[128,2048]{1,0:T(8,128)(2,1)} collective-permute-done((bf16[128,2048]{1,0:T(8,128)(2,1)S(1)}, bf16[128,2048]{1,0:T(8,128)(2,1)}, u32[]{:S(2)}, u32[]{:S(2)}) %collective-permute-start.7) | collective-permute-done | bytes 524320 | tf_op jit(solution)/shard_map/ppermute | solution.py:272
  177.7 22.9 %experts.4 = (bf16[512,2048]{1,0:T(8,128)(2,1)}, bf16[512,2048]{1,0:T(8,128)(2,1)}, f32[1024,2]{1,0:T(8,128)}, bf16[4096,2048]{1,0:T(8,128)(2,1)}, bf16[4096,204...) custom-call(s32[2,32]{1,0:T(2,128)} %fusion.74.ids_ref, ...), custom_call_target="tpu_custom_call" | custom-call | flops 26843545600 | bytes 37748736 | tf_op jit(solution)/shard_map/experts/pallas_call | solution.py:581
  202.3 2.7 collective-permute-done.35
  218.1 21.6 %collective-permute-done.34.refs_2_ = bf16[128,2048]{1,0:T(8,128)(2,1)} collective-permute-done((bf16[128,2048]{1,0:T(8,128)(2,1)}, bf16[128,2048]{1,0:T(8,128)(2,1)}, u32[]{:S(2)}, u32[]{:S(2)}) %collective-permute-start.34) | collective-permute-done | bytes 524320 | tf_op jit(solution)/shard_map/ppermute | solution.py:272
  240.3 5.1 collective-permute-done.24.refs_2_
  250.0 22.9 %experts.5 = (bf16[512,2048]{1,0:T(8,128)(2,1)}, bf16[512,2048]{1,0:T(8,128)(2,1)}, f32[1024,2]{1,0:T(8,128)}, bf16[4096,2048]{1,0:T(8,128)(2,1)}, bf16[4096,204...) custom-call(s32[2,32]{1,0:T(2,128)} %fusion.74.ids_ref, ...), custom_call_target="tpu_custom_call", output_to_operand_aliasing={{3}: (15, {}), {4}: (16, {}), {5}: (17, {}), {6}: (18, {}),... | custom-call | flops 26843545600 | bytes 37748736 | tf_op jit(solution)/shard_map/experts/pallas_call | solution.py:581
  277.5 23.1 %experts.6 = (bf16[512,2048]{1,0:T(8,128)(2,1)}, bf16[512,2048]{1,0:T(8,128)(2,1)}, f32[1024,2]{1,0:T(8,128)}, bf16[4096,2048]{1,0:T(8,128)(2,1)}, bf16[4096,204...) custom-call(s32[2,32]{1,0:T(2,128)} %fusion.74.ids_ref, ...), custom_call_target="tpu_custom_call", output_to_operand_aliasing={{3}: (15, {}), {4}: (16, {}), {5}: (17, {}), {6}: (18, {}),... | custom-call | flops 26843545600 | bytes 37748736 | tf_op jit(solution)/shard_map/experts/pallas_call | solution.py:581
  307.1 22.9 %experts.7 = (bf16[512,2048]{1,0:T(8,128)(2,1)}, bf16[512,2048]{1,0:T(8,128)(2,1)}, f32[1024,2]{1,0:T(8,128)}, bf16[4096,2048]{1,0:T(8,128)(2,1)}, bf16[4096,204...) custom-call(s32[2,32]{1,0:T(2,128)} %fusion.74.ids_ref, ...), custom_call_target="tpu_custom_call", output_to_operand_aliasing={{3}: (15, {}), {4}: (16, {}), {5}: (17, {}), {6}: (18, {}),... | custom-call | flops 26843545600 | bytes 37748736 | tf_op jit(solution)/shard_map/experts/pallas_call | solution.py:581
  330.3 2.9 add_convert_fusion.2
  339.2 9.3 %collective-permute-done.49 = bf16[256,2048]{1,0:T(8,128)(2,1)S(1)} collective-permute-done((bf16[256,2048]{1,0:T(8,128)(2,1)}, bf16[256,2048]{1,0:T(8,128)(2,1)S(1)}, u32[]{:S(2)}, u32[]{:S(2)}) %collective-permute-start.49) | collective-permute-done | bytes 1048608 | tf_op jit(solution)/shard_map/ppermute | solution.py:272
  355.4 11.9 %collective-permute-done.51 = bf16[128,2048]{1,0:T(8,128)(2,1)S(1)} collective-permute-done((bf16[128,2048]{1,0:T(8,128)(2,1)S(1)}, bf16[128,2048]{1,0:T(8,128)(2,1)S(1)}, u32[]{:S(2)}, u32[]{:S(2)}) %collective-permute-start.51) | collective-permute-done | bytes 524320 | tf_op jit(solution)/shard_map/ppermute | solution.py:272
  375.7 13.7 %collective-permute-done.56 = bf16[256,2048]{1,0:T(8,128)(2,1)S(1)} collective-permute-done((bf16[256,2048]{1,0:T(8,128)(2,1)S(1)}, bf16[256,2048]{1,0:T(8,128)(2,1)S(1)}, u32[]{:S(2)}, u32[]{:S(2)}) %collective-permute-start.56) | collective-permute-done | bytes 1048608 | tf_op jit(solution)/shard_map/ppermute | solution.py:272
  394.9 3.0 collective-permute-done.54
  403.8 4.4 collective-permute-start.66
  408.2 15.7 %collective-permute-done.67 = f32[16,128]{1,0:T(8,128)S(1)} collective-permute-done((f32[16,128]{1,0:T(8,128)S(1)}, f32[16,128]{1,0:T(8,128)S(1)}, u32[]{:S(2)}, u32[]{:S(2)}) %collective-permute-start.67) | collective-permute-done | bytes 8224 | tf_op jit(solution)/shard_map/ppermute | solution.py:272
  425.2 12.3 %collective-permute-done.61 = bf16[128,2048]{1,0:T(8,128)(2,1)} collective-permute-done((bf16[128,2048]{1,0:T(8,128)(2,1)}, bf16[128,2048]{1,0:T(8,128)(2,1)}, u32[]{:S(2)}, u32[]{:S(2)}) %collective-permute-start.61) | collective-permute-done | bytes 524320 | tf_op jit(solution)/shard_map/ppermute | solution.py:272
  440.7 11.3 %collective-permute-done.69 = bf16[128,2048]{1,0:T(8,128)(2,1)S(1)} collective-permute-done((bf16[128,2048]{1,0:T(8,128)(2,1)S(1)}, bf16[128,2048]{1,0:T(8,128)(2,1)S(1)}, u32[]{:S(2)}, u32[]{:S(2)}) %collective-permute-start.69) | collective-permute-done | bytes 524320 | tf_op jit(solution)/shard_map/ppermute | solution.py:272
  456.5 8.7 %attend_back.2 = (bf16[512,256]{1,0:T(8,128)(2,1)}, bf16[512,256]{1,0:T(8,128)(2,1)}, bf16[512,256]{1,0:T(8,128)(2,1)}, f32[1,256]{1,0:T(1,128)}, f32[1,256]{1,0:T(1,128)}) custom-call(s32[1]{0:T(128)} %bitcast.35.which_ref, bf16[512,2048]{1,0:T(8,128)(2,1)} %pad_maximum_fusion.3.row_grad_ref, bf16[512,2048]{1,0:T(8,128)(2,1)} %output_weight.3, ...), custom_call_target="tpu_custom_call" | custom-call | flops 4831838208 | bytes 5242880 | tf_op jit(solution)/shard_map/attend_back/pallas_call | solution.py:232
  467.1 19.1 %collective-permute-done.71 = bf16[512,768]{1,0:T(8,128)(2,1)} collective-permute-done((bf16[512,768]{1,0:T(8,128)(2,1)S(1)}, bf16[512,768]{1,0:T(8,128)(2,1)}, u32[]{:S(2)}, u32[]{:S(2)}) %collective-permute-start.71) | collective-permute-done | bytes 786464 | tf_op jit(solution)/shard_map/ppermute | solution.py:272
  491.1 8.8 %attend_back.3 = (bf16[512,256]{1,0:T(8,128)(2,1)}, bf16[512,256]{1,0:T(8,128)(2,1)}, bf16[512,256]{1,0:T(8,128)(2,1)}, f32[1,256]{1,0:T(1,128)}, f32[1,256]{1,0:T(1,128)}) custom-call(s32[1]{0:T(128)} %bitcast.65.which_ref, bf16[512,2048]{1,0:T(8,128)(2,1)} %pad_maximum_fusion.3.row_grad_ref, bf16[512,2048]{1,0:T(8,128)(2,1)} %output_weight.3, ...), custom_call_target="tpu_custom_call" | custom-call | flops 4831838208 | bytes 5242880 | tf_op jit(solution)/shard_map/attend_back/pallas_call | solution.py:232
  500.0 3.4 fusion.35
  524.9 8.6 %collective-permute-done.76 = bf16[1024,256]{1,0:T(8,128)(2,1)S(1)} collective-permute-done((bf16[1024,256]{1,0:T(8,128)(2,1)S(1)}, bf16[1024,256]{1,0:T(8,128)(2,1)S(1)}, u32[]{:S(2)}, u32[]{:S(2)}) %collective-permute-start.76) | collective-permute-done | bytes 524320 | tf_op jit(solution)/shard_map/ppermute | solution.py:272
  533.7 4.4 collective-permute-start.78
  540.5 13.5 %collective-permute-done.73 = bf16[128,2048]{1,0:T(8,128)(2,1)S(1)} collective-permute-done((bf16[128,2048]{1,0:T(8,128)(2,1)S(1)}, bf16[128,2048]{1,0:T(8,128)(2,1)S(1)}, u32[]{:S(2)}, u32[]{:S(2)}) %collective-permute-start.73) | collective-permute-done | bytes 524320 | tf_op jit(solution)/shard_map/ppermute | solution.py:272
  557.5 5.8 collective-permute-done.77
  569.4 9.0 %convolution_bitcast_fusion.2 = f32[1,2048,256]{2,1,0:T(8,128)S(1)} fusion(bf16[4096,2048]{1,0:T(8,128)(2,1)} %get-tuple-element.244, bf16[2,4096,256]{2,1,0:T(8,128)(2,1)S(1)} %copy-done.52), kind=kOutput, calls=%fused_computation.8 | convolution fusion | flops 4294967296 | bytes 20971520 | tf_op jit(solution)/shard_map/dot_general | solution.py:31
  578.4 8.3 %convolution_bitcast_fusion.3 = f32[1,2048,256]{2,1,0:T(8,128)S(1)} fusion(bf16[4096,2048]{1,0:T(8,128)(2,1)} %get-tuple-element.244, bf16[2,4096,256]{2,1,0:T(8,128)(2,1)S(1)} %copy-done.52), kind=kOutput, calls=%fused_computation.9 | convolution fusion | flops 4294967296 | bytes 20971520 | tf_op jit(solution)/shard_map/dot_general | solution.py:31
  590.8 4.8 collective-permute-done.82
  595.6 7.3 collective-permute-done.83
  602.9 3.4 collective-permute-start.84
  606.4 2.6 collective-permute-start.85
  609.9 2.9 collective-permute-start.87
  612.8 6.3 collective-permute-done.84
  620.1 9.0 %collective-permute-done.86 = bf16[512,256]{1,0:T(8,128)(2,1)} collective-permute-done((bf16[512,256]{1,0:T(8,128)(2,1)S(1)}, bf16[512,256]{1,0:T(8,128)(2,1)}, u32[]{:S(2)}, u32[]{:S(2)}) %collective-permute-start.86) | collective-permute-done | bytes 262176 | tf_op jit(solution)/shard_map/ppermute | solution.py:272
  630.3 29.9 %collective-permute-done.87 = bf16[512,256]{1,0:T(8,128)(2,1)} collective-permute-done((bf16[512,256]{1,0:T(8,128)(2,1)}, bf16[512,256]{1,0:T(8,128)(2,1)}, u32[]{:S(2)}, u32[]{:S(2)}) %collective-permute-start.87) | collective-permute-done | bytes 262176 | tf_op jit(solution)/shard_map/ppermute | solution.py:272
  664.1 3.5 collective-permute-start.94
  669.9 8.3 %convolution_bitcast_fusion = f32[1,2048,256]{2,1,0:T(8,128)S(1)} fusion(bf16[4096,2048]{1,0:T(8,128)(2,1)} %get-tuple-element.244, bf16[2,4096,256]{2,1,0:T(8,128)(2,1)S(1)} %copy-done.53), kind=kOutput, calls=%fused_computation.5 | convolution fusion | flops 4294967296 | bytes 20971520 | tf_op jit(solution)/shard_map/dot_general | solution.py:31
  678.2 8.5 %convolution_bitcast_fusion.1 = f32[1,2048,256]{2,1,0:T(8,128)S(1)} fusion(bf16[4096,2048]{1,0:T(8,128)(2,1)} %get-tuple-element.244, bf16[2,4096,256]{2,1,0:T(8,128)(2,1)S(1)} %copy-done.53), kind=kOutput, calls=%fused_computation.6 | convolution fusion | flops 4294967296 | bytes 20971520 | tf_op jit(solution)/shard_map/dot_general | solution.py:31
  689.2 7.8 collective-permute-done.93
  697.3 9.4 %collective-permute-done.91 = bf16[2048,256]{1,0:T(8,128)(2,1)S(1)} collective-permute-done((bf16[2048,256]{1,0:T(8,128)(2,1)S(1)}, bf16[2048,256]{1,0:T(8,128)(2,1)S(1)}, u32[]{:S(2)}, u32[]{:S(2)}) %collective-permute-start.91) | collective-permute-done | bytes 1048608 | tf_op jit(solution)/shard_map/ppermute | solution.py:272
  706.6 2.7 fusion
  709.4 7.5 collective-permute-start.95
  718.6 4.2 collective-permute-done.95
  722.8 6.7 collective-permute-done.98
  729.6 7.4 collective-permute-done.97
  737.3 4.3 collective-permute-done.96
  741.6 2.7 fusion.1
  746.8 14.1 %fusion.96 = f32[512,2048]{1,0:T(8,128)} fusion(bf16[4096,512]{1,0:T(8,128)(2,1)S(1)} %copy-done.51, bf16[4096,2048]{1,0:T(8,128)(2,1)} %get-tuple-element.268), kind=kOutput, calls=%fused_computation.252 | convolution fusion | flops 8589934592 | bytes 25165824 | tf_op jit(solution)/shard_map/dot_general | solution.py:31
  761.2 7.7 collective-permute-done.99
  768.9 2.7 fusion.2
  779.4 15.2 %collective-permute-done.101 = bf16[256,2048]{1,0:T(8,128)(2,1)} collective-permute-done((bf16[256,2048]{1,0:T(8,128)(2,1)S(1)}, bf16[256,2048]{1,0:T(8,128)(2,1)}, u32[]{:S(2)}, u32[]{:S(2)}) %collective-permute-start.101) | collective-permute-done | bytes 1048608 | tf_op jit(solution)/shard_map/ppermute | solution.py:272
  794.6 4.3 fusion.3
  (447 shorter events, 183.3 us)
Async XLA Ops:
  7.2 45.9 %all-gather.3.cloned.1.call-start = ((), (), s32[]{:S(2)}) async-start(), calls=%async_computation.1 | async-start | bytes 4718592 | tf_op jit(solution)/shard_map/all_gather | solution.py:905
  7.9 241.3 %all-gather.5.cloned.1.call-start = ((), (), s32[]{:S(2)}) async-start(), calls=%async_computation.2 | async-start | bytes 14155776 | tf_op jit(solution)/shard_map/all_gather | solution.py:934
  10.5 18.9 %collective-permute-start.1 = (bf16[128,2048]{1,0:T(8,128)(2,1)S(1)}, bf16[128,2048]{1,0:T(8,128)(2,1)}, u32[]{:S(2)}, u32[]{:S(2)}) collective-permute-start(bf16[128,2048]{1,0:T(8,128)(2,1)S(1)} %fusion.18), channel_id=1, source_target_pairs={{0,2},{1,3},{2,0},{3,1},{4,6},{5,7},{6,4},{7,5},{8,10},{9,11},{10,... | collective-permute-start | bytes 1572872 | tf_op jit(solution)/shard_map/ppermute | solution.py:272
  13.5 20.3 %collective-permute-start = (bf16[128,2048]{1,0:T(8,128)(2,1)S(1)}, bf16[128,2048]{1,0:T(8,128)(2,1)}, u32[]{:S(2)}, u32[]{:S(2)}) collective-permute-start(bf16[128,2048]{1,0:T(8,128)(2,1)S(1)} %fusion.18), channel_id=1, source_target_pairs={{0,1},{1,0},{2,3},{3,2},{4,5},{5,4},{6,7},{7,6},{8,9},{9,8},{10,11... | collective-permute-start | bytes 1572872 | tf_op jit(solution)/shard_map/ppermute | solution.py:272
  13.5 36.5 %collective-permute-start.31 = (bf16[128,2048]{1,0:T(8,128)(2,1)S(1)}, bf16[128,2048]{1,0:T(8,128)(2,1)S(1)}, u32[]{:S(2)}, u32[]{:S(2)}) collective-permute-start(bf16[128,2048]{1,0:T(8,128)(2,1)S(1)} %copy-done.17), channel_id=1, source_target_pairs={{0,8},{1,9},{2,10},{3,11},{4,12},{5,13},{6,14},{7,15},{8,16},{9,17... | collective-permute-start | bytes 1572872 | tf_op jit(solution)/shard_map/ppermute | solution.py:272
  15.1 37.2 %collective-permute-start.30 = (bf16[128,2048]{1,0:T(8,128)(2,1)S(1)}, bf16[128,2048]{1,0:T(8,128)(2,1)S(1)}, u32[]{:S(2)}, u32[]{:S(2)}) collective-permute-start(bf16[128,2048]{1,0:T(8,128)(2,1)S(1)} %copy-done.17), channel_id=1, source_target_pairs={{0,16},{1,17},{2,18},{3,19},{4,20},{5,21},{6,22},{7,23},{8,24},{9,... | collective-permute-start | bytes 1572872 | tf_op jit(solution)/shard_map/ppermute | solution.py:272
  17.7 34.6 %collective-permute-start.32 = (bf16[128,2048]{1,0:T(8,128)(2,1)S(1)}, bf16[128,2048]{1,0:T(8,128)(2,1)S(1)}, u32[]{:S(2)}, u32[]{:S(2)}) collective-permute-start(bf16[128,2048]{1,0:T(8,128)(2,1)S(1)} %copy-done.17), channel_id=1, source_target_pairs={{0,24},{1,25},{2,26},{3,27},{4,28},{5,29},{6,30},{7,31},{8,0},{9,1... | collective-permute-start | bytes 1572872 | tf_op jit(solution)/shard_map/ppermute | solution.py:272
  54.4 744.5 %reduce-scatter.2.cloned.1.call-start = ((), (), s32[]{:S(2)}) async-start(), calls=%async_computation.3 | async-start | bytes 17301504 | tf_op jit(solution)/shard_map/reduce_scatter | solution.py:1004
  63.3 35.2 %collective-permute-start.17 = (bf16[16,128]{1,0:T(8,128)(2,1)S(1)}, bf16[16,128]{1,0:T(8,128)(2,1)S(1)}, u32[]{:S(2)}, u32[]{:S(2)}) collective-permute-start(bf16[16,128]{1,0:T(8,128)(2,1)S(1)} %fusion.17), channel_id=1, source_target_pairs={{0,24},{1,25},{2,26},{3,27},{4,28},{5,29},{6,30},{7,31},{8,0},{9,1... | collective-permute-start | bytes 12296 | tf_op jit(solution)/shard_map/ppermute | solution.py:272
  74.4 24.1 %collective-permute-start.16 = (bf16[16,128]{1,0:T(8,128)(2,1)S(1)}, bf16[16,128]{1,0:T(8,128)(2,1)S(1)}, u32[]{:S(2)}, u32[]{:S(2)}) collective-permute-start(bf16[16,128]{1,0:T(8,128)(2,1)S(1)} %fusion.17), channel_id=1, source_target_pairs={{0,16},{1,17},{2,18},{3,19},{4,20},{5,21},{6,22},{7,23},{8,24},{9,... | collective-permute-start | bytes 12296 | tf_op jit(solution)/shard_map/ppermute | solution.py:272
  74.8 23.6 %collective-permute-start.15 = (bf16[16,128]{1,0:T(8,128)(2,1)S(1)}, bf16[16,128]{1,0:T(8,128)(2,1)S(1)}, u32[]{:S(2)}, u32[]{:S(2)}) collective-permute-start(bf16[16,128]{1,0:T(8,128)(2,1)S(1)} %fusion.17), channel_id=1, source_target_pairs={{0,8},{1,9},{2,10},{3,11},{4,12},{5,13},{6,14},{7,15},{8,16},{9,17... | collective-permute-start | bytes 12296 | tf_op jit(solution)/shard_map/ppermute | solution.py:272
  79.6 41.7 %collective-permute-start.8 = (bf16[128,2048]{1,0:T(8,128)(2,1)S(1)}, bf16[128,2048]{1,0:T(8,128)(2,1)}, u32[]{:S(2)}, u32[]{:S(2)}) collective-permute-start(bf16[128,2048]{1,0:T(8,128)(2,1)S(1)} %multiply_convert_fusion.refs_0_), channel_id=1, source_target_pairs={{0,4},{1,3},{2,6},{3,1},{4,0},{5,7},{6,2},{7,5},{8,12},{9,11},{10,... | collective-permute-start | bytes 1572872 | tf_op jit(solution)/shard_map/ppermute | solution.py:272
  81.2 37.1 %collective-permute-start.5 = (bf16[128,2048]{1,0:T(8,128)(2,1)S(1)}, bf16[128,2048]{1,0:T(8,128)(2,1)S(1)}, u32[]{:S(2)}, u32[]{:S(2)}) collective-permute-start(bf16[128,2048]{1,0:T(8,128)(2,1)S(1)} %multiply_convert_fusion.refs_0_), channel_id=1, source_target_pairs={{0,16},{1,17},{2,18},{3,19},{4,20},{5,21},{6,22},{7,23},{8,24},{9,... | collective-permute-start | bytes 1572872 | tf_op jit(solution)/shard_map/ppermute | solution.py:272
  99.1 24.9 %collective-permute-start.9 = (bf16[128,2048]{1,0:T(8,128)(2,1)S(1)}, bf16[128,2048]{1,0:T(8,128)(2,1)}, u32[]{:S(2)}, u32[]{:S(2)}) collective-permute-start(bf16[128,2048]{1,0:T(8,128)(2,1)S(1)} %multiply_convert_fusion.refs_0_), channel_id=1, source_target_pairs={{0,2},{1,5},{2,0},{3,7},{4,6},{5,1},{6,4},{7,3},{8,10},{9,13},{10,... | collective-permute-start | bytes 1572872 | tf_op jit(solution)/shard_map/ppermute | solution.py:272
  102.5 19.3 %collective-permute-start.19 = (bf16[2,4,16,128]{3,2,1,0:T(8,128)(2,1)S(1)}, bf16[2,4,16,128]{3,2,1,0:T(8,128)(2,1)S(1)}, u32[]{:S(2)}, u32[]{:S(2)}) collective-permute-start(bf16[2,4,16,128]{3,2,1,0:T(8,128)(2,1)S(1)} %pad_maximum_fusion.12), channel_id=1, source_target_pairs={{0,2},{1,5},{2,0},{3,7},{4,6},{5,1},{6,4},{7,3},{8,10},{9,13},{10,... | collective-permute-start | bytes 98312 | tf_op jit(solution)/shard_map/ppermute | solution.py:272
  118.2 42.9 %collective-permute-start.22 = (bf16[128,2048]{1,0:T(8,128)(2,1)S(1)}, bf16[128,2048]{1,0:T(8,128)(2,1)S(1)}, u32[]{:S(2)}, u32[]{:S(2)}) collective-permute-start(bf16[128,2048]{1,0:T(8,128)(2,1)S(1)} %collective-permute-done.5.refs_0_), channel_id=1, source_target_pairs={{0,2},{1,5},{2,0},{3,7},{4,6},{5,1},{6,4},{7,3},{8,10},{9,13},{10,... | collective-permute-start | bytes 1572872 | tf_op jit(solution)/shard_map/ppermute | solution.py:272
  119.8 41.8 %collective-permute-start.21 = (bf16[128,2048]{1,0:T(8,128)(2,1)S(1)}, bf16[128,2048]{1,0:T(8,128)(2,1)S(1)}, u32[]{:S(2)}, u32[]{:S(2)}) collective-permute-start(bf16[128,2048]{1,0:T(8,128)(2,1)S(1)} %collective-permute-done.5.refs_0_), channel_id=1, source_target_pairs={{0,4},{1,3},{2,6},{3,1},{4,0},{5,7},{6,2},{7,5},{8,12},{9,11},{10,... | collective-permute-start | bytes 1572872 | tf_op jit(solution)/shard_map/ppermute | solution.py:272
  121.3 39.2 %collective-permute-start.10 = (bf16[128,2048]{1,0:T(8,128)(2,1)}, bf16[128,2048]{1,0:T(8,128)(2,1)}, u32[]{:S(2)}, u32[]{:S(2)}) collective-permute-start(bf16[128,2048]{1,0:T(8,128)(2,1)} %collective-permute-done.8.refs_1_), channel_id=1, source_target_pairs={{0,2},{1,5},{2,0},{3,7},{4,6},{5,1},{6,4},{7,3},{8,10},{9,13},{10,... | collective-permute-start | bytes 1572872 | tf_op jit(solution)/shard_map/ppermute | solution.py:272
  121.8 38.8 %collective-permute-start.6 = (bf16[128,2048]{1,0:T(8,128)(2,1)S(1)}, bf16[128,2048]{1,0:T(8,128)(2,1)}, u32[]{:S(2)}, u32[]{:S(2)}) collective-permute-start(bf16[128,2048]{1,0:T(8,128)(2,1)S(1)} %multiply_convert_fusion.refs_0_), channel_id=1, source_target_pairs={{0,8},{1,9},{2,10},{3,11},{4,12},{5,13},{6,14},{7,15},{8,16},{9,17... | collective-permute-start | bytes 1572872 | tf_op jit(solution)/shard_map/ppermute | solution.py:272
  124.0 37.0 %collective-permute-start.20 = (bf16[4,4,16,128]{3,2,1,0:T(8,128)(2,1)S(1)}, bf16[4,4,16,128]{3,2,1,0:T(8,128)(2,1)S(1)}, u32[]{:S(2)}, u32[]{:S(2)}) collective-permute-start(bf16[4,4,16,128]{3,2,1,0:T(8,128)(2,1)S(1)} %pad_maximum_fusion.11), channel_id=1, source_target_pairs={{0,1},{1,0},{2,3},{3,2},{4,5},{5,4},{6,7},{7,6},{8,9},{9,8},{10,11... | collective-permute-start | bytes 196616 | tf_op jit(solution)/shard_map/ppermute | solution.py:272
  208.0 38.0 %collective-permute-start.42 = (bf16[256,2048]{1,0:T(8,128)(2,1)S(1)}, bf16[256,2048]{1,0:T(8,128)(2,1)}, u32[]{:S(2)}, u32[]{:S(2)}) collective-permute-start(bf16[256,2048]{1,0:T(8,128)(2,1)S(1)} %add_convert_fusion.3), channel_id=1, source_target_pairs={{0,2},{1,5},{2,0},{3,7},{4,6},{5,1},{6,4},{7,3},{8,10},{9,13},{10,... | collective-permute-start | bytes 3145736 | tf_op jit(solution)/shard_map/ppermute | solution.py:272
  209.6 30.1 %collective-permute-start.34 = (bf16[128,2048]{1,0:T(8,128)(2,1)}, bf16[128,2048]{1,0:T(8,128)(2,1)}, u32[]{:S(2)}, u32[]{:S(2)}) collective-permute-start(bf16[128,2048]{1,0:T(8,128)(2,1)} %collective-permute-done.6.refs_0_), channel_id=1, source_target_pairs={{0,2},{1,5},{2,0},{3,7},{4,6},{5,1},{6,4},{7,3},{8,10},{9,13},{10,... | collective-permute-start | bytes 1572872 | tf_op jit(solution)/shard_map/ppermute | solution.py:272
  210.2 29.6 %collective-permute-start.33 = (bf16[128,2048]{1,0:T(8,128)(2,1)}, bf16[128,2048]{1,0:T(8,128)(2,1)}, u32[]{:S(2)}, u32[]{:S(2)}) collective-permute-start(bf16[128,2048]{1,0:T(8,128)(2,1)} %collective-permute-done.6.refs_0_), channel_id=1, source_target_pairs={{0,4},{1,3},{2,6},{3,1},{4,0},{5,7},{6,2},{7,5},{8,12},{9,11},{10,... | collective-permute-start | bytes 1572872 | tf_op jit(solution)/shard_map/ppermute | solution.py:272
  211.4 34.0 %collective-permute-start.24 = (bf16[128,2048]{1,0:T(8,128)(2,1)}, bf16[128,2048]{1,0:T(8,128)(2,1)}, u32[]{:S(2)}, u32[]{:S(2)}) collective-permute-start(bf16[128,2048]{1,0:T(8,128)(2,1)} %collective-permute-done.7.refs_0_), channel_id=1, source_target_pairs={{0,2},{1,5},{2,0},{3,7},{4,6},{5,1},{6,4},{7,3},{8,10},{9,13},{10,... | collective-permute-start | bytes 1572872 | tf_op jit(solution)/shard_map/ppermute | solution.py:272
  213.0 32.4 %collective-permute-start.23 = (bf16[128,2048]{1,0:T(8,128)(2,1)}, bf16[128,2048]{1,0:T(8,128)(2,1)}, u32[]{:S(2)}, u32[]{:S(2)}) collective-permute-start(bf16[128,2048]{1,0:T(8,128)(2,1)} %collective-permute-done.7.refs_0_), channel_id=1, source_target_pairs={{0,4},{1,3},{2,6},{3,1},{4,0},{5,7},{6,2},{7,5},{8,12},{9,11},{10,... | collective-permute-start | bytes 1572872 | tf_op jit(solution)/shard_map/ppermute | solution.py:272
  245.9 27.0 %collective-permute-start.37 = (bf16[128,2048]{1,0:T(8,128)(2,1)}, bf16[128,2048]{1,0:T(8,128)(2,1)}, u32[]{:S(2)}, u32[]{:S(2)}) collective-permute-start(bf16[128,2048]{1,0:T(8,128)(2,1)} %collective-permute-done.33.refs_1_), channel_id=1, source_target_pairs={{0,2},{1,5},{2,0},{3,7},{4,6},{5,1},{6,4},{7,3},{8,10},{9,13},{10,... | collective-permute-start | bytes 1572872 | tf_op jit(solution)/shard_map/ppermute | solution.py:272
  275.3 26.4 %collective-permute-start.36 = (bf16[128,2048]{1,0:T(8,128)(2,1)}, bf16[128,2048]{1,0:T(8,128)(2,1)}, u32[]{:S(2)}, u32[]{:S(2)}) collective-permute-start(bf16[128,2048]{1,0:T(8,128)(2,1)} %collective-permute-done.23.refs_1_), channel_id=1, source_target_pairs={{0,2},{1,5},{2,0},{3,7},{4,6},{5,1},{6,4},{7,3},{8,10},{9,13},{10,... | collective-permute-start | bytes 1572872 | tf_op jit(solution)/shard_map/ppermute | solution.py:272
  276.0 26.7 %collective-permute-start.48 = (bf16[128,2048]{1,0:T(8,128)(2,1)S(1)}, bf16[128,2048]{1,0:T(8,128)(2,1)S(1)}, u32[]{:S(2)}, u32[]{:S(2)}) collective-permute-start(bf16[128,2048]{1,0:T(8,128)(2,1)S(1)} %add_convert_fusion.11), channel_id=1, source_target_pairs={{0,4},{1,3},{2,6},{3,1},{4,0},{5,7},{6,2},{7,5},{8,12},{9,11},{10,... | collective-permute-start | bytes 1572872 | tf_op jit(solution)/shard_map/ppermute | solution.py:272
  277.1 28.5 %collective-permute-start.47 = (bf16[512,2048]{1,0:T(8,128)(2,1)}, bf16[512,2048]{1,0:T(8,128)(2,1)}, u32[]{:S(2)}, u32[]{:S(2)}) collective-permute-start(bf16[512,2048]{1,0:T(8,128)(2,1)} %get-tuple-element.192), channel_id=1, source_target_pairs={{0,1},{1,0},{2,3},{3,2},{4,5},{5,4},{6,7},{7,6},{8,9},{9,8},{10,11... | collective-permute-start | bytes 6291464 | tf_op jit(solution)/shard_map/ppermute | solution.py:272
  305.7 31.4 %collective-permute-start.50 = (bf16[512,2048]{1,0:T(8,128)(2,1)}, bf16[512,2048]{1,0:T(8,128)(2,1)}, u32[]{:S(2)}, u32[]{:S(2)}) collective-permute-start(bf16[512,2048]{1,0:T(8,128)(2,1)} %get-tuple-element.205), channel_id=1, source_target_pairs={{0,1},{1,0},{2,3},{3,2},{4,5},{5,4},{6,7},{7,6},{8,9},{9,8},{10,11... | collective-permute-start | bytes 6291464 | tf_op jit(solution)/shard_map/ppermute | solution.py:272
  330.1 23.7 %collective-permute-start.52 = (bf16[512,2048]{1,0:T(8,128)(2,1)}, bf16[512,2048]{1,0:T(8,128)(2,1)}, u32[]{:S(2)}, u32[]{:S(2)}) collective-permute-start(bf16[512,2048]{1,0:T(8,128)(2,1)} %get-tuple-element.207), channel_id=1, source_target_pairs={{0,1},{1,0},{2,3},{3,2},{4,5},{5,4},{6,7},{7,6},{8,9},{9,8},{10,11... | collective-permute-start | bytes 6291464 | tf_op jit(solution)/shard_map/ppermute | solution.py:272
  348.5 20.4 %collective-permute-start.53 = (bf16[256,2048]{1,0:T(8,128)(2,1)S(1)}, bf16[256,2048]{1,0:T(8,128)(2,1)S(1)}, u32[]{:S(2)}, u32[]{:S(2)}) collective-permute-start(bf16[256,2048]{1,0:T(8,128)(2,1)S(1)} %add_convert_fusion.1), channel_id=1, source_target_pairs={{0,2},{1,5},{2,0},{3,7},{4,6},{5,1},{6,4},{7,3},{8,10},{9,13},{10,... | collective-permute-start | bytes 3145736 | tf_op jit(solution)/shard_map/ppermute | solution.py:272
  350.3 20.4 %collective-permute-start.64 = (f32[1,4,16,128]{3,2,1,0:T(8,128)S(1)}, f32[1,4,16,128]{3,2,1,0:T(8,128)S(1)}, u32[]{:S(2)}, u32[]{:S(2)}) collective-permute-start(f32[1,4,16,128]{3,2,1,0:T(8,128)S(1)} %slice.400), channel_id=1, source_target_pairs={{0,4},{1,3},{2,6},{3,1},{4,0},{5,7},{6,2},{7,5},{8,12},{9,11},{10,... | collective-permute-start | bytes 98312 | tf_op jit(solution)/shard_map/ppermute | solution.py:272
  368.9 20.4 %collective-permute-start.56 = (bf16[256,2048]{1,0:T(8,128)(2,1)S(1)}, bf16[256,2048]{1,0:T(8,128)(2,1)S(1)}, u32[]{:S(2)}, u32[]{:S(2)}) collective-permute-start(bf16[256,2048]{1,0:T(8,128)(2,1)S(1)} %add_convert_fusion), channel_id=1, source_target_pairs={{0,2},{1,5},{2,0},{3,7},{4,6},{5,1},{6,4},{7,3},{8,10},{9,13},{10,... | collective-permute-start | bytes 3145736 | tf_op jit(solution)/shard_map/ppermute | solution.py:272
  373.4 24.4 %collective-permute-start.54 = (bf16[128,2048]{1,0:T(8,128)(2,1)S(1)}, bf16[128,2048]{1,0:T(8,128)(2,1)S(1)}, u32[]{:S(2)}, u32[]{:S(2)}) collective-permute-start(bf16[128,2048]{1,0:T(8,128)(2,1)S(1)} %add_convert_fusion.9), channel_id=1, source_target_pairs={{0,16},{1,17},{2,18},{3,19},{4,20},{5,21},{6,22},{7,23},{8,24},{9,... | collective-permute-start | bytes 1572872 | tf_op jit(solution)/shard_map/ppermute | solution.py:272
  374.9 18.7 %collective-permute-start.55 = (bf16[128,2048]{1,0:T(8,128)(2,1)S(1)}, bf16[128,2048]{1,0:T(8,128)(2,1)S(1)}, u32[]{:S(2)}, u32[]{:S(2)}) collective-permute-start(bf16[128,2048]{1,0:T(8,128)(2,1)S(1)} %add_convert_fusion.8), channel_id=1, source_target_pairs={{0,4},{1,3},{2,6},{3,1},{4,0},{5,7},{6,2},{7,5},{8,12},{9,11},{10,... | collective-permute-start | bytes 1572872 | tf_op jit(solution)/shard_map/ppermute | solution.py:272
  397.8 26.0 %collective-permute-start.57 = (bf16[128,2048]{1,0:T(8,128)(2,1)S(1)}, bf16[128,2048]{1,0:T(8,128)(2,1)S(1)}, u32[]{:S(2)}, u32[]{:S(2)}) collective-permute-start(bf16[128,2048]{1,0:T(8,128)(2,1)S(1)} %add_convert_fusion.7), channel_id=1, source_target_pairs={{0,24},{1,25},{2,26},{3,27},{4,28},{5,29},{6,30},{7,31},{8,0},{9,1... | collective-permute-start | bytes 1572872 | tf_op jit(solution)/shard_map/ppermute | solution.py:272
  400.3 23.5 %collective-permute-start.60 = (bf16[128,2048]{1,0:T(8,128)(2,1)S(1)}, bf16[128,2048]{1,0:T(8,128)(2,1)}, u32[]{:S(2)}, u32[]{:S(2)}) collective-permute-start(bf16[128,2048]{1,0:T(8,128)(2,1)S(1)} %copy-done.20), channel_id=1, source_target_pairs={{0,4},{1,5},{2,6},{3,7},{4,0},{5,1},{6,2},{7,3},{8,12},{9,13},{10,... | collective-permute-start | bytes 1572872 | tf_op jit(solution)/shard_map/ppermute | solution.py:272
  402.3 22.5 %collective-permute-start.59 = (bf16[128,2048]{1,0:T(8,128)(2,1)S(1)}, bf16[128,2048]{1,0:T(8,128)(2,1)S(1)}, u32[]{:S(2)}, u32[]{:S(2)}) collective-permute-start(bf16[128,2048]{1,0:T(8,128)(2,1)S(1)} %add_convert_fusion.5), channel_id=1, source_target_pairs={{0,8},{1,9},{2,10},{3,11},{4,12},{5,13},{6,14},{7,15},{8,16},{9,17... | collective-permute-start | bytes 1572872 | tf_op jit(solution)/shard_map/ppermute | solution.py:272
  403.6 20.3 %collective-permute-start.67 = (f32[16,128]{1,0:T(8,128)S(1)}, f32[16,128]{1,0:T(8,128)S(1)}, u32[]{:S(2)}, u32[]{:S(2)}) collective-permute-start(f32[16,128]{1,0:T(8,128)S(1)} %get-tuple-element.362), channel_id=1, source_target_pairs={{0,8},{1,9},{2,10},{3,11},{4,12},{5,13},{6,14},{7,15},{8,16},{9,17... | collective-permute-start | bytes 24584 | tf_op jit(solution)/shard_map/ppermute | solution.py:272
  403.8 20.1 %collective-permute-start.66 = (f32[16,128]{1,0:T(8,128)S(1)}, f32[16,128]{1,0:T(8,128)S(1)}, u32[]{:S(2)}, u32[]{:S(2)}) collective-permute-start(f32[16,128]{1,0:T(8,128)S(1)} %get-tuple-element.363), channel_id=1, source_target_pairs={{0,24},{1,25},{2,26},{3,27},{4,28},{5,29},{6,30},{7,31},{8,0},{9,1... | collective-permute-start | bytes 24584 | tf_op jit(solution)/shard_map/ppermute | solution.py:272
  466.4 19.8 %collective-permute-start.71 = (bf16[512,768]{1,0:T(8,128)(2,1)S(1)}, bf16[512,768]{1,0:T(8,128)(2,1)}, u32[]{:S(2)}, u32[]{:S(2)}) collective-permute-start(bf16[512,768]{1,0:T(8,128)(2,1)S(1)} %pad_maximum_fusion.7), channel_id=1, source_target_pairs={{0,4},{1,5},{2,6},{3,7},{4,0},{5,1},{6,2},{7,3},{8,12},{9,13},{10,... | collective-permute-start | bytes 2359304 | tf_op jit(solution)/shard_map/ppermute | solution.py:272
  509.1 59.6 %collective-permute-start.88 = (bf16[256,2048]{1,0:T(8,128)(2,1)S(1)}, bf16[256,2048]{1,0:T(8,128)(2,1)S(1)}, u32[]{:S(2)}, u32[]{:S(2)}) collective-permute-start(bf16[256,2048]{1,0:T(8,128)(2,1)S(1)} %convolution_convert_fusion), channel_id=1, source_target_pairs={{0,4},{1,5},{2,6},{3,7},{4,0},{5,1},{6,2},{7,3},{8,12},{9,13},{10,... | collective-permute-start | bytes 3145736 | tf_op jit(solution)/shard_map/ppermute | solution.py:272
  513.7 19.9 %collective-permute-start.76 = (bf16[1024,256]{1,0:T(8,128)(2,1)S(1)}, bf16[1024,256]{1,0:T(8,128)(2,1)S(1)}, u32[]{:S(2)}, u32[]{:S(2)}) collective-permute-start(bf16[1024,256]{1,0:T(8,128)(2,1)S(1)} %dynamic-slice_convert_fusion.3), channel_id=1, source_target_pairs={{0,8},{1,9},{2,10},{3,11},{4,12},{5,13},{6,14},{7,15},{8,0},{9,1},... | collective-permute-start | bytes 1572872 | tf_op jit(solution)/shard_map/ppermute | solution.py:272
  523.0 31.0 %collective-permute-start.73 = (bf16[128,2048]{1,0:T(8,128)(2,1)S(1)}, bf16[128,2048]{1,0:T(8,128)(2,1)S(1)}, u32[]{:S(2)}, u32[]{:S(2)}) collective-permute-start(bf16[128,2048]{1,0:T(8,128)(2,1)S(1)} %fusion.25), channel_id=1, source_target_pairs={{0,2},{1,3},{2,0},{3,1},{4,6},{5,7},{6,4},{7,5},{8,10},{9,11},{10,... | collective-permute-start | bytes 1572872 | tf_op jit(solution)/shard_map/ppermute | solution.py:272
  533.7 23.7 %collective-permute-start.78 = (bf16[512,256]{1,0:T(8,128)(2,1)S(1)}, bf16[512,256]{1,0:T(8,128)(2,1)S(1)}, u32[]{:S(2)}, u32[]{:S(2)}) collective-permute-start(bf16[512,256]{1,0:T(8,128)(2,1)S(1)} %dynamic-slice_convert_fusion.7), channel_id=1, source_target_pairs={{0,16},{1,17},{2,18},{3,19},{4,20},{5,21},{6,22},{7,23},{8,24},{9,... | collective-permute-start | bytes 786440 | tf_op jit(solution)/shard_map/ppermute | solution.py:272
  538.1 25.2 %collective-permute-start.79 = (bf16[1024,256]{1,0:T(8,128)(2,1)S(1)}, bf16[1024,256]{1,0:T(8,128)(2,1)S(1)}, u32[]{:S(2)}, u32[]{:S(2)}) collective-permute-start(bf16[1024,256]{1,0:T(8,128)(2,1)S(1)} %dynamic-slice_convert_fusion.2), channel_id=1, source_target_pairs={{0,8},{1,9},{2,10},{3,11},{4,12},{5,13},{6,14},{7,15},{8,0},{9,1},... | collective-permute-start | bytes 1572872 | tf_op jit(solution)/shard_map/ppermute | solution.py:272
  563.5 26.4 %collective-permute-start.80 = (f32[37888]{0:T(1024)S(1)}, f32[37888]{0:T(1024)S(1)}, u32[]{:S(2)}, u32[]{:S(2)}) collective-permute-start(f32[37888]{0:T(1024)S(1)} %add.414), channel_id=1, source_target_pairs={{0,8},{1,9},{2,10},{3,11},{4,12},{5,13},{6,14},{7,15},{8,0},{9,1},... | collective-permute-start | bytes 454664 | tf_op jit(solution)/shard_map/ppermute | solution.py:272
  565.6 25.0 %collective-permute-start.81 = (bf16[512,256]{1,0:T(8,128)(2,1)S(1)}, bf16[512,256]{1,0:T(8,128)(2,1)S(1)}, u32[]{:S(2)}, u32[]{:S(2)}) collective-permute-start(bf16[512,256]{1,0:T(8,128)(2,1)S(1)} %add_convert_fusion.15), channel_id=1, source_target_pairs={{0,16},{1,17},{2,18},{3,19},{4,20},{5,21},{6,22},{7,23},{8,24},{9,... | collective-permute-start | bytes 786440 | tf_op jit(solution)/shard_map/ppermute | solution.py:272
  568.0 27.6 %collective-permute-start.82 = (bf16[512,256]{1,0:T(8,128)(2,1)S(1)}, bf16[512,256]{1,0:T(8,128)(2,1)S(1)}, u32[]{:S(2)}, u32[]{:S(2)}) collective-permute-start(bf16[512,256]{1,0:T(8,128)(2,1)S(1)} %dynamic-slice_convert_fusion.6), channel_id=1, source_target_pairs={{0,16},{1,17},{2,18},{3,19},{4,20},{5,21},{6,22},{7,23},{8,24},{9,... | collective-permute-start | bytes 786440 | tf_op jit(solution)/shard_map/ppermute | solution.py:272
  568.5 34.5 %collective-permute-start.83 = (bf16[1024,256]{1,0:T(8,128)(2,1)S(1)}, bf16[1024,256]{1,0:T(8,128)(2,1)S(1)}, u32[]{:S(2)}, u32[]{:S(2)}) collective-permute-start(bf16[1024,256]{1,0:T(8,128)(2,1)S(1)} %dynamic-slice_convert_fusion.1), channel_id=1, source_target_pairs={{0,8},{1,9},{2,10},{3,11},{4,12},{5,13},{6,14},{7,15},{8,0},{9,1},... | collective-permute-start | bytes 1572872 | tf_op jit(solution)/shard_map/ppermute | solution.py:272
  606.3 22.7 %collective-permute-start.86 = (bf16[512,256]{1,0:T(8,128)(2,1)S(1)}, bf16[512,256]{1,0:T(8,128)(2,1)}, u32[]{:S(2)}, u32[]{:S(2)}) collective-permute-start(bf16[512,256]{1,0:T(8,128)(2,1)S(1)} %add_convert_fusion.14), channel_id=1, source_target_pairs={{0,16},{1,17},{2,18},{3,19},{4,20},{5,21},{6,22},{7,23},{8,24},{9,... | collective-permute-start | bytes 786440 | tf_op jit(solution)/shard_map/ppermute | solution.py:272
  606.4 54.8 %collective-permute-start.85 = (bf16[1024,256]{1,0:T(8,128)(2,1)S(1)}, bf16[1024,256]{1,0:T(8,128)(2,1)}, u32[]{:S(2)}, u32[]{:S(2)}) collective-permute-start(bf16[1024,256]{1,0:T(8,128)(2,1)S(1)} %maximum_select_fusion.14), channel_id=1, source_target_pairs={{0,8},{1,9},{2,10},{3,11},{4,12},{5,13},{6,14},{7,15},{8,0},{9,1},... | collective-permute-start | bytes 1572872 | tf_op jit(solution)/shard_map/ppermute | solution.py:272
  609.0 52.2 %collective-permute-start.89 = (bf16[128,2048]{1,0:T(8,128)(2,1)}, bf16[128,2048]{1,0:T(8,128)(2,1)}, u32[]{:S(2)}, u32[]{:S(2)}) collective-permute-start(bf16[128,2048]{1,0:T(8,128)(2,1)} %dynamic-slice_convert_fusion), channel_id=1, source_target_pairs={{0,8},{1,9},{2,10},{3,11},{4,12},{5,13},{6,14},{7,15},{8,0},{9,1},... | collective-permute-start | bytes 1572872 | tf_op jit(solution)/shard_map/ppermute | solution.py:272
  609.9 50.3 %collective-permute-start.87 = (bf16[512,256]{1,0:T(8,128)(2,1)}, bf16[512,256]{1,0:T(8,128)(2,1)}, u32[]{:S(2)}, u32[]{:S(2)}) collective-permute-start(bf16[512,256]{1,0:T(8,128)(2,1)} %dynamic-slice_convert_fusion.5), channel_id=1, source_target_pairs={{0,16},{1,17},{2,18},{3,19},{4,20},{5,21},{6,22},{7,23},{8,24},{9,... | collective-permute-start | bytes 786440 | tf_op jit(solution)/shard_map/ppermute | solution.py:272
  662.8 26.3 %collective-permute-start.90 = (f32[37888]{0:T(1024)S(1)}, f32[37888]{0:T(1024)S(1)}, u32[]{:S(2)}, u32[]{:S(2)}) collective-permute-start(f32[37888]{0:T(1024)S(1)} %add.425), channel_id=1, source_target_pairs={{0,1},{1,0},{2,3},{3,2},{4,5},{5,4},{6,7},{7,6},{8,9},{9,8},{10,11... | collective-permute-start | bytes 454664 | tf_op jit(solution)/shard_map/ppermute | solution.py:272
  664.1 25.0 %collective-permute-start.94 = (bf16[64,2048]{1,0:T(8,128)(2,1)S(1)}, bf16[64,2048]{1,0:T(8,128)(2,1)S(1)}, u32[]{:S(2)}, u32[]{:S(2)}) collective-permute-start(bf16[64,2048]{1,0:T(8,128)(2,1)S(1)} %dynamic-slice_convert_fusion.4), channel_id=1, source_target_pairs={{0,16},{1,17},{2,18},{3,19},{4,20},{5,21},{6,22},{7,23},{8,24},{9,... | collective-permute-start | bytes 786440 | tf_op jit(solution)/shard_map/ppermute | solution.py:272
  667.6 29.4 %collective-permute-start.93 = (bf16[512,256]{1,0:T(8,128)(2,1)S(1)}, bf16[512,256]{1,0:T(8,128)(2,1)S(1)}, u32[]{:S(2)}, u32[]{:S(2)}) collective-permute-start(bf16[512,256]{1,0:T(8,128)(2,1)S(1)} %add_convert_fusion.13), channel_id=1, source_target_pairs={{0,16},{1,17},{2,18},{3,19},{4,20},{5,21},{6,22},{7,23},{8,24},{9,... | collective-permute-start | bytes 786440 | tf_op jit(solution)/shard_map/ppermute | solution.py:272
  667.7 41.7 %collective-permute-start.92 = (bf16[1024,256]{1,0:T(8,128)(2,1)S(1)}, bf16[1024,256]{1,0:T(8,128)(2,1)S(1)}, u32[]{:S(2)}, u32[]{:S(2)}) collective-permute-start(bf16[1024,256]{1,0:T(8,128)(2,1)S(1)} %maximum_select_fusion.15), channel_id=1, source_target_pairs={{0,8},{1,9},{2,10},{3,11},{4,12},{5,13},{6,14},{7,15},{8,0},{9,1},... | collective-permute-start | bytes 1572872 | tf_op jit(solution)/shard_map/ppermute | solution.py:272
  669.9 36.7 %collective-permute-start.91 = (bf16[2048,256]{1,0:T(8,128)(2,1)S(1)}, bf16[2048,256]{1,0:T(8,128)(2,1)S(1)}, u32[]{:S(2)}, u32[]{:S(2)}) collective-permute-start(bf16[2048,256]{1,0:T(8,128)(2,1)S(1)} %maximum_select_fusion.4), channel_id=1, source_target_pairs={{0,4},{1,5},{2,6},{3,7},{4,0},{5,1},{6,2},{7,3},{8,12},{9,13},{10,... | collective-permute-start | bytes 3145736 | tf_op jit(solution)/shard_map/ppermute | solution.py:272
  717.3 19.7 %collective-permute-start.97 = (bf16[1024,256]{1,0:T(8,128)(2,1)S(1)}, bf16[1024,256]{1,0:T(8,128)(2,1)S(1)}, u32[]{:S(2)}, u32[]{:S(2)}) collective-permute-start(bf16[1024,256]{1,0:T(8,128)(2,1)S(1)} %maximum_select_fusion.16), channel_id=1, source_target_pairs={{0,8},{1,9},{2,10},{3,11},{4,12},{5,13},{6,14},{7,15},{8,0},{9,1},... | collective-permute-start | bytes 1572872 | tf_op jit(solution)/shard_map/ppermute | solution.py:272
  717.3 24.2 %collective-permute-start.96 = (bf16[2048,256]{1,0:T(8,128)(2,1)S(1)}, bf16[2048,256]{1,0:T(8,128)(2,1)S(1)}, u32[]{:S(2)}, u32[]{:S(2)}) collective-permute-start(bf16[2048,256]{1,0:T(8,128)(2,1)S(1)} %maximum_select_fusion.5), channel_id=1, source_target_pairs={{0,4},{1,5},{2,6},{3,7},{4,0},{5,1},{6,2},{7,3},{8,12},{9,13},{10,... | collective-permute-start | bytes 3145736 | tf_op jit(solution)/shard_map/ppermute | solution.py:272
  745.6 23.3 %collective-permute-start.99 = (bf16[2048,256]{1,0:T(8,128)(2,1)S(1)}, bf16[2048,256]{1,0:T(8,128)(2,1)S(1)}, u32[]{:S(2)}, u32[]{:S(2)}) collective-permute-start(bf16[2048,256]{1,0:T(8,128)(2,1)S(1)} %maximum_select_fusion.6), channel_id=1, source_target_pairs={{0,4},{1,5},{2,6},{3,7},{4,0},{5,1},{6,2},{7,3},{8,12},{9,13},{10,... | collective-permute-start | bytes 3145736 | tf_op jit(solution)/shard_map/ppermute | solution.py:272
  771.6 23.0 %collective-permute-start.101 = (bf16[256,2048]{1,0:T(8,128)(2,1)S(1)}, bf16[256,2048]{1,0:T(8,128)(2,1)}, u32[]{:S(2)}, u32[]{:S(2)}) collective-permute-start(bf16[256,2048]{1,0:T(8,128)(2,1)S(1)} %maximum_select_fusion.7), channel_id=1, source_target_pairs={{0,4},{1,5},{2,6},{3,7},{4,0},{5,1},{6,2},{7,3},{8,12},{9,13},{10,... | collective-permute-start | bytes 3145736 | tf_op jit(solution)/shard_map/ppermute | solution.py:272
  (95 other events, 1022.1 us)
Sparse Core Ops, SparseCore 0:
  9.9 43.1 all-gather.2
  55.6 109.2 all-gather.4
  486.3 237.0 reduce-scatter.1
